TPU v7x, 32 devices: a whole 2x2x4 slice. The times are simulated.
32 devices in a mesh: dp: 8 (over z, x), rows: 4 (over y, core).
Axes of the slice: x: 2, y: 2, z: 4, core: 2. Of those that a mesh axis runs over, the one named last changes fastest.
Arguments:
- atoms: bfloat16 [24, 256, 512], P('dp', 'rows'), may hold values from -6 to 6
- pair_bias: bfloat16 [24, 64, 256, 256], P('dp', None, 'rows'), may hold values from -6 to 6
- mol_counts: int32 [24, 8], P('dp'), may hold values from 1 to 96, 256 in all within a row
- attn_gain: bfloat16 [512], replicated, may hold values from 0.5 to 1.5
- attn_shift: bfloat16 [512], replicated, may hold values from -1.75 to 1.75
- query_weight: bfloat16 [512, 512], replicated, may hold values from -0.25 to 0.25
- query_bias: bfloat16 [512], replicated, may hold values from -3 to 3
- key_weight: bfloat16 [512, 512], replicated, may hold values from -0.25 to 0.25
- value_weight: bfloat16 [512, 512], replicated, may hold values from -0.25 to 0.25
- value_bias: bfloat16 [512], replicated, may hold values from -3 to 3
- out_weight: bfloat16 [512, 512], replicated, may hold values from -0.75 to 0.75
- out_bias: bfloat16 [512], replicated, may hold values from -1.75 to 1.75
- ffn_gain: bfloat16 [512], replicated, may hold values from 0.5 to 1.5
- ffn_shift: bfloat16 [512], replicated, may hold values from -1.75 to 1.75
- inner_weight: bfloat16 [512, 2048], replicated, may hold values from -0.25 to 0.25
- inner_bias: bfloat16 [2048], replicated, may hold values from -3 to 3
- outer_weight: bfloat16 [2048, 512], replicated, may hold values from -0.1875 to 0.1875
- outer_bias: bfloat16 [512], replicated, may hold values from -1.75 to 1.75
- atoms_cotangent: bfloat16 [24, 256, 512], P('dp', 'rows'), may hold values from -6 to 6
- pair_cotangent: bfloat16 [24, 64, 256, 256], P('dp', None, 'rows'), may hold values from -6 to 6
Outputs:
- atoms_out: bfloat16 [24, 256, 512], P('dp', 'rows')
- pair_out: bfloat16 [24, 64, 256, 256], P('dp', None, 'rows')
- atoms_grad: bfloat16 [24, 256, 512], P('dp', 'rows')
- pair_grad: bfloat16 [24, 64, 256, 256], P('dp', None, 'rows')
- attn_gain_grad: float32 [512], P('dp')
- attn_shift_grad: float32 [512], P('dp')
- query_weight_grad: float32 [512, 512], P('dp')
- query_bias_grad: float32 [512], P('dp')
- key_weight_grad: float32 [512, 512], P('dp')
- value_weight_grad: float32 [512, 512], P('dp')
- value_bias_grad: float32 [512], P('dp')
- out_weight_grad: float32 [512, 512], P('dp')
- out_bias_grad: float32 [512], P('dp')
- ffn_gain_grad: float32 [512], P('dp')
- ffn_shift_grad: float32 [512], P('dp')
- inner_weight_grad: float32 [512, 2048], P('dp')
- inner_bias_grad: float32 [2048], P('dp')
- outer_weight_grad: float32 [2048, 512], P('dp')
- outer_bias_grad: float32 [512], P('dp')
Inputs may be any that keep to these rules, and one draw needn't show every extreme that they name: `mol_counts`: each slot's counts sum to 256, and the largest count of every slot is 96.
All inputs are finite; a program needn't handle non-finite values.
Results may differ from a plain program's by a relative error of at most 0.0083.
Values may be sent and summed in bfloat16 or wider, within the bound.
A program may use at most 128 MiB of HBM per device.

v0:
```python
import jax
import jax.numpy as jnp
from jax import lax
from jax.sharding import PartitionSpec as P


def standardize(value):
    centred = value - jnp.mean(value, axis=-1, keepdims=True)
    inverse = lax.rsqrt(jnp.mean(centred * centred, axis=-1, keepdims=True) + 1e-05)
    return (centred * inverse, inverse)


def norm_back(grad_normed, standard, inverse):
    return inverse * (
        grad_normed
        - jnp.mean(grad_normed, axis=-1, keepdims=True)
        - standard * jnp.mean(grad_normed * standard, axis=-1, keepdims=True)
    )


def matmul(left, right):
    return jnp.dot(left, right, preferred_element_type=jnp.float32)


def times_transposed(left, right):
    return lax.dot_general(
        left, right, (((1,), (1,)), ((), ())), preferred_element_type=jnp.float32
    )


def outer_sum(left, right):
    return lax.dot_general(
        left, right, (((0,), (0,)), ((), ())), preferred_element_type=jnp.float32
    )


def exact_gelu(value):
    return jax.nn.gelu(value, approximate=False)


def local(
    atoms,
    pair_bias,
    mol_counts,
    attn_gain,
    attn_shift,
    query_weight,
    query_bias,
    key_weight,
    value_weight,
    value_bias,
    out_weight,
    out_bias,
    ffn_gain,
    ffn_shift,
    inner_weight,
    inner_bias,
    outer_weight,
    outer_bias,
    atoms_cotangent,
    pair_cotangent,
):
    slots, part_rows, width = atoms.shape
    heads = pair_bias.shape[1]
    full = pair_bias.shape[3]
    depth = width // heads
    scale = depth ** (-0.5)
    tokens_here = slots * part_rows
    cumulative = jnp.cumsum(mol_counts, axis=1)
    position = jnp.arange(full, dtype=jnp.int32)
    segment = jnp.sum(
        (cumulative[:, None, :] <= position[None, :, None]).astype(jnp.int32), axis=-1
    )
    first = lax.axis_index("rows") * part_rows
    query_segment = lax.dynamic_slice_in_dim(segment, first, part_rows, 1)
    allowed = (query_segment[:, :, None] == segment[:, None, :])[:, None]
    gain_one = attn_gain.astype(jnp.float32)
    gain_two = ffn_gain.astype(jnp.float32)
    atoms_flat = atoms.astype(jnp.float32).reshape(tokens_here, width)
    standard_one, inverse_one = standardize(atoms_flat)
    normed = (standard_one * gain_one + attn_shift.astype(jnp.float32)).astype(jnp.bfloat16)
    queries = ((matmul(normed, query_weight) + query_bias.astype(jnp.float32)) * scale).astype(
        jnp.bfloat16
    )
    keys = matmul(normed, key_weight).astype(jnp.bfloat16)
    values = (matmul(normed, value_weight) + value_bias.astype(jnp.float32)).astype(jnp.bfloat16)
    local_keys = keys.reshape(slots, part_rows, width)
    local_values = values.reshape(slots, part_rows, width)
    key_all, value_all = (
        lax.all_gather(local_keys, "rows", axis=1, tiled=True),
        lax.all_gather(local_values, "rows", axis=1, tiled=True),
    )
    query_heads = queries.reshape(slots, part_rows, heads, depth)
    key_heads = key_all.reshape(slots, full, heads, depth)
    value_heads = value_all.reshape(slots, full, heads, depth)
    scores = jnp.einsum(
        "sqhd,skhd->shqk", query_heads, key_heads, preferred_element_type=jnp.float32
    )
    scores = scores + pair_bias.astype(jnp.float32)
    pair_out = scores.astype(jnp.bfloat16)
    masked = jnp.where(allowed, scores, -1000000000.0)
    highest = jnp.max(masked, axis=-1, keepdims=True)
    weights = jnp.exp(masked - highest)
    probs = weights / jnp.sum(weights, axis=-1, keepdims=True)
    probs_low = probs.astype(jnp.bfloat16)
    mixed = jnp.einsum(
        "shqk,skhd->sqhd", probs_low, value_heads, preferred_element_type=jnp.float32
    )
    mixed = mixed.reshape(tokens_here, width).astype(jnp.bfloat16)
    middle = atoms_flat + matmul(mixed, out_weight) + out_bias.astype(jnp.float32)
    standard_two, inverse_two = standardize(middle)
    inner = (standard_two * gain_two + ffn_shift.astype(jnp.float32)).astype(jnp.bfloat16)
    pre = matmul(inner, inner_weight) + inner_bias.astype(jnp.float32)
    activation, gelu_back = jax.vjp(exact_gelu, pre)
    act_low = activation.astype(jnp.bfloat16)
    result = middle + matmul(act_low, outer_weight) + outer_bias.astype(jnp.float32)
    atoms_out = result.astype(jnp.bfloat16).reshape(slots, part_rows, width)
    grad_top = atoms_cotangent.reshape(tokens_here, width)
    grad_outer_weight = outer_sum(act_low, grad_top)
    grad_outer_bias = jnp.sum(grad_top.astype(jnp.float32), axis=0)
    grad_act = times_transposed(grad_top, outer_weight)
    grad_pre = gelu_back(grad_act)[0].astype(jnp.bfloat16)
    grad_inner_weight = outer_sum(inner, grad_pre)
    grad_inner_bias = jnp.sum(grad_pre.astype(jnp.float32), axis=0)
    grad_inner = times_transposed(grad_pre, inner_weight)
    grad_ffn_gain = jnp.sum(grad_inner * standard_two, axis=0)
    grad_ffn_shift = jnp.sum(grad_inner, axis=0)
    grad_middle = grad_top.astype(jnp.float32) + norm_back(
        grad_inner * gain_two, standard_two, inverse_two
    )
    grad_branch = grad_middle.astype(jnp.bfloat16)
    grad_out_weight = outer_sum(mixed, grad_branch)
    grad_out_bias = jnp.sum(grad_branch.astype(jnp.float32), axis=0)
    grad_mixed = times_transposed(grad_branch, out_weight).astype(jnp.bfloat16)
    grad_mixed = grad_mixed.reshape(slots, part_rows, heads, depth)
    grad_probs = jnp.einsum(
        "sqhd,skhd->shqk", grad_mixed, value_heads, preferred_element_type=jnp.float32
    )
    grad_values = jnp.einsum(
        "shqk,sqhd->skhd", probs_low, grad_mixed, preferred_element_type=jnp.float32
    )
    grad_soft = probs * (grad_probs - jnp.sum(probs * grad_probs, axis=-1, keepdims=True))
    pair_grad = (grad_soft + pair_cotangent.astype(jnp.float32)).astype(jnp.bfloat16)
    grad_queries = jnp.einsum(
        "shqk,skhd->sqhd", pair_grad, key_heads, preferred_element_type=jnp.float32
    )
    grad_queries = grad_queries.reshape(tokens_here, width).astype(jnp.bfloat16)
    grad_keys = jnp.einsum(
        "shqk,sqhd->skhd", pair_grad, query_heads, preferred_element_type=jnp.float32
    )
    grad_keys = grad_keys.reshape(slots, full, width)
    grad_values = grad_values.reshape(slots, full, width)
    key_sum, value_sum = (
        lax.psum_scatter(grad_keys, "rows", scatter_dimension=1, tiled=True),
        lax.psum_scatter(grad_values, "rows", scatter_dimension=1, tiled=True),
    )
    key_low = key_sum.astype(jnp.bfloat16).reshape(tokens_here, width)
    value_low = value_sum.astype(jnp.bfloat16).reshape(tokens_here, width)
    grad_query_weight = outer_sum(normed, grad_queries) * scale
    grad_query_bias = jnp.sum(grad_queries.astype(jnp.float32), axis=0) * scale
    grad_key_weight = outer_sum(normed, key_low)
    grad_value_weight = outer_sum(normed, value_low)
    grad_value_bias = jnp.sum(value_low.astype(jnp.float32), axis=0)
    grad_normed = (
        times_transposed(grad_queries, query_weight) * scale
        + times_transposed(key_low, key_weight)
        + times_transposed(value_low, value_weight)
    )
    grad_attn_gain = jnp.sum(grad_normed * standard_one, axis=0)
    grad_attn_shift = jnp.sum(grad_normed, axis=0)
    atoms_grad = grad_middle + norm_back(grad_normed * gain_one, standard_one, inverse_one)
    atoms_grad = atoms_grad.astype(jnp.bfloat16).reshape(slots, part_rows, width)
    partials = (
        grad_attn_gain,
        grad_attn_shift,
        grad_query_weight,
        grad_query_bias,
        grad_key_weight,
        grad_value_weight,
        grad_value_bias,
        grad_out_weight,
        grad_out_bias,
        grad_ffn_gain,
        grad_ffn_shift,
        grad_inner_weight,
        grad_inner_bias,
        grad_outer_weight,
        grad_outer_bias,
    )
    totals = lax.psum(
        (
            partials[0],
            partials[1],
            partials[2],
            partials[3],
            partials[4],
            partials[5],
            partials[6],
            partials[7],
            partials[8],
            partials[9],
            partials[10],
            partials[11],
            partials[12],
            partials[13],
            partials[14],
        ),
        "rows",
    )
    shares = (
        lax.psum_scatter(totals[0], "dp", scatter_dimension=0, tiled=True),
        lax.psum_scatter(totals[1], "dp", scatter_dimension=0, tiled=True),
        lax.psum_scatter(totals[2], "dp", scatter_dimension=0, tiled=True),
        lax.psum_scatter(totals[3], "dp", scatter_dimension=0, tiled=True),
        lax.psum_scatter(totals[4], "dp", scatter_dimension=0, tiled=True),
        lax.psum_scatter(totals[5], "dp", scatter_dimension=0, tiled=True),
        lax.psum_scatter(totals[6], "dp", scatter_dimension=0, tiled=True),
        lax.psum_scatter(totals[7], "dp", scatter_dimension=0, tiled=True),
        lax.psum_scatter(totals[8], "dp", scatter_dimension=0, tiled=True),
        lax.psum_scatter(totals[9], "dp", scatter_dimension=0, tiled=True),
        lax.psum_scatter(totals[10], "dp", scatter_dimension=0, tiled=True),
        lax.psum_scatter(totals[11], "dp", scatter_dimension=0, tiled=True),
        lax.psum_scatter(totals[12], "dp", scatter_dimension=0, tiled=True),
        lax.psum_scatter(totals[13], "dp", scatter_dimension=0, tiled=True),
        lax.psum_scatter(totals[14], "dp", scatter_dimension=0, tiled=True),
    )
    return (
        atoms_out,
        pair_out,
        atoms_grad,
        pair_grad,
        shares[0],
        shares[1],
        shares[2],
        shares[3],
        shares[4],
        shares[5],
        shares[6],
        shares[7],
        shares[8],
        shares[9],
        shares[10],
        shares[11],
        shares[12],
        shares[13],
        shares[14],
    )


def solution(mesh):
    in_specs = (
        P("dp", "rows", None),
        P("dp", None, "rows", None),
        P("dp", None),
        P(),
        P(),
        P(),
        P(),
        P(),
        P(),
        P(),
        P(),
        P(),
        P(),
        P(),
        P(),
        P(),
        P(),
        P(),
        P("dp", "rows", None),
        P("dp", None, "rows", None),
    )
    out_specs = (
        P("dp", "rows", None),
        P("dp", None, "rows", None),
        P("dp", "rows", None),
        P("dp", None, "rows", None),
        P("dp"),
        P("dp"),
        P("dp", None),
        P("dp"),
        P("dp", None),
        P("dp", None),
        P("dp"),
        P("dp", None),
        P("dp"),
        P("dp"),
        P("dp"),
        P("dp", None),
        P("dp"),
        P("dp", None),
        P("dp"),
    )
    return jax.shard_map(local, mesh=mesh, in_specs=in_specs, out_specs=out_specs, check_vma=False)
```

profile of v0, /device:TPU:0, one launch (start us, length us, event | category | flops | bytes accessed | tf_op | source)
XLA Modules:
  0.0 754.8 jit_solution(14454918908746279297)
XLA Ops:
  19.3 1.9 fusion.43
  21.2 1.4 fusion.35
  24.4 1.5 reshape.226
  26.9 10.1 %all_gather.6 = bf16[3,256,512]{2,1,0:T(8,128)(2,1)S(1)} all-gather(bf16[3,64,512]{2,1,0:T(8,128)(2,1)S(1)} %bitcast.101), channel_id=1, replica_groups=mesh['dp'=8,'rows'=4] {'rows'}, dimensions={1}, use_global_device_ids=true | all-gather | bytes 983040 | tf_op jit(solution)/shard_map/all_gather | solution.py:91
  38.1 10.3 %all_gather.7 = bf16[3,256,512]{2,1,0:T(8,128)(2,1)} all-gather(bf16[3,64,512]{2,1,0:T(8,128)(2,1)} %bitcast.100), channel_id=1, replica_groups=mesh['dp'=8,'rows'=4] {'rows'}, dimensions={1}, use_global_device_ids=true | all-gather | bytes 983040 | tf_op jit(solution)/shard_map/all_gather | solution.py:90
  48.4 1.4 copy.73
  49.8 11.5 %fusion.10 = (bf16[3,64,64,256]{3,2,1,0:T(8,128)(2,1)}, f32[3,64,64,256]{3,2,1,0:T(8,128)}) fusion(bf16[3,64,64,256]{3,2,1,0:T(8,128)(2,1)} %param.21, bf16[3,256,512]{1,2,0:T(8,128)(2,1)S(1)} %copy.73, bf16[3,64,64,8]{1,0,3,2:T(4,128)(2,1)S(1)} %reshape.226), kind=kOutput, calls=%fused_computation.12 | convolution fusion | flops 59768832 | bytes 26148864 | tf_op jit(solution)/shard_map/sqhd,skhd->shqk/dot_general | solution.py:96
  61.3 19.9 %fusion.55 = (f32[3,64,64]{2,1,0:T(8,128)S(1)}, f32[3,64,64,256]{3,2,1,0:T(8,128)}) fusion(pred[3,64,256]{2,1,0:T(8,128)(4,1)S(1)} %copy-done.23, f32[3,64,64,256]{3,2,1,0:T(8,128)} %get-tuple-element.67, bf16[3,64,64,256]{3,2,1,0:T(8,128)(2,1)} %param.21), kind=kOutput, calls=%fused_computation.110 | output fusion | flops 25166080 | bytes 31555584 | tf_op jit(solution)/shard_map/sub | solution.py:103
  81.3 5.9 fusion.27
  88.3 2.1 convert_element_type.150
  90.5 1.5 fusion.56
  92.2 2.3 convolution_add_fusion
  94.5 5.7 convert_reduce_fusion
  100.2 1.5 multiply_reduce_fusion.1
  104.3 1.8 copy.76
  106.0 2.1 reshape.231
  108.1 6.7 fusion.21
  114.8 3.1 copy.82
  118.1 7.9 %fusion.40 = f32[3,64,64,256]{3,2,1,0:T(8,128)} fusion(bf16[3,256,512]{1,2,0:T(8,128)(2,1)} %copy.71, bf16[3,64,64,8]{1,0,3,2:T(4,128)(2,1)} %reshape.231), kind=kOutput, calls=%fused_computation.63 | convolution fusion | flops 50331648 | bytes 13565952 | tf_op jit(solution)/shard_map/sqhd,skhd->shqk/dot_general | solution.py:136
  126.1 81.7 %add_convert_fusion = bf16[3,64,64,256]{3,2,1,0:T(8,128)(2,1)} fusion(bf16[3,64,64,256]{3,2,1,0:T(8,128)(2,1)} %param.39, f32[3,64,64,256]{3,2,1,0:T(8,128)} %fusion.40, f32[3,64,64,256]{3,2,1,0:T(8,128)} %get-tuple-element.63, f32[3,64,64]{2,1,0:T(8,128)S(1)} %copy-done.25), kind=kOutput, calls=%fused_computation.2 | output fusion | flops 25178368 | bytes 37797888 | tf_op jit(solution)/shard_map/sub | solution.py:142
  207.7 4.9 convolution_bitcast_fusion
  212.6 3.0 copy.80
  215.7 2.4 fusion.48
  218.2 4.6 convert_reduce_fusion.1
  224.0 1.5 convert_element_type.168
  225.7 1.3 convolution_multiply_fusion
  228.8 1.3 convolution_bitcast_fusion.1
  230.2 14.2 %reduce-scatter.9.cloned.1.call-done = f32[3,64,512]{2,1,0:T(8,128)} async-done(((f32[3,256,512]{2,1,0:T(8,128)}), f32[3,64,512]{2,1,0:T(8,128)}) %reduce-scatter.9.cloned.1.call-update) | async-done | bytes 393232 | tf_op jit(solution)/shard_map/reduce_scatter | solution.py:154
  246.2 1.3 convolution_bitcast_fusion.2
  248.6 2.8 fusion.52
  251.7 2.1 multiply_convert_fusion
  253.9 2.7 fusion.57
  260.3 1.5 convolution_multiply_fusion.1
  264.1 47.1 %reduce-scatter.19.cloned.1.call-done = f32[64,512]{1,0:T(8,128)} async-done(((f32[512,512]{1,0:T(8,128)}), f32[64,512]{1,0:T(8,128)}) %reduce-scatter.19.cloned.1.call-update) | async-done | bytes 131088 | tf_op jit(solution)/shard_map/reduce_scatter | solution.py:218
  311.2 66.1 %reduce-scatter.13.cloned.1.call-done = f32[64,512]{1,0:T(8,128)} async-done(((f32[512,512]{1,0:T(8,128)}), f32[64,512]{1,0:T(8,128)}) %reduce-scatter.13.cloned.1.call-update) | async-done | bytes 131088 | tf_op jit(solution)/shard_map/reduce_scatter | solution.py:213
  377.3 65.7 %reduce-scatter.17.cloned.1.call-done = f32[64,512]{1,0:T(8,128)} async-done(((f32[512,512]{1,0:T(8,128)}), f32[64,512]{1,0:T(8,128)}) %reduce-scatter.17.cloned.1.call-update) | async-done | bytes 131088 | tf_op jit(solution)/shard_map/reduce_scatter | solution.py:216
  443.0 66.1 %reduce-scatter.15.cloned.1.call-done = f32[64,512]{1,0:T(8,128)} async-done(((f32[512,512]{1,0:T(8,128)}), f32[64,512]{1,0:T(8,128)}) %reduce-scatter.15.cloned.1.call-update) | async-done | bytes 131088 | tf_op jit(solution)/shard_map/reduce_scatter | solution.py:215
  509.0 90.6 %reduce-scatter.21.cloned.1.call-done = f32[64,2048]{1,0:T(8,128)} async-done(((f32[512,2048]{1,0:T(8,128)}), f32[64,2048]{1,0:T(8,128)}) %reduce-scatter.21.cloned.1.call-update) | async-done | bytes 524304 | tf_op jit(solution)/shard_map/reduce_scatter | solution.py:222
  599.6 91.7 %reduce-scatter.23.cloned.1.call-done = f32[256,512]{1,0:T(8,128)} async-done(((f32[2048,512]{1,0:T(8,128)}), f32[256,512]{1,0:T(8,128)}) %reduce-scatter.23.cloned.1.call-update) | async-done | bytes 524304 | tf_op jit(solution)/shard_map/reduce_scatter | solution.py:224
  691.5 2.3 fusion.53
  693.8 35.9 %all-reduce.9 = (f32[512]{0:T(512)S(1)}, f32[512]{0:T(512)S(1)}, f32[512]{0:T(512)S(1)}, f32[512]{0:T(512)S(1)}, f32[512]{0:T(512)S(1)}, /*index=5*/f32[512]{0:T...) all-reduce(f32[512]{0:T(512)S(1)} %get-tuple-element.26, ...), channel_id=4, replica_groups=mesh['dp'=8,'rows'=4] {'dp'}, use_global_device_ids=true, to_apply=%region_17.18.clone | all-reduce | flops 6144 | bytes 49152
  730.4 7.0 all-reduce.10
  737.4 1.9 add_convert_fusion.3
  739.3 1.6 copy.99
  740.9 1.6 copy.100
  742.5 1.6 copy.101
  744.0 1.6 copy.102
  745.6 1.9 copy.103
  (156 shorter events, 32.8 us)
Async XLA Ops:
  7.2 87.3 %copy-start = (bf16[2048,512]{1,0:T(8,128)(2,1)S(1)}, bf16[2048,512]{1,0:T(8,128)(2,1)}, u32[]{:S(2)}) copy-start(bf16[2048,512]{1,0:T(8,128)(2,1)} %param.36) | copy-start | bytes 6291460
  7.2 16.2 %copy-start.8 = (bf16[512,512]{1,0:T(8,128)(2,1)S(1)}, bf16[512,512]{1,0:T(8,128)(2,1)}, u32[]{:S(2)}) copy-start(bf16[512,512]{1,0:T(8,128)(2,1)} %param.27) | copy-start | bytes 1572868
  7.2 219.9 %reduce-scatter.11.cloned.1.call-start = ((), (), s32[]{:S(2)}) async-start(), calls=%async_computation.9 | async-start | bytes 1966080 | tf_op jit(solution)/shard_map/reduce_scatter | solution.py:155
  8.6 10.8 %copy-start.31 = (f32[192]{0:T(256)}, f32[192]{0:T(256)S(1)}, u32[]{:S(2)}) copy-start(f32[192]{0:T(256)S(1)} %div.35) | copy-start | bytes 2308
  11.8 7.6 %copy-start.27 = (f32[512]{0:T(512)}, f32[512]{0:T(512)S(1)}, u32[]{:S(2)}) copy-start(f32[512]{0:T(512)S(1)} %convert_element_type.138) | copy-start | bytes 6148
  17.2 1.5 copy-start.29
  17.3 2.1 copy-start.33
  21.2 4.6 copy-start.10
  25.9 24.0 %copy-start.5 = (bf16[3,64,64,8]{1,0,3,2:T(4,128)(2,1)}, bf16[3,64,64,8]{1,0,3,2:T(4,128)(2,1)S(1)}, u32[]{:S(2)}) copy-start(bf16[3,64,64,8]{1,0,3,2:T(4,128)(2,1)S(1)} %reshape.226) | copy-start | bytes 589828
  49.8 11.5 %copy-start.23 = (pred[3,64,256]{2,1,0:T(8,128)(4,1)S(1)}, pred[3,64,256]{2,1,0:T(8,128)(4,1)}, u32[]{:S(2)}) copy-start(pred[3,64,256]{2,1,0:T(8,128)(4,1)} %broadcast_compare_fusion) | copy-start | bytes 147460
  81.3 5.9 copy-start.24
  87.2 3.3 copy-start.1
  87.2 3.3 copy-start.36
  87.2 5.0 copy-start.26
  92.2 2.3 copy-start.14
  94.5 5.8 copy-start.2
  94.5 5.7 copy-start.13
  100.2 1.5 copy-start.20
  101.7 1.5 copy-start.12
  102.5 0.8 copy-start.3
  117.9 126.6 %reduce-scatter.9.cloned.1.call-start = ((), (), s32[]{:S(2)}) async-start(), calls=%async_computation.8 | async-start | bytes 1966080 | tf_op jit(solution)/shard_map/reduce_scatter | solution.py:154
  118.1 7.9 %copy-start.25 = (f32[3,64,64]{2,1,0:T(8,128)S(1)}, f32[3,64,64]{2,1,0:T(8,128)}, u32[]{:S(2)}) copy-start(f32[3,64,64]{2,1,0:T(8,128)} %copy-done.24) | copy-start | bytes 147460
  126.1 81.7 %copy-start.6 = (bf16[3,64,64,8]{1,0,3,2:T(4,128)(2,1)S(1)}, bf16[3,64,64,8]{1,0,3,2:T(4,128)(2,1)}, u32[]{:S(2)}) copy-start(bf16[3,64,64,8]{1,0,3,2:T(4,128)(2,1)} %copy-done.5) | copy-start | bytes 589828
  215.7 95.6 %reduce-scatter.19.cloned.1.call-start = ((), (), s32[]{:S(2)}) async-start(), calls=%async_computation.13 | async-start | bytes 1179648 | tf_op jit(solution)/shard_map/reduce_scatter | solution.py:218
  218.2 159.1 %reduce-scatter.13.cloned.1.call-start = ((), (), s32[]{:S(2)}) async-start(), calls=%async_computation.10 | async-start | bytes 1179648 | tf_op jit(solution)/shard_map/reduce_scatter | solution.py:213
  222.8 2.7 copy-start.28
  222.8 2.7 copy-start.30
  225.5 2.6 copy-start.7
  227.0 215.9 %reduce-scatter.17.cloned.1.call-start = ((), (), s32[]{:S(2)}) async-start(), calls=%async_computation.12 | async-start | bytes 1179648 | tf_op jit(solution)/shard_map/reduce_scatter | solution.py:216
  230.2 278.9 %reduce-scatter.15.cloned.1.call-start = ((), (), s32[]{:S(2)}) async-start(), calls=%async_computation.11 | async-start | bytes 1179648 | tf_op jit(solution)/shard_map/reduce_scatter | solution.py:215
  247.5 1.1 copy-start.21
  247.5 352.1 %reduce-scatter.21.cloned.1.call-start = ((), (), s32[]{:S(2)}) async-start(), calls=%async_computation.14 | async-start | bytes 4718592 | tf_op jit(solution)/shard_map/reduce_scatter | solution.py:222
  251.4 440.0 %reduce-scatter.23.cloned.1.call-start = ((), (), s32[]{:S(2)}) async-start(), calls=%async_computation.15 | async-start | bytes 4718592 | tf_op jit(solution)/shard_map/reduce_scatter | solution.py:224
  251.7 2.2 copy-start.15
  256.6 2.5 copy-start.40
  256.6 482.6 %all-reduce.14.cloned.1.call-start = ((), (), s32[]{:S(2)}) async-start(), calls=%async_computation.16 | async-start | bytes 3145728 | tf_op jit(solution)/shard_map/psum | solution.py:190
  261.7 1.3 copy-start.9
  261.7 1.3 copy-start.19
  263.0 428.4 %copy-start.11 = (bf16[512,512]{1,0:T(8,128)(2,1)S(1)}, bf16[512,512]{1,0:T(8,128)(2,1)}, u32[]{:S(2)}) copy-start(bf16[512,512]{1,0:T(8,128)(2,1)} %param.28) | copy-start | bytes 1572868
  263.0 428.4 %copy-start.17 = (bf16[3,64,512]{2,1,0:T(8,128)(2,1)S(1)}, bf16[3,64,512]{2,1,0:T(8,128)(2,1)}, u32[]{:S(2)}) copy-start(bf16[3,64,512]{2,1,0:T(8,128)(2,1)} %copy-done.16) | copy-start | bytes 589828
  263.0 428.4 %copy-start.32 = (f32[192]{0:T(256)S(1)}, f32[192]{0:T(256)}, u32[]{:S(2)}) copy-start(f32[192]{0:T(256)} %copy-done.31) | copy-start | bytes 2308
  263.0 428.4 %copy-start.34 = (f32[192]{0:T(256)S(1)}, f32[192]{0:T(256)}, u32[]{:S(2)}) copy-start(f32[192]{0:T(256)} %copy-done.33) | copy-start | bytes 2308
  691.4 2.4 copy-start.35
  691.4 2.4 copy-start.37
  691.4 2.4 copy-start.38
  691.4 2.4 copy-start.39
  691.4 46.0 %copy-start.4 = (f32[192,512]{1,0:T(8,128)S(1)}, f32[192,512]{1,0:T(8,128)}, u32[]{:S(2)}) copy-start(f32[192,512]{1,0:T(8,128)} %copy-done.3) | copy-start | bytes 1179652
  739.3 8.2 %copy-start.22 = (f32[256,512]{1,0:T(8,128)S(1)}, f32[256,512]{1,0:T(8,128)}, u32[]{:S(2)}) copy-start(f32[256,512]{1,0:T(8,128)} %get-tuple-element.91) | copy-start | bytes 1572868
  (3 other events, 2.0 us)
Sparse Core Ops, SparseCore 0:
  118.0 28.8 reduce-scatter.10
  215.8 28.6 reduce-scatter.8
  247.9 63.3 reduce-scatter.18
  314.9 62.3 reduce-scatter.12
  380.6 62.3 reduce-scatter.16
  446.6 62.4 reduce-scatter.14
  512.7 86.9 reduce-scatter.20
  603.7 87.6 reduce-scatter.22
  694.2 43.8 all-reduce.13
where the time goes:
time: 756 us; the launch traced here: 755 us
  waiting for transfers between devices  442 us (58%)
  other arithmetic  123 us (16%)
  matrix products  74.7 us (10%)
  blocking collectives  63.3 us (8%)
  local copies, waits for them, and re-layouts  35.2 us (5%)
  between operations  15.6 us (2%)
    reduce_scatter x1, waiting for transfers between devices, local(): lax.psum_scatter(totals[13], 'dp', scatter_dimension=0, tiled=True)  91.7 us
    reduce_scatter x1, waiting for transfers between devices, local(): lax.psum_scatter(totals[11], 'dp', scatter_dimension=0, tiled=True)  90.6 us
    sub x1, other arithmetic, local(): grad_probs - jnp.sum(probs * grad_probs, axis=-1, keepdims=True)  81.7 us
    reduce_scatter x1, waiting for transfers between devices, local(): lax.psum_scatter(totals[4], 'dp', scatter_dimension=0, tiled=True)  66.1 us
    reduce_scatter x1, waiting for transfers between devices, local(): lax.psum_scatter(totals[2], 'dp', scatter_dimension=0, tiled=True)  66.1 us
    reduce_scatter x1, waiting for transfers between devices, local(): lax.psum_scatter(totals[5], 'dp', scatter_dimension=0, tiled=True)  65.7 us
    reduce_scatter x1, waiting for transfers between devices, local(): lax.psum_scatter(totals[7], 'dp', scatter_dimension=0, tiled=True)  47.1 us
    unnamed x1, blocking collectives  35.9 us
  transfers between devices with their start and end apart: 9, of which 7 were waited for; matrix products, arithmetic and copies ran while one was open for 17% of the time, Pallas kernels for 0%

commit v1 on v0

v1 whole, which is shorter than its diff:
```python
import functools

import jax
import jax.numpy as jnp
from jax import lax
from jax.experimental import pallas as pl
from jax.experimental.pallas import tpu as pltpu
from jax.sharding import PartitionSpec as P

f32, bf16 = jnp.float32, jnp.bfloat16
BIG = 1e9
HPL = 16
CHUNK = 8
STEP = 32


def standardize(value):
    centred = value - jnp.mean(value, axis=-1, keepdims=True)
    inverse = lax.rsqrt(jnp.mean(centred * centred, axis=-1, keepdims=True) + 1e-05)
    return (centred * inverse, inverse)


def norm_back(grad_normed, standard, inverse):
    return inverse * (
        grad_normed
        - jnp.mean(grad_normed, axis=-1, keepdims=True)
        - standard * jnp.mean(grad_normed * standard, axis=-1, keepdims=True)
    )


def matmul(left, right):
    return jnp.dot(left, right, preferred_element_type=f32)


def times_transposed(left, right):
    return lax.dot_general(left, right, (((1,), (1,)), ((), ())), preferred_element_type=f32)


def outer_sum(left, right):
    return lax.dot_general(left, right, (((0,), (0,)), ((), ())), preferred_element_type=f32)


def forward_kernel(q_ref, kt_ref, v_ref, bias_ref, mask_ref, out_ref, e_ref, mix_ref, rl_ref):
    _, heads, rows, full = bias_ref.shape
    lane_head = lax.broadcasted_iota(jnp.int32, (rows, 128), 1) // 8
    mask = mask_ref[0]
    ones = jnp.ones((full, 128), bf16)
    for b in range(heads // HPL):
        cols = slice(128 * b, 128 * b + 128)
        q = q_ref[0, :, cols].astype(f32)
        kt = kt_ref[0, cols, :]
        v = jnp.concatenate([v_ref[0, :, cols], ones], axis=1)
        mixed = jnp.zeros((rows, 128), f32)
        total = jnp.zeros((rows, 128), f32)
        for c in range(HPL // CHUNK):
            own = [lane_head == CHUNK * c + i for i in range(CHUNK)]
            left = jnp.concatenate([jnp.where(o, q, 0.0).astype(bf16) for o in own], axis=0)
            scores = matmul(left, kt).reshape(CHUNK, rows, full)
            hs = slice(HPL * b + CHUNK * c, HPL * b + CHUNK * (c + 1))
            scores = scores + bias_ref[0, hs].astype(f32)
            out_ref[0, hs] = scores.astype(bf16)
            scores = scores + mask[None]
            highest = jnp.max(scores, axis=-1, keepdims=True)
            e = jnp.exp(scores - highest).astype(bf16)
            e_ref[0, hs] = e
            sums = matmul(e.reshape(CHUNK * rows, full), v)
            for i, o in enumerate(own):
                mixed = jnp.where(o, sums[rows * i : rows * (i + 1), :128], mixed)
                total = jnp.where(o, sums[rows * i : rows * (i + 1), 128:], total)
        inverse = 1.0 / total
        mix_ref[0, :, cols] = mixed * inverse
        rl_ref[0, :, cols] = inverse


def attention_forward(q, kt, v, bias, mask):
    slots, heads, rows, full = bias.shape
    step = min(STEP, heads)
    width = step * 8
    natural = lambda n: pl.BlockSpec((1, n, width), lambda s, h: (s, 0, h))
    pair = pl.BlockSpec((1, step, rows, full), lambda s, h: (s, h, 0, 0))
    return pl.pallas_call(
        forward_kernel,
        grid=(slots, heads // step),
        in_specs=[
            natural(rows),
            pl.BlockSpec((1, width, full), lambda s, h: (s, h, 0)),
            natural(full),
            pair,
            pl.BlockSpec((1, rows, full), lambda s, h: (s, 0, 0)),
        ],
        out_specs=[pair, pair, natural(rows), natural(rows)],
        out_shape=[
            jax.ShapeDtypeStruct(bias.shape, bf16),
            jax.ShapeDtypeStruct(bias.shape, bf16),
            jax.ShapeDtypeStruct(q.shape, f32),
            jax.ShapeDtypeStruct(q.shape, f32),
        ],
        name="attention_forward",
        cost_estimate=pl.CostEstimate(
            flops=2 * bias.size * 512, transcendentals=bias.size, bytes_accessed=bias.size * 6
        ),
        compiler_params=pltpu.CompilerParams(vmem_limit_bytes=48 << 20),
    )(q, kt, v, bias, mask)


def backward_kernel(
    qt_ref, dm_ref, dmt_ref, nm_ref, k_ref, vt_ref, e_ref, cot_ref, pg_ref, dq_ref, dkt_ref, dvt_ref
):
    _, heads, rows, full = cot_ref.shape
    lane_head = lax.broadcasted_iota(jnp.int32, (rows, 128), 1) // 8
    shape = (8 * CHUNK, CHUNK * rows)
    same = lax.broadcasted_iota(jnp.int32, shape, 0) // 8 == lax.broadcasted_iota(jnp.int32, shape, 1) // rows
    ones = jnp.ones((128, full), bf16)
    for b in range(heads // HPL):
        cols = slice(128 * b, 128 * b + 128)
        dm = dm_ref[0, :, cols].astype(f32)
        nm = nm_ref[0, :, cols].astype(f32)
        vt = jnp.concatenate([vt_ref[0, cols, :], ones], axis=0)
        k = k_ref[0, :, cols]
        dq = jnp.zeros((rows, 128), f32)
        for c in range(HPL // CHUNK):
            own = [lane_head == CHUNK * c + i for i in range(CHUNK)]
            left = jnp.concatenate(
                [
                    jnp.concatenate([jnp.where(o, dm, 0.0), jnp.where(o, nm, 0.0)], axis=1).astype(bf16)
                    for o in own
                ],
                axis=0,
            )
            centred = matmul(left, vt).reshape(CHUNK, rows, full)
            hs = slice(HPL * b + CHUNK * c, HPL * b + CHUNK * (c + 1))
            e = e_ref[0, hs]
            grad = (e.astype(f32) * centred + cot_ref[0, hs].astype(f32)).astype(bf16)
            pg_ref[0, hs] = grad
            grad = grad.reshape(CHUNK * rows, full)
            sums = matmul(grad, k)
            for i, o in enumerate(own):
                dq = jnp.where(o, sums[rows * i : rows * (i + 1)], dq)
            rs = slice(hs.start * 8, hs.stop * 8)
            spread = lambda ref: jnp.where(
                same, jnp.concatenate([ref[0, rs, :].astype(f32)] * CHUNK, axis=1), 0.0
            ).astype(bf16)
            dkt_ref[0, rs, :] = matmul(spread(qt_ref), grad).astype(bf16)
            dvt_ref[0, rs, :] = matmul(spread(dmt_ref), e.reshape(CHUNK * rows, full)).astype(bf16)
        dq_ref[0, :, cols] = dq.astype(bf16)


def attention_backward(qt, dm, dmt, nm, k, vt, e, cot):
    slots, heads, rows, full = cot.shape
    step = min(STEP, heads)
    width = step * 8
    natural = lambda n: pl.BlockSpec((1, n, width), lambda s, h: (s, 0, h))
    turned = lambda n: pl.BlockSpec((1, width, n), lambda s, h: (s, h, 0))
    pair = pl.BlockSpec((1, step, rows, full), lambda s, h: (s, h, 0, 0))
    return pl.pallas_call(
        backward_kernel,
        grid=(slots, heads // step),
        in_specs=[
            turned(rows),
            natural(rows),
            turned(rows),
            natural(rows),
            natural(full),
            turned(full),
            pair,
            pair,
        ],
        out_specs=[pair, natural(rows), turned(full), turned(full)],
        out_shape=[
            jax.ShapeDtypeStruct(cot.shape, bf16),
            jax.ShapeDtypeStruct(dm.shape, bf16),
            jax.ShapeDtypeStruct(vt.shape, bf16),
            jax.ShapeDtypeStruct(vt.shape, bf16),
        ],
        name="attention_backward",
        cost_estimate=pl.CostEstimate(
            flops=2 * cot.size * 768, transcendentals=0, bytes_accessed=cot.size * 6
        ),
        compiler_params=pltpu.CompilerParams(vmem_limit_bytes=48 << 20),
    )(qt, dm, dmt, nm, k, vt, e, cot)


def ffn_grad_kernel(me_ref, act_ref, dy_ref, inner_ref, dpre_ref, mixed_ref, branch_ref, out_ref):
    parts = out_ref.shape[0]
    me = me_ref[0]
    tall = act_ref.shape[2] // parts
    short = inner_ref.shape[2] // parts
    half = dy_ref.shape[2]
    blocks = dpre_ref.shape[2] // half
    both = lambda left, right: sum(outer_sum(left[i], right[i]) for i in range(2))
    inner = [inner_ref[i] for i in range(2)]
    for cb in range(blocks):
        grad = both(inner, [dpre_ref[i, :, half * cb : half * (cb + 1)] for i in range(2)]).astype(bf16)
        for j in range(parts):
            out_ref[me ^ j, pl.ds(tall + short * cb, short), :] = grad[short * j : short * (j + 1)]
    grad = both([mixed_ref[i] for i in range(2)], [branch_ref[i] for i in range(2)]).astype(bf16)
    for j in range(parts):
        out_ref[me ^ j, pl.ds(tall + short * blocks, short), :] = grad[short * j : short * (j + 1)]
    dy = [dy_ref[i] for i in range(2)]
    wide = max(tall, 256)
    for n in range(act_ref.shape[2] // wide):
        grad = both([act_ref[i, :, wide * n : wide * (n + 1)] for i in range(2)], dy).astype(bf16)
        for j in range(wide // tall):
            out_ref[me ^ (n * (wide // tall) + j), pl.ds(0, tall), :] = grad[tall * j : tall * (j + 1)]


def ffn_grads(me, parts, act, dy, inner, dpre, mixed, branch):
    half = dy.shape[2]
    rows = (act.shape[2] * 2 + mixed.shape[2]) // parts
    vm = pl.BlockSpec(memory_space=pltpu.VMEM)
    return pl.pallas_call(
        ffn_grad_kernel,
        in_specs=[pl.BlockSpec(memory_space=pltpu.SMEM)] + [vm] * 6,
        out_specs=vm,
        out_shape=jax.ShapeDtypeStruct((parts, rows, half), bf16),
        name="ffn_grads",
        cost_estimate=pl.CostEstimate(flops=2 * 384 * 2304 * 512, transcendentals=0, bytes_accessed=6 << 20),
        compiler_params=pltpu.CompilerParams(vmem_limit_bytes=40 << 20),
    )(me, act, dy, inner, dpre, mixed, branch)


def attn_grad_kernel(scale, me_ref, normed_ref, own_ref, dq_ref, dkt_ref, dvt_ref, vec_ref, out_ref):
    parts = out_ref.shape[0]
    me = me_ref[0]
    short = normed_ref.shape[2] // parts
    slots = normed_ref.shape[0]

    def put(grad, at):
        grad = grad.astype(bf16)
        for j in range(parts):
            out_ref[me ^ j, pl.ds(at * short, short), :] = grad[short * j : short * (j + 1)]

    put(sum(outer_sum(own_ref[i], dq_ref[i]) for i in range(2)) * scale, 0)
    normed = [normed_ref[s].T for s in range(slots)]
    for at, ref in ((1, dkt_ref), (2, dvt_ref)):
        total = 0.0
        for s in range(slots):
            both = (ref[0, s].astype(f32) + ref[1, s].astype(f32)).astype(bf16)
            total = total + times_transposed(normed[s], both)
        put(total, at)
    out_ref[:, pl.ds(3 * short, 16), :] = vec_ref[...]


def attn_grads(me, parts, scale, normed, own, dq, dkt, dvt, vec):
    half = dq.shape[2]
    vm = pl.BlockSpec(memory_space=pltpu.VMEM)
    return pl.pallas_call(
        functools.partial(attn_grad_kernel, scale),
        in_specs=[pl.BlockSpec(memory_space=pltpu.SMEM)] + [vm] * 6,
        out_specs=vm,
        out_shape=jax.ShapeDtypeStruct((parts, 3 * normed.shape[2] // parts + 16, half), bf16),
        name="attn_grads",
        cost_estimate=pl.CostEstimate(flops=2 * 768 * 512 * 768, transcendentals=0, bytes_accessed=4 << 20),
        compiler_params=pltpu.CompilerParams(vmem_limit_bytes=40 << 20),
    )(me, normed, own, dq, dkt, dvt, vec)


def make_swap(parts, group):
    def swap(array, dp_bit=None, row_bit=None):
        pairs = []
        for d in range(parts):
            for r in range(group):
                e = d if dp_bit is None else d ^ (1 << dp_bit)
                t = r if row_bit is None else r ^ (1 << row_bit)
                pairs.append((d * group + r, e * group + t))
        return lax.ppermute(array, ("dp", "rows"), pairs)

    return swap


def add_low(left, right):
    return (left.astype(f32) + right.astype(f32)).astype(bf16)


def fold(swap, grads, bit):
    count = grads.shape[0]
    low = 1 << bit
    view = grads.reshape((count // (2 * low), 2, low) + grads.shape[1:])
    got = swap(view[:, 1], dp_bit=bit)
    return view[:, 0], got


def scatter_first(swap, grads, bits):
    remaining = list(bits)
    for n, bit in enumerate(remaining):
        view, got = fold_at(swap, grads, bit, remaining[n + 1 :])
        grads = add_low(view, got)
    return grads


def fold_at(swap, grads, bit, later):
    at = sum(1 for b in later if b < bit)
    low = 1 << at
    view = grads.reshape((grads.shape[0] // (2 * low), 2, low) + grads.shape[1:])
    keep, send = view[:, 0], view[:, 1]
    flat = lambda a: a.reshape((-1,) + grads.shape[1:])
    return flat(keep), swap(flat(send), dp_bit=bit)


def reduce_x_first(swap, grads, bits):
    total = scatter_first(swap, grads, bits)[0]
    return total.astype(f32) + swap(total, row_bit=1).astype(f32)


def reduce_y_first(swap, grads, bits, y):
    parts, rows, half = grads.shape
    view = grads.reshape(parts, 2, rows // 2, half)
    keep = lax.dynamic_index_in_dim(view, y, 1, keepdims=False)
    send = lax.dynamic_index_in_dim(view, 1 - y, 1, keepdims=False)
    total = scatter_first(swap, add_low(keep, swap(send, row_bit=1)), bits)[0]
    other = swap(total, row_bit=1)
    lower = jnp.where(y == 0, total, other)
    upper = jnp.where(y == 0, other, total)
    return jnp.concatenate([lower, upper], axis=0).astype(f32)


def local(
    parts,
    group,
    atoms,
    pair_bias,
    mol_counts,
    attn_gain,
    attn_shift,
    query_weight,
    query_bias,
    key_weight,
    value_weight,
    value_bias,
    out_weight,
    out_bias,
    ffn_gain,
    ffn_shift,
    inner_weight,
    inner_bias,
    outer_weight,
    outer_bias,
    atoms_cotangent,
    pair_cotangent,
):
    slots, part_rows, width = atoms.shape
    heads = pair_bias.shape[1]
    full = pair_bias.shape[3]
    depth = width // heads
    scale = depth ** (-0.5)
    here = slots * part_rows
    hidden = inner_weight.shape[1]
    half = width // 2
    swap = make_swap(parts, group)
    row = lax.axis_index("rows")
    core, y = row % 2, row // 2
    dp = lax.axis_index("dp")
    me = dp.astype(jnp.int32).reshape(1)
    dp_bits = list(range(parts.bit_length() - 1))

    sibling = swap(atoms, row_bit=0)
    across = swap(atoms, row_bit=1)
    corner = swap(across, row_bit=0)
    stack = jnp.stack([atoms, sibling, across, corner])
    order = jnp.arange(group, dtype=jnp.int32) ^ row
    atoms_all = jnp.take(stack, order, axis=0)
    atoms_all = jnp.swapaxes(atoms_all, 0, 1).reshape(slots, full, width)
    top_other = swap(atoms_cotangent, row_bit=0)

    cumulative = jnp.cumsum(mol_counts, axis=1)
    position = jnp.arange(full, dtype=jnp.int32)
    segment = jnp.sum(
        (cumulative[:, None, :] <= position[None, :, None]).astype(jnp.int32), axis=-1
    )
    query_segment = lax.dynamic_slice_in_dim(segment, row * part_rows, part_rows, 1)
    mask = jnp.where(query_segment[:, :, None] == segment[:, None, :], 0.0, -BIG).astype(f32)

    gain_one = attn_gain.astype(f32)
    shift_one = attn_shift.astype(f32)
    gain_two = ffn_gain.astype(f32)
    atoms_flat = atoms.astype(f32).reshape(here, width)
    standard_one, inverse_one = standardize(atoms_flat)
    normed = (standard_one * gain_one + shift_one).astype(bf16)
    standard_sib, _ = standardize(sibling.astype(f32).reshape(here, width))
    normed_sib = (standard_sib * gain_one + shift_one).astype(bf16)
    standard_all, _ = standardize(atoms_all.astype(f32).reshape(slots * full, width))
    normed_all = (standard_all * gain_one + shift_one).astype(bf16)
    queries = ((matmul(normed, query_weight) + query_bias.astype(f32)) * scale).astype(bf16)
    keys = matmul(normed_all, key_weight).astype(bf16).reshape(slots, full, width)
    values = (matmul(normed_all, value_weight) + value_bias.astype(f32)).astype(bf16)
    values = values.reshape(slots, full, width)
    queries = queries.reshape(slots, part_rows, width)
    turn = lambda a: jnp.swapaxes(a, 1, 2)
    values_turned = turn(values)
    pair_out, weights, mixed_wide, inverse_sum = attention_forward(
        queries, turn(keys), values, pair_bias, mask
    )
    mixed = mixed_wide.reshape(here, width).astype(bf16)
    middle = atoms_flat + matmul(mixed, out_weight) + out_bias.astype(f32)
    standard_two, inverse_two = standardize(middle)
    inner = (standard_two * gain_two + ffn_shift.astype(f32)).astype(bf16)
    pre = matmul(inner, inner_weight) + inner_bias.astype(f32)
    activation, gelu_back = jax.vjp(lambda u: jax.nn.gelu(u, approximate=False), pre)
    act_low = activation.astype(bf16)
    result = middle + matmul(act_low, outer_weight) + outer_bias.astype(f32)
    atoms_out = result.astype(bf16).reshape(slots, part_rows, width)
    grad_top = atoms_cotangent.reshape(here, width)
    grad_act = times_transposed(grad_top, outer_weight)
    grad_pre = gelu_back(grad_act)[0].astype(bf16)
    grad_inner = times_transposed(grad_pre, inner_weight)
    grad_middle = grad_top.astype(f32) + norm_back(grad_inner * gain_two, standard_two, inverse_two)
    grad_branch = grad_middle.astype(bf16)
    grad_mixed = times_transposed(grad_branch, out_weight).astype(bf16)

    def pick(array, which):
        return lax.dynamic_slice_in_dim(array, which * (array.shape[1] // 2), array.shape[1] // 2, 1)

    pair_of = lambda own, send: jnp.stack([own, swap(send, row_bit=0)])
    act_two = pair_of(act_low, act_low)
    inner_two = pair_of(inner, inner)
    mixed_two = pair_of(mixed, mixed)
    pre_two = pair_of(pick(grad_pre, core), pick(grad_pre, 1 - core))
    branch_two = pair_of(pick(grad_branch, core), pick(grad_branch, 1 - core))
    top_two = jnp.stack([pick(grad_top, core), pick(top_other.reshape(here, width), core)])
    ffn_packed = ffn_grads(me, parts, act_two, top_two, inner_two, pre_two, mixed_two, branch_two)
    cut = hidden // parts
    ffn_first = ffn_packed[:, :cut]
    ffn_second = ffn_packed[:, cut:]
    first_total = reduce_x_first(swap, ffn_first, dp_bits)
    second_total = reduce_y_first(swap, ffn_second, dp_bits, y)

    scaled = grad_mixed.astype(f32) * inverse_sum.reshape(here, width)
    centre = (-scaled * mixed_wide.reshape(here, width)).astype(bf16).reshape(queries.shape)
    scaled = scaled.astype(bf16).reshape(queries.shape)
    pair_grad, grad_queries, dkt, dvt = attention_backward(
        turn(queries), scaled, turn(scaled), centre, keys, values_turned, weights, pair_cotangent
    )
    grad_queries = grad_queries.reshape(here, width)

    partial = jnp.einsum("sok,io->ski", dkt, key_weight, preferred_element_type=f32) + jnp.einsum(
        "sok,io->ski", dvt, value_weight, preferred_element_type=f32
    )
    partial = partial.astype(bf16).reshape(slots, group, part_rows, width)
    partial = jnp.take(jnp.swapaxes(partial, 0, 1), order, axis=0)
    partial = partial.reshape(2, 2, slots, part_rows, width)
    chip = add_low(partial[:, 0], swap(partial[:, 1], row_bit=0))
    grad_normed = (
        times_transposed(grad_queries, query_weight) * scale
        + (chip[0].astype(f32) + swap(chip[1], row_bit=1).astype(f32)).reshape(here, width)
    )
    atoms_grad = grad_middle + norm_back(grad_normed * gain_one, standard_one, inverse_one)
    atoms_grad = atoms_grad.astype(bf16).reshape(slots, part_rows, width)

    short = (
        jnp.sum(grad_normed * standard_one, axis=0),
        jnp.sum(grad_normed, axis=0),
        jnp.sum(grad_queries.astype(f32), axis=0) * scale,
        jnp.sum(dvt.astype(f32), axis=(0, 2)),
        jnp.sum(grad_branch.astype(f32), axis=0),
        jnp.sum(grad_inner * standard_two, axis=0),
        jnp.sum(grad_inner, axis=0),
        jnp.sum(grad_top.astype(f32), axis=0),
    )
    vectors = jnp.concatenate(
        [v.reshape(parts, -1) for v in short] + [jnp.sum(grad_pre.astype(f32), axis=0).reshape(parts, -1)],
        axis=1,
    )
    vectors = vectors + swap(vectors, row_bit=0)
    vectors = jnp.take(vectors, jnp.arange(parts, dtype=jnp.int32) ^ dp, axis=0)
    vec = jnp.pad(vectors.astype(bf16), ((0, 0), (0, 16 * half - vectors.shape[1]))).reshape(parts, 16, half)

    def pick_rows(array, which):
        return lax.dynamic_slice_in_dim(array, which * half, half, 1)

    attn_packed = attn_grads(
        me,
        parts,
        scale,
        normed_all.reshape(slots, full, width),
        jnp.stack([normed, normed_sib]),
        pair_of(pick(grad_queries, core), pick(grad_queries, 1 - core)),
        pair_of(pick_rows(dkt, core), pick_rows(dkt, 1 - core)),
        pair_of(pick_rows(dvt, core), pick_rows(dvt, 1 - core)),
        vec,
    )
    share = width // parts
    third_total = reduce_x_first(swap, attn_packed[:, : attn_packed.shape[1] // 2], dp_bits)
    fourth_total = reduce_y_first(swap, attn_packed[:, attn_packed.shape[1] // 2 :], dp_bits, y)

    total = jnp.concatenate([first_total, second_total, third_total, fourth_total], axis=0)
    other = swap(total, row_bit=0)
    left = jnp.where(core == 0, total, other)
    right = jnp.where(core == 0, other, total)
    joined = jnp.stack([left, right])
    outer_share = hidden // parts
    blocks = hidden // 2 // half

    def flat(a, n):
        return jnp.swapaxes(joined[:, a : a + n], 0, 1).reshape(n, width)

    grad_outer_weight = flat(0, outer_share)
    a = outer_share
    grad_inner_weight = joined[:, a : a + share * blocks].reshape(2, blocks, share, half)
    grad_inner_weight = grad_inner_weight.transpose(2, 0, 1, 3).reshape(share, hidden)
    a += share * blocks
    grad_out_weight = flat(a, share)
    a += share
    grad_query_weight, grad_key_weight, grad_value_weight = (flat(a + share * i, share) for i in range(3))
    a += 3 * share
    vec_total = joined[0, a : a + 16].reshape(-1)
    v = [vec_total[share * i : share * (i + 1)] for i in range(8)]
    grad_inner_bias = vec_total[8 * share : 8 * share + outer_share]
    return (
        atoms_out,
        pair_out,
        atoms_grad,
        pair_grad,
        v[0],
        v[1],
        grad_query_weight,
        v[2],
        grad_key_weight,
        grad_value_weight,
        v[3],
        grad_out_weight,
        v[4],
        v[5],
        v[6],
        grad_inner_weight,
        grad_inner_bias,
        grad_outer_weight,
        v[7],
    )


def solution(mesh):
    one, two = P("dp"), P("dp", None)
    atoms_spec, pair_spec = P("dp", "rows", None), P("dp", None, "rows", None)
    in_specs = (atoms_spec, pair_spec, two) + (P(),) * 15 + (atoms_spec, pair_spec)
    out_specs = (
        (atoms_spec, pair_spec, atoms_spec, pair_spec, one, one, two, one, two, two, one, two)
        + (one, one, one, two, one, two, one)
    )
    run = functools.partial(local, mesh.shape["dp"], mesh.shape["rows"])
    return jax.shard_map(run, mesh=mesh, in_specs=in_specs, out_specs=out_specs, check_vma=False)
```

time: 756 us -> 211 us (0.28)
  waiting for transfers between devices: 442 us -> 32.1 us
  other arithmetic: 123 us -> 48.3 us
  blocking collectives: 63.3 us -> 0 us
  matrix products: 74.7 us -> 21.4 us
  starting transfers between devices: 0.85 us -> 32.1 us
  Pallas kernels: 0 us -> 24.2 us
  between operations: 15.6 us -> 1.77 us
  local copies, waits for them, and re-layouts: 35.2 us -> 48.6 us
    reduce_scatter x8 -> x0, waiting for transfers between devices: 442 us -> none  [the longest x1 91.7 us: local(): lax.psum_scatter(totals[13], 'dp', scatter_dimension=0, tiled=True)]
    sub x2 -> x0, other arithmetic: 102 us -> none  [the longest x1 81.7 us: local(): grad_probs - jnp.sum(probs * grad_probs, axis=-1, keepdims=True)]
    dot_general x18 -> x8, matrix products: 61.6 us -> 13.3 us  [the longest x6 10 us: matmul(): return jnp.dot(left, right, preferred_element_type=f32)]
    unnamed x1 -> x0, blocking collectives: 35.9 us -> none
    ppermute x0 -> x34, waiting for transfers between devices: none -> 32.1 us  [swap(): return lax.ppermute(array, ('dp', 'rows'), pairs)]
    ppermute x0 -> x34, starting transfers between devices: none -> 32.1 us  [swap(): return lax.ppermute(array, ('dp', 'rows'), pairs)]
    pallas_call x0 -> x4, Pallas kernels: none -> 24.2 us  [the longest x1 11.6 us: attention_backward(): pl.pallas_call(backward_kernel, grid=(slots, heads // step), in_specs=[tu...]
    all_gather x2 -> x0, blocking collectives: 20.4 us -> none  [the longest x1 10.3 us: local(): lax.all_gather(local_keys, 'rows', axis=1, tiled=True)]
  transfers between devices with their start and end apart: 9 -> 34, of which waited for: 7 -> 11; matrix products, arithmetic and copies ran while one was open for 17% -> 39% of each run, Pallas kernels for 0% -> 7%
where the time goes in v1:
time: 211 us; the launch traced here: 209 us
  local copies, waits for them, and re-layouts  48.6 us (23%)
  other arithmetic  48.3 us (23%)
  starting transfers between devices  32.1 us (15%)
  waiting for transfers between devices  32.1 us (15%)
  Pallas kernels  24.2 us (11%)
  matrix products  21.4 us (10%)
    ppermute x34, waiting for transfers between devices, swap(): return lax.ppermute(array, ('dp', 'rows'), pairs)  32.1 us
    ppermute x34, starting transfers between devices, swap(): return lax.ppermute(array, ('dp', 'rows'), pairs)  32.1 us
    unnamed x129, local copies, waits for them, and re-layouts  13.5 us
    pallas_call x1, Pallas kernels, attention_backward(): pl.pallas_call(backward_kernel, grid=(slots, heads // step), in_specs=[tu...  11.6 us
    another operation x9, other arithmetic, local(): pair_of = lambda own, send: jnp.stack([own, swap(send, row_bit=0)])  11.3 us
    pallas_call x1, Pallas kernels, attention_forward(): pl.pallas_call(forward_kernel, grid=(slots, heads // step), in_specs=[nat...  10.3 us
    dot_general x6, matrix products, matmul(): return jnp.dot(left, right, preferred_element_type=f32)  10 us
    dot_general x4, matrix products, times_transposed(): lax.dot_general(left, right, (((1,), (1,)), ((), ())), preferred_element_...  8.08 us
  transfers between devices with their start and end apart: 34, of which 11 were waited for; matrix products, arithmetic and copies ran while one was open for 39% of the time, Pallas kernels for 7%

profile of v1, /device:TPU:0, one launch (start us, length us, event | category | flops | bytes accessed | tf_op | source)
XLA Modules:
  0.0 208.5 jit_solution(4411605024092872369)
XLA Ops:
  1.2 2.6 %collective-permute-start.1 = (bf16[3,64,512]{2,1,0:T(8,128)(2,1)}, bf16[3,64,512]{2,1,0:T(8,128)(2,1)}, u32[]{:S(2)}, u32[]{:S(2)}) collective-permute-start(bf16[3,64,512]{2,1,0:T(8,128)(2,1)} %param.22), channel_id=1, source_target_pairs={{0,2},{1,3},{2,0},{3,1},{4,6},{5,7},{6,4},{7,5},{8,10},{9,11},{10,... | collective-permute-start | bytes 589832 | tf_op jit(solution)/shard_map/ppermute | solution.py:266
  15.8 1.5 fusion.19
  18.9 1.5 dynamic-slice_bitcast_fusion.8
  21.0 1.5 dynamic-slice_bitcast_fusion.7
  25.0 1.9 pad_maximum_fusion.2
  26.9 1.7 gather_fusion.1
  29.1 1.3 convert_bitcast_fusion
  30.9 1.6 copy.218
  35.6 1.9 add_convert_fusion.2
  37.6 10.3 %attention_forward.1 = (bf16[3,64,64,256]{3,2,1,0:T(8,128)(2,1)}, bf16[3,64,64,256]{3,2,1,0:T(8,128)(2,1)}, f32[3,64,512]{2,1,0:T(8,128)S(1)}, f32[3,64,512]{2,1,0:T(8,128)S(1)}) custom-call(bf16[3,64,512]{2,1,0:T(8,128)(2,1)S(1)} %bitcast.364, bf16[3,512,256]{2,1,0:T(8,128)(2,1)S(1)} %copy-done.13, bf16[3,256,512]{2,1,0:T(8,128)(2,1)S(1)} %bitcast.359, ...), custom_call_target="tpu_custom_call" | custom-call | flops 3221225472 | bytes 18874368 | tf_op jit(solution)/shard_map/attention_forward/pallas_call | solution.py:81
  52.3 2.3 %copy.225 = bf16[3,256,512]{1,2,0:T(8,128)(2,1)} copy(bf16[3,256,512]{2,1,0:T(8,128)(2,1)} %bitcast.360) | data formatting | bytes 1572864 | tf_op jit(solution)/shard_map/reshape | solution.py:386
  54.8 2.3 %convolution_add_fusion = f32[192,2048]{1,0:T(8,128)S(1)} fusion(bf16[192,512]{1,0:T(8,128)(2,1)} %add_convert_fusion.4, bf16[512,2048]{1,0:T(8,128)(2,1)} %param.36, f32[2048]{0:T(1024)S(1)} %convert_element_type.427), kind=kOutput, calls=%fused_computation.3 | convolution fusion | flops 403046400 | bytes 3874816 | tf_op jit(solution)/shard_map/dot_general | solution.py:32
  57.1 5.7 %convert_reduce_fusion = (f32[2048]{0:T(1024)}, bf16[192,2048]{1,0:T(8,128)(2,1)S(1)}, f32[192,2048]{1,0:T(8,128)}) fusion(f32[192,2048]{1,0:T(8,128)S(1)} %convolution_add_fusion, bf16[192,512]{1,0:T(8,128)(2,1)S(1)} %bitcast.395, bf16[2048,512]{1,0:T(8,128)(2,1)S(1)} %copy-done), kind=kOutput, calls=%fused_computation.18 | convolution fusion | flops 431749120 | bytes 6234112 | tf_op jit(solution)/shard_map/dot_general | solution.py:36
  73.6 11.6 %attention_backward.1 = (bf16[3,64,64,256]{3,2,1,0:T(8,128)(2,1)}, bf16[3,64,512]{2,1,0:T(8,128)(2,1)S(1)}, bf16[3,512,256]{2,1,0:T(8,128)(2,1)S(1)}, bf16[3,512,256]{2,1,0:T(8,128)(2,1)S(1)}) custom-call(bf16[3,512,64]{2,1,0:T(8,128)(2,1)S(1)} %bitcast.365, bf16[3,64,512]{2,1,0:T(8,128)(2,1)S(1)} %bitcast.362, bf16[3,512,64]{2,1,0:T(8,128)(2,1)S(1)} %bitcast.366, ...), custom_call_target="tpu_custom_call" | custom-call | flops 4831838208 | bytes 18874368 | tf_op jit(solution)/shard_map/attention_backward/pallas_call | solution.py:155
  86.4 1.8 fusion.29
  89.6 3.1 %multiply_convert_fusion = bf16[192,2048]{1,0:T(8,128)(2,1)} fusion(f32[192,2048]{1,0:T(8,128)} %get-tuple-element.143, f32[192,2048]{1,0:T(8,128)} %copy-done.31), kind=kLoop, calls=%fused_computation.22 | loop fusion | flops 1179648 | bytes 3932160 | tf_op jit(solution)/shard_map/convert_element_type | solution.py:399
  92.9 1.5 add_convert_fusion
  94.4 2.6 %gather_fusion.2 = bf16[4,3,64,512]{3,2,1,0:T(8,128)(2,1)} fusion(bf16[4,3,64,512]{3,2,0,1:T(8,128)(2,1)} %bitcast.377, s32[1024]{0:T(1024)S(1)} %pad_clamp_fusion.1), kind=kCustom, calls=%fused_computation.1.clone | custom fusion | bytes 1572880 | tf_op jit(solution)/shard_map/jit(_take)/gather | solution.py:439
  103.7 1.6 pad_maximum_fusion.12.branch_ref
  106.5 1.8 pad_maximum_fusion.8.inner_ref
  108.7 1.7 pad_maximum_fusion.9.mixed_ref
  112.8 5.8 %collective-permute-done.4 = bf16[3,64,512]{2,1,0:T(8,128)(2,1)S(1)} collective-permute-done((bf16[3,64,512]{2,1,0:T(8,128)(2,1)S(1)}, bf16[3,64,512]{2,1,0:T(8,128)(2,1)S(1)}, u32[]{:S(2)}, u32[]{:S(2)}) %collective-permute-start.4) | collective-permute-done | bytes 196640 | tf_op jit(solution)/shard_map/ppermute | solution.py:266
  120.1 2.1 pad_maximum_fusion.4.dkt_ref
  128.7 1.5 collective-permute-start.24
  130.9 1.6 pad_maximum_fusion.act_ref
  132.6 1.5 ffn_grads.1
  137.4 1.7 collective-permute-start.15
  139.9 1.7 reshape.720
  141.6 1.4 fusion.70
  143.0 1.5 collective-permute-start.29
  145.7 1.6 collective-permute-start.25
  147.3 5.3 %collective-permute-done.29 = bf16[4,52,256]{2,1,0:T(8,128)(2,1)S(1)} collective-permute-done((bf16[4,52,256]{2,1,0:T(8,128)(2,1)S(1)}, bf16[4,52,256]{2,1,0:T(8,128)(2,1)S(1)}, u32[]{:S(2)}, u32[]{:S(2)}) %collective-permute-start.29) | collective-permute-done | bytes 106528 | tf_op jit(solution)/shard_map/ppermute | solution.py:266
  152.6 1.7 collective-permute-start.30
  154.3 2.6 %collective-permute-start.26 = (bf16[1,104,256]{2,1,0:T(8,128)(2,1)S(1)}, bf16[1,104,256]{2,1,0:T(8,128)(2,1)S(1)}, u32[]{:S(2)}, u32[]{:S(2)}) collective-permute-start(bf16[1,104,256]{2,1,0:T(8,128)(2,1)S(1)} %slice_bitcast_fusion.22), channel_id=1, source_target_pairs={{0,16},{1,17},{2,18},{3,19},{4,20},{5,21},{6,22},{7,23},{8,24},{9,... | collective-permute-start | bytes 159752 | tf_op jit(solution)/shard_map/ppermute | solution.py:266
  157.0 2.5 %collective-permute-start.31 = (bf16[1,52,256]{2,1,0:T(8,128)(2,1)S(1)}, bf16[1,52,256]{2,1,0:T(8,128)(2,1)S(1)}, u32[]{:S(2)}, u32[]{:S(2)}) collective-permute-start(bf16[1,52,256]{2,1,0:T(8,128)(2,1)S(1)} %slice_bitcast_fusion.24), channel_id=1, source_target_pairs={{0,16},{1,17},{2,18},{3,19},{4,20},{5,21},{6,22},{7,23},{8,24},{9,... | collective-permute-start | bytes 79880 | tf_op jit(solution)/shard_map/ppermute | solution.py:266
  160.6 1.6 collective-permute-start.27
  163.5 1.4 collective-permute-done.27
  164.9 1.3 collective-permute-done.32
  170.5 3.4 %collective-permute-done.12 = bf16[2,256,256]{2,1,0:T(8,128)(2,1)S(1)} collective-permute-done((bf16[2,256,256]{2,1,0:T(8,128)(2,1)S(1)}, bf16[2,256,256]{2,1,0:T(8,128)(2,1)S(1)}, u32[]{:S(2)}, u32[]{:S(2)}) %collective-permute-start.12) | collective-permute-done | bytes 262176 | tf_op jit(solution)/shard_map/ppermute | solution.py:266
  173.9 3.1 %collective-permute-done.16 = bf16[4,160,256]{2,1,0:T(8,128)(2,1)S(1)} collective-permute-done((bf16[4,160,256]{2,1,0:T(8,128)(2,1)S(1)}, bf16[4,160,256]{2,1,0:T(8,128)(2,1)S(1)}, u32[]{:S(2)}, u32[]{:S(2)}) %collective-permute-start.16) | collective-permute-done | bytes 327712 | tf_op jit(solution)/shard_map/ppermute | solution.py:266
  178.1 2.2 %collective-permute-start.13 = (bf16[1,256,256]{2,1,0:T(8,128)(2,1)S(1)}, bf16[1,256,256]{2,1,0:T(8,128)(2,1)S(1)}, u32[]{:S(2)}, u32[]{:S(2)}) collective-permute-start(bf16[1,256,256]{2,1,0:T(8,128)(2,1)S(1)} %slice_bitcast_fusion.14), channel_id=1, source_target_pairs={{0,16},{1,17},{2,18},{3,19},{4,20},{5,21},{6,22},{7,23},{8,24},{9,... | collective-permute-start | bytes 393224 | tf_op jit(solution)/shard_map/ppermute | solution.py:266
  180.3 4.5 %collective-permute-done.17 = bf16[2,160,256]{2,1,0:T(8,128)(2,1)S(1)} collective-permute-done((bf16[2,160,256]{2,1,0:T(8,128)(2,1)S(1)}, bf16[2,160,256]{2,1,0:T(8,128)(2,1)S(1)}, u32[]{:S(2)}, u32[]{:S(2)}) %collective-permute-start.17) | collective-permute-done | bytes 163872 | tf_op jit(solution)/shard_map/ppermute | solution.py:266
  185.4 1.6 collective-permute-start.14
  187.0 3.2 %collective-permute-done.18 = bf16[1,160,256]{2,1,0:T(8,128)(2,1)S(1)} collective-permute-done((bf16[1,160,256]{2,1,0:T(8,128)(2,1)S(1)}, bf16[1,160,256]{2,1,0:T(8,128)(2,1)S(1)}, u32[]{:S(2)}, u32[]{:S(2)}) %collective-permute-start.18) | collective-permute-done | bytes 81952 | tf_op jit(solution)/shard_map/ppermute | solution.py:266
  190.3 1.6 collective-permute-start.19
  191.9 2.9 %collective-permute-done.19 = bf16[160,256]{1,0:T(8,128)(2,1)S(1)} collective-permute-done((bf16[160,256]{1,0:T(8,128)(2,1)S(1)}, bf16[160,256]{1,0:T(8,128)(2,1)S(1)}, u32[]{:S(2)}, u32[]{:S(2)}) %collective-permute-start.19) | collective-permute-done | bytes 81952 | tf_op jit(solution)/shard_map/ppermute | solution.py:266
  195.0 2.5 %fusion.18 = bf16[192,512]{1,0:T(8,128)(2,1)} fusion(f32[192,512]{1,0:T(8,128)S(1)} %copy-done.24, bf16[192,2048]{1,0:T(8,128)(2,1)} %multiply_convert_fusion, bf16[2048,512]{1,0:T(8,128)(2,1)S(1)} %copy-done, f32[512]{0:T(512)S(1)} %convert_element_type.429), kind=kOutput, calls=%fused_computation.48 | convolution fusion | flops 402948096 | bytes 3475456 | tf_op jit(solution)/shard_map/dot_general | solution.py:32
  204.3 1.6 copy.271
  (325 shorter events, 81.6 us)
Async XLA Ops:
  0.7 56.4 %copy-start = (bf16[2048,512]{1,0:T(8,128)(2,1)S(1)}, bf16[2048,512]{1,0:T(8,128)(2,1)}, u32[]{:S(2)}) copy-start(bf16[2048,512]{1,0:T(8,128)(2,1)} %param.38) | copy-start | bytes 6291460
  0.7 15.0 %copy-start.27 = (bf16[3,64,512]{2,1,0:T(8,128)(2,1)S(1)}, bf16[3,64,512]{2,1,0:T(8,128)(2,1)}, u32[]{:S(2)}) copy-start(bf16[3,64,512]{2,1,0:T(8,128)(2,1)} %param.22) | copy-start | bytes 589828
  0.7 21.8 %collective-permute-start = (bf16[3,64,512]{2,1,0:T(8,128)(2,1)}, bf16[3,64,512]{2,1,0:T(8,128)(2,1)S(1)}, u32[]{:S(2)}, u32[]{:S(2)}) collective-permute-start(bf16[3,64,512]{2,1,0:T(8,128)(2,1)} %param.22), channel_id=1, source_target_pairs={{0,1},{1,0},{2,3},{3,2},{4,5},{5,4},{6,7},{7,6},{8,9},{9,8},{10,11... | collective-permute-start | bytes 589832 | tf_op jit(solution)/shard_map/ppermute | solution.py:266
  1.2 22.1 %collective-permute-start.1 = (bf16[3,64,512]{2,1,0:T(8,128)(2,1)}, bf16[3,64,512]{2,1,0:T(8,128)(2,1)}, u32[]{:S(2)}, u32[]{:S(2)}) collective-permute-start(bf16[3,64,512]{2,1,0:T(8,128)(2,1)} %param.22), channel_id=1, source_target_pairs={{0,2},{1,3},{2,0},{3,1},{4,6},{5,7},{6,4},{7,5},{8,10},{9,11},{10,... | collective-permute-start | bytes 589832 | tf_op jit(solution)/shard_map/ppermute | solution.py:266
  3.8 17.2 %collective-permute-start.6 = (bf16[3,64,512]{2,1,0:T(8,128)(2,1)}, bf16[3,64,512]{2,1,0:T(8,128)(2,1)}, u32[]{:S(2)}, u32[]{:S(2)}) collective-permute-start(bf16[3,64,512]{2,1,0:T(8,128)(2,1)} %param.40), channel_id=1, source_target_pairs={{0,1},{1,0},{2,3},{3,2},{4,5},{5,4},{6,7},{7,6},{8,9},{9,8},{10,11... | collective-permute-start | bytes 589832 | tf_op jit(solution)/shard_map/ppermute | solution.py:266
  7.2 15.9 %copy-start.36 = (f32[3,64,512]{2,1,0:T(8,128)}, f32[3,64,512]{2,1,0:T(8,128)S(1)}, u32[]{:S(2)}) copy-start(f32[3,64,512]{2,1,0:T(8,128)S(1)} %convert_element_type.407) | copy-start | bytes 1179652
  7.2 11.7 %copy-start.61 = (bf16[512]{0:T(512)(128)(2,1)S(1)}, bf16[512]{0:T(512)(128)(2,1)}, u32[]{:S(2)}) copy-start(bf16[512]{0:T(512)(128)(2,1)} %param.39) | copy-start | bytes 3076
  15.8 7.3 %copy-start.34 = (f32[192,512]{1,0:T(8,128)}, f32[192,512]{1,0:T(8,128)S(1)}, u32[]{:S(2)}) copy-start(f32[192,512]{1,0:T(8,128)S(1)} %fusion.42) | copy-start | bytes 1179652
  23.3 1.7 collective-permute-start.2
  37.6 10.4 %copy-start.12 = (bf16[768,512]{1,0:T(8,128)(2,1)}, bf16[768,512]{1,0:T(8,128)(2,1)S(1)}, u32[]{:S(2)}) copy-start(bf16[768,512]{1,0:T(8,128)(2,1)S(1)} %add_convert_fusion.2) | copy-start | bytes 2359300
  37.6 11.2 %copy-start.37 = (f32[3,64,512]{2,1,0:T(8,128)S(1)}, f32[3,64,512]{2,1,0:T(8,128)}, u32[]{:S(2)}) copy-start(f32[3,64,512]{2,1,0:T(8,128)} %copy-done.36) | copy-start | bytes 1179652
  37.6 11.2 %copy-start.41 = (bf16[512,512]{1,0:T(8,128)(2,1)S(1)}, bf16[512,512]{1,0:T(8,128)(2,1)}, u32[]{:S(2)}) copy-start(bf16[512,512]{1,0:T(8,128)(2,1)} %param.32) | copy-start | bytes 1572868
  52.0 56.3 %collective-permute-start.9 = (bf16[192,512]{1,0:T(8,128)(2,1)}, bf16[192,512]{1,0:T(8,128)(2,1)}, u32[]{:S(2)}, u32[]{:S(2)}) collective-permute-start(bf16[192,512]{1,0:T(8,128)(2,1)} %get-tuple-element.168), channel_id=1, source_target_pairs={{0,1},{1,0},{2,3},{3,2},{4,5},{5,4},{6,7},{7,6},{8,9},{9,8},{10,11... | collective-permute-start | bytes 589832 | tf_op jit(solution)/shard_map/ppermute | solution.py:266
  54.6 51.7 %collective-permute-start.7 = (bf16[192,512]{1,0:T(8,128)(2,1)}, bf16[192,512]{1,0:T(8,128)(2,1)}, u32[]{:S(2)}, u32[]{:S(2)}) collective-permute-start(bf16[192,512]{1,0:T(8,128)(2,1)} %add_convert_fusion.4), channel_id=1, source_target_pairs={{0,1},{1,0},{2,3},{3,2},{4,5},{5,4},{6,7},{7,6},{8,9},{9,8},{10,11... | collective-permute-start | bytes 589832 | tf_op jit(solution)/shard_map/ppermute | solution.py:266
  57.1 5.8 %copy-start.31 = (f32[192,2048]{1,0:T(8,128)}, f32[192,2048]{1,0:T(8,128)S(1)}, u32[]{:S(2)}) copy-start(f32[192,2048]{1,0:T(8,128)S(1)} %convolution_add_fusion) | copy-start | bytes 4718596
  57.1 5.7 %copy-start.23 = (f32[192,512]{1,0:T(8,128)S(1)}, f32[192,512]{1,0:T(8,128)}, u32[]{:S(2)}) copy-start(f32[192,512]{1,0:T(8,128)} %copy-done.22) | copy-start | bytes 1179652
  89.3 14.2 %collective-permute-start.10 = (bf16[192,256]{1,0:T(8,128)(2,1)}, bf16[192,256]{1,0:T(8,128)(2,1)}, u32[]{:S(2)}, u32[]{:S(2)}) collective-permute-start(bf16[192,256]{1,0:T(8,128)(2,1)} %get-tuple-element.174), channel_id=1, source_target_pairs={{0,1},{1,0},{2,3},{3,2},{4,5},{5,4},{6,7},{7,6},{8,9},{9,8},{10,11... | collective-permute-start | bytes 294920 | tf_op jit(solution)/shard_map/ppermute | solution.py:266
  92.8 38.1 %collective-permute-start.5 = (bf16[192,2048]{1,0:T(8,128)(2,1)}, bf16[192,2048]{1,0:T(8,128)(2,1)}, u32[]{:S(2)}, u32[]{:S(2)}) collective-permute-start(bf16[192,2048]{1,0:T(8,128)(2,1)} %multiply_convert_fusion), channel_id=1, source_target_pairs={{0,1},{1,0},{2,3},{3,2},{4,5},{5,4},{6,7},{7,6},{8,9},{9,8},{10,11... | collective-permute-start | bytes 2359304 | tf_op jit(solution)/shard_map/ppermute | solution.py:266
  99.1 11.2 %collective-permute-start.3 = (bf16[2,3,64,512]{3,2,1,0:T(8,128)(2,1)}, bf16[2,3,64,512]{3,2,1,0:T(8,128)(2,1)}, u32[]{:S(2)}, u32[]{:S(2)}) collective-permute-start(bf16[2,3,64,512]{3,2,1,0:T(8,128)(2,1)} %slice_bitcast_fusion.2), channel_id=1, source_target_pairs={{0,1},{1,0},{2,3},{3,2},{4,5},{5,4},{6,7},{7,6},{8,9},{9,8},{10,11... | collective-permute-start | bytes 1179656 | tf_op jit(solution)/shard_map/ppermute | solution.py:266
  103.5 1.8 collective-permute-start.20
  105.3 6.4 %collective-permute-start.8 = (bf16[192,1024]{1,0:T(8,128)(2,1)S(1)}, bf16[192,1024]{1,0:T(8,128)(2,1)S(1)}, u32[]{:S(2)}, u32[]{:S(2)}) collective-permute-start(bf16[192,1024]{1,0:T(8,128)(2,1)S(1)} %get-tuple-element.160), channel_id=1, source_target_pairs={{0,1},{1,0},{2,3},{3,2},{4,5},{5,4},{6,7},{7,6},{8,9},{9,8},{10,11... | collective-permute-start | bytes 1179656 | tf_op jit(solution)/shard_map/ppermute | solution.py:266
  106.4 5.4 %collective-permute-start.22 = (bf16[3,256,256]{2,1,0:T(8,128)(2,1)S(1)}, bf16[3,256,256]{2,1,0:T(8,128)(2,1)S(1)}, u32[]{:S(2)}, u32[]{:S(2)}) collective-permute-start(bf16[3,256,256]{2,1,0:T(8,128)(2,1)S(1)} %copy-done.57), channel_id=1, source_target_pairs={{0,1},{1,0},{2,3},{3,2},{4,5},{5,4},{6,7},{7,6},{8,9},{9,8},{10,11... | collective-permute-start | bytes 1179656 | tf_op jit(solution)/shard_map/ppermute | solution.py:266
  108.3 11.8 %collective-permute-start.21 = (bf16[3,256,256]{2,1,0:T(8,128)(2,1)}, bf16[3,256,256]{2,1,0:T(8,128)(2,1)}, u32[]{:S(2)}, u32[]{:S(2)}) collective-permute-start(bf16[3,256,256]{2,1,0:T(8,128)(2,1)} %get-tuple-element.164), channel_id=1, source_target_pairs={{0,1},{1,0},{2,3},{3,2},{4,5},{5,4},{6,7},{7,6},{8,9},{9,8},{10,11... | collective-permute-start | bytes 1179656 | tf_op jit(solution)/shard_map/ppermute | solution.py:266
  111.5 7.0 %collective-permute-start.4 = (bf16[3,64,512]{2,1,0:T(8,128)(2,1)S(1)}, bf16[3,64,512]{2,1,0:T(8,128)(2,1)S(1)}, u32[]{:S(2)}, u32[]{:S(2)}) collective-permute-start(bf16[3,64,512]{2,1,0:T(8,128)(2,1)S(1)} %slice_bitcast_fusion.10), channel_id=1, source_target_pairs={{0,2},{1,3},{2,0},{3,1},{4,6},{5,7},{6,4},{7,5},{8,10},{9,11},{10,... | collective-permute-start | bytes 589832 | tf_op jit(solution)/shard_map/ppermute | solution.py:266
  111.8 6.8 %copy-start.40 = (bf16[512,512]{1,0:T(8,128)(2,1)S(1)}, bf16[512,512]{1,0:T(8,128)(2,1)}, u32[]{:S(2)}) copy-start(bf16[512,512]{1,0:T(8,128)(2,1)} %param.27) | copy-start | bytes 1572868
  111.8 7.1 %copy-start.28 = (bf16[3,64,512]{2,1,0:T(8,128)(2,1)S(1)}, bf16[3,64,512]{2,1,0:T(8,128)(2,1)}, u32[]{:S(2)}) copy-start(bf16[3,64,512]{2,1,0:T(8,128)(2,1)} %param.22) | copy-start | bytes 589828
  111.8 7.1 %copy-start.35 = (f32[192,512]{1,0:T(8,128)S(1)}, f32[192,512]{1,0:T(8,128)}, u32[]{:S(2)}) copy-start(f32[192,512]{1,0:T(8,128)} %copy-done.34) | copy-start | bytes 1179652
  120.1 2.1 %collective-permute-start.23 = (f32[8,768]{1,0:T(8,128)S(1)}, f32[8,768]{1,0:T(8,128)S(1)}, u32[]{:S(2)}, u32[]{:S(2)}) collective-permute-start(f32[8,768]{1,0:T(8,128)S(1)} %concatenate.13), channel_id=1, source_target_pairs={{0,1},{1,0},{2,3},{3,2},{4,5},{5,4},{6,7},{7,6},{8,9},{9,8},{10,11... | collective-permute-start | bytes 73736 | tf_op jit(solution)/shard_map/ppermute | solution.py:266
  128.7 15.9 %collective-permute-start.24 = (bf16[4,104,256]{2,1,0:T(8,128)(2,1)}, bf16[4,104,256]{2,1,0:T(8,128)(2,1)}, u32[]{:S(2)}, u32[]{:S(2)}) collective-permute-start(bf16[4,104,256]{2,1,0:T(8,128)(2,1)} %slice_bitcast_fusion.8), channel_id=1, source_target_pairs={{0,4},{1,5},{2,6},{3,7},{4,0},{5,1},{6,2},{7,3},{8,12},{9,13},{10,... | collective-permute-start | bytes 638984 | tf_op jit(solution)/shard_map/ppermute | solution.py:266
  130.3 8.8 %collective-permute-start.28 = (bf16[8,52,256]{2,0,1:T(8,128)(2,1)S(1)}, bf16[8,52,256]{2,0,1:T(8,128)(2,1)S(1)}, u32[]{:S(2)}, u32[]{:S(2)}) collective-permute-start(bf16[8,52,256]{2,0,1:T(8,128)(2,1)S(1)} %dynamic-slice_bitcast_fusion.4), channel_id=1, source_target_pairs={{0,2},{1,3},{2,0},{3,1},{4,6},{5,7},{6,4},{7,5},{8,10},{9,11},{10,... | collective-permute-start | bytes 638984 | tf_op jit(solution)/shard_map/ppermute | solution.py:266
  136.1 30.1 %collective-permute-start.11 = (bf16[4,256,256]{2,1,0:T(8,128)(2,1)}, bf16[4,256,256]{2,1,0:T(8,128)(2,1)}, u32[]{:S(2)}, u32[]{:S(2)}) collective-permute-start(bf16[4,256,256]{2,1,0:T(8,128)(2,1)} %slice_bitcast_fusion), channel_id=1, source_target_pairs={{0,4},{1,5},{2,6},{3,7},{4,0},{5,1},{6,2},{7,3},{8,12},{9,13},{10,... | collective-permute-start | bytes 1572872 | tf_op jit(solution)/shard_map/ppermute | solution.py:266
  137.4 31.2 %collective-permute-start.15 = (bf16[8,160,256]{2,1,0:T(8,128)(2,1)}, bf16[8,160,256]{2,1,0:T(8,128)(2,1)}, u32[]{:S(2)}, u32[]{:S(2)}) collective-permute-start(bf16[8,160,256]{2,1,0:T(8,128)(2,1)} %dynamic-slice_bitcast_fusion), channel_id=1, source_target_pairs={{0,2},{1,3},{2,0},{3,1},{4,6},{5,7},{6,4},{7,5},{8,10},{9,11},{10,... | collective-permute-start | bytes 1966088 | tf_op jit(solution)/shard_map/ppermute | solution.py:266
  143.0 23.2 %copy-start.33 = (bf16[8,256,256]{2,1,0:T(8,128)(2,1)S(1)}, bf16[8,256,256]{2,1,0:T(8,128)(2,1)}, u32[]{:S(2)}) copy-start(bf16[8,256,256]{2,1,0:T(8,128)(2,1)} %copy-done.32) | copy-start | bytes 3145732
  143.0 9.5 %collective-permute-start.29 = (bf16[4,52,256]{2,1,0:T(8,128)(2,1)S(1)}, bf16[4,52,256]{2,1,0:T(8,128)(2,1)S(1)}, u32[]{:S(2)}, u32[]{:S(2)}) collective-permute-start(bf16[4,52,256]{2,1,0:T(8,128)(2,1)S(1)} %bitcast.411), channel_id=1, source_target_pairs={{0,4},{1,5},{2,6},{3,7},{4,0},{5,1},{6,2},{7,3},{8,12},{9,13},{10,... | collective-permute-start | bytes 319496 | tf_op jit(solution)/shard_map/ppermute | solution.py:266
  145.7 8.6 %collective-permute-start.25 = (bf16[2,104,256]{2,1,0:T(8,128)(2,1)S(1)}, bf16[2,104,256]{2,1,0:T(8,128)(2,1)S(1)}, u32[]{:S(2)}, u32[]{:S(2)}) collective-permute-start(bf16[2,104,256]{2,1,0:T(8,128)(2,1)S(1)} %slice_bitcast_fusion.16), channel_id=1, source_target_pairs={{0,8},{1,9},{2,10},{3,11},{4,12},{5,13},{6,14},{7,15},{8,0},{9,1},... | collective-permute-start | bytes 319496 | tf_op jit(solution)/shard_map/ppermute | solution.py:266
  152.6 4.4 %collective-permute-start.30 = (bf16[2,52,256]{2,1,0:T(8,128)(2,1)S(1)}, bf16[2,52,256]{2,1,0:T(8,128)(2,1)S(1)}, u32[]{:S(2)}, u32[]{:S(2)}) collective-permute-start(bf16[2,52,256]{2,1,0:T(8,128)(2,1)S(1)} %slice_bitcast_fusion.20), channel_id=1, source_target_pairs={{0,8},{1,9},{2,10},{3,11},{4,12},{5,13},{6,14},{7,15},{8,0},{9,1},... | collective-permute-start | bytes 159752 | tf_op jit(solution)/shard_map/ppermute | solution.py:266
  154.3 6.3 %collective-permute-start.26 = (bf16[1,104,256]{2,1,0:T(8,128)(2,1)S(1)}, bf16[1,104,256]{2,1,0:T(8,128)(2,1)S(1)}, u32[]{:S(2)}, u32[]{:S(2)}) collective-permute-start(bf16[1,104,256]{2,1,0:T(8,128)(2,1)S(1)} %slice_bitcast_fusion.22), channel_id=1, source_target_pairs={{0,16},{1,17},{2,18},{3,19},{4,20},{5,21},{6,22},{7,23},{8,24},{9,... | collective-permute-start | bytes 159752 | tf_op jit(solution)/shard_map/ppermute | solution.py:266
  157.0 5.2 %collective-permute-start.31 = (bf16[1,52,256]{2,1,0:T(8,128)(2,1)S(1)}, bf16[1,52,256]{2,1,0:T(8,128)(2,1)S(1)}, u32[]{:S(2)}, u32[]{:S(2)}) collective-permute-start(bf16[1,52,256]{2,1,0:T(8,128)(2,1)S(1)} %slice_bitcast_fusion.24), channel_id=1, source_target_pairs={{0,16},{1,17},{2,18},{3,19},{4,20},{5,21},{6,22},{7,23},{8,24},{9,... | collective-permute-start | bytes 79880 | tf_op jit(solution)/shard_map/ppermute | solution.py:266
  160.6 4.2 %collective-permute-start.27 = (bf16[104,256]{1,0:T(8,128)(2,1)S(1)}, bf16[104,256]{1,0:T(8,128)(2,1)S(1)}, u32[]{:S(2)}, u32[]{:S(2)}) collective-permute-start(bf16[104,256]{1,0:T(8,128)(2,1)S(1)} %fusion.59), channel_id=1, source_target_pairs={{0,2},{1,3},{2,0},{3,1},{4,6},{5,7},{6,4},{7,5},{8,10},{9,11},{10,... | collective-permute-start | bytes 159752 | tf_op jit(solution)/shard_map/ppermute | solution.py:266
  162.2 3.9 %collective-permute-start.32 = (bf16[52,256]{1,0:T(8,128)(2,1)S(1)}, bf16[52,256]{1,0:T(8,128)(2,1)S(1)}, u32[]{:S(2)}, u32[]{:S(2)}) collective-permute-start(bf16[52,256]{1,0:T(8,128)(2,1)S(1)} %fusion.62), channel_id=1, source_target_pairs={{0,2},{1,3},{2,0},{3,1},{4,6},{5,7},{6,4},{7,5},{8,10},{9,11},{10,... | collective-permute-start | bytes 79880 | tf_op jit(solution)/shard_map/ppermute | solution.py:266
  167.4 6.4 %collective-permute-start.12 = (bf16[2,256,256]{2,1,0:T(8,128)(2,1)S(1)}, bf16[2,256,256]{2,1,0:T(8,128)(2,1)S(1)}, u32[]{:S(2)}, u32[]{:S(2)}) collective-permute-start(bf16[2,256,256]{2,1,0:T(8,128)(2,1)S(1)} %slice_bitcast_fusion.6), channel_id=1, source_target_pairs={{0,8},{1,9},{2,10},{3,11},{4,12},{5,13},{6,14},{7,15},{8,0},{9,1},... | collective-permute-start | bytes 786440 | tf_op jit(solution)/shard_map/ppermute | solution.py:266
  169.9 7.1 %collective-permute-start.16 = (bf16[4,160,256]{2,1,0:T(8,128)(2,1)S(1)}, bf16[4,160,256]{2,1,0:T(8,128)(2,1)S(1)}, u32[]{:S(2)}, u32[]{:S(2)}) collective-permute-start(bf16[4,160,256]{2,1,0:T(8,128)(2,1)S(1)} %slice_bitcast_fusion.4), channel_id=1, source_target_pairs={{0,4},{1,5},{2,6},{3,7},{4,0},{5,1},{6,2},{7,3},{8,12},{9,13},{10,... | collective-permute-start | bytes 983048 | tf_op jit(solution)/shard_map/ppermute | solution.py:266
  177.1 7.7 %collective-permute-start.17 = (bf16[2,160,256]{2,1,0:T(8,128)(2,1)S(1)}, bf16[2,160,256]{2,1,0:T(8,128)(2,1)S(1)}, u32[]{:S(2)}, u32[]{:S(2)}) collective-permute-start(bf16[2,160,256]{2,1,0:T(8,128)(2,1)S(1)} %slice_bitcast_fusion.12), channel_id=1, source_target_pairs={{0,8},{1,9},{2,10},{3,11},{4,12},{5,13},{6,14},{7,15},{8,0},{9,1},... | collective-permute-start | bytes 491528 | tf_op jit(solution)/shard_map/ppermute | solution.py:266
  178.1 7.3 %collective-permute-start.13 = (bf16[1,256,256]{2,1,0:T(8,128)(2,1)S(1)}, bf16[1,256,256]{2,1,0:T(8,128)(2,1)S(1)}, u32[]{:S(2)}, u32[]{:S(2)}) collective-permute-start(bf16[1,256,256]{2,1,0:T(8,128)(2,1)S(1)} %slice_bitcast_fusion.14), channel_id=1, source_target_pairs={{0,16},{1,17},{2,18},{3,19},{4,20},{5,21},{6,22},{7,23},{8,24},{9,... | collective-permute-start | bytes 393224 | tf_op jit(solution)/shard_map/ppermute | solution.py:266
  184.8 5.4 %collective-permute-start.18 = (bf16[1,160,256]{2,1,0:T(8,128)(2,1)S(1)}, bf16[1,160,256]{2,1,0:T(8,128)(2,1)S(1)}, u32[]{:S(2)}, u32[]{:S(2)}) collective-permute-start(bf16[1,160,256]{2,1,0:T(8,128)(2,1)S(1)} %slice_bitcast_fusion.18), channel_id=1, source_target_pairs={{0,16},{1,17},{2,18},{3,19},{4,20},{5,21},{6,22},{7,23},{8,24},{9,... | collective-permute-start | bytes 245768 | tf_op jit(solution)/shard_map/ppermute | solution.py:266
  185.4 6.4 %collective-permute-start.14 = (bf16[256,256]{1,0:T(8,128)(2,1)S(1)}, bf16[256,256]{1,0:T(8,128)(2,1)S(1)}, u32[]{:S(2)}, u32[]{:S(2)}) collective-permute-start(bf16[256,256]{1,0:T(8,128)(2,1)S(1)} %fusion.50), channel_id=1, source_target_pairs={{0,2},{1,3},{2,0},{3,1},{4,6},{5,7},{6,4},{7,5},{8,10},{9,11},{10,... | collective-permute-start | bytes 393224 | tf_op jit(solution)/shard_map/ppermute | solution.py:266
  190.3 4.5 %collective-permute-start.19 = (bf16[160,256]{1,0:T(8,128)(2,1)S(1)}, bf16[160,256]{1,0:T(8,128)(2,1)S(1)}, u32[]{:S(2)}, u32[]{:S(2)}) collective-permute-start(bf16[160,256]{1,0:T(8,128)(2,1)S(1)} %fusion.54), channel_id=1, source_target_pairs={{0,2},{1,3},{2,0},{3,1},{4,6},{5,7},{6,4},{7,5},{8,10},{9,11},{10,... | collective-permute-start | bytes 245768 | tf_op jit(solution)/shard_map/ppermute | solution.py:266
  195.0 3.5 %collective-permute-start.33 = (f32[784,256]{1,0:T(8,128)S(1)}, f32[784,256]{1,0:T(8,128)S(1)}, u32[]{:S(2)}, u32[]{:S(2)}) collective-permute-start(f32[784,256]{1,0:T(8,128)S(1)} %pad_maximum_fusion.1), channel_id=1, source_target_pairs={{0,1},{1,0},{2,3},{3,2},{4,5},{5,4},{6,7},{7,6},{8,9},{9,8},{10,11... | collective-permute-start | bytes 2408456 | tf_op jit(solution)/shard_map/ppermute | solution.py:266
  (48 other events, 101.4 us)

commit v2 on v1

--- a/solution.py
+++ b/solution.py
@@ -180,43 +180,232 @@
     )(qt, dm, dmt, nm, k, vt, e, cot)
 
 
-def ffn_grad_kernel(me_ref, act_ref, dy_ref, inner_ref, dpre_ref, mixed_ref, branch_ref, out_ref):
-    parts = out_ref.shape[0]
-    me = me_ref[0]
-    tall = act_ref.shape[2] // parts
-    short = inner_ref.shape[2] // parts
-    half = dy_ref.shape[2]
-    blocks = dpre_ref.shape[2] // half
-    both = lambda left, right: sum(outer_sum(left[i], right[i]) for i in range(2))
-    inner = [inner_ref[i] for i in range(2)]
-    for cb in range(blocks):
-        grad = both(inner, [dpre_ref[i, :, half * cb : half * (cb + 1)] for i in range(2)]).astype(bf16)
-        for j in range(parts):
-            out_ref[me ^ j, pl.ds(tall + short * cb, short), :] = grad[short * j : short * (j + 1)]
-    grad = both([mixed_ref[i] for i in range(2)], [branch_ref[i] for i in range(2)]).astype(bf16)
-    for j in range(parts):
-        out_ref[me ^ j, pl.ds(tall + short * blocks, short), :] = grad[short * j : short * (j + 1)]
-    dy = [dy_ref[i] for i in range(2)]
-    wide = max(tall, 256)
-    for n in range(act_ref.shape[2] // wide):
-        grad = both([act_ref[i, :, wide * n : wide * (n + 1)] for i in range(2)], dy).astype(bf16)
-        for j in range(wide // tall):
-            out_ref[me ^ (n * (wide // tall) + j), pl.ds(0, tall), :] = grad[tall * j : tall * (j + 1)]
-
-
-def ffn_grads(me, parts, act, dy, inner, dpre, mixed, branch):
-    half = dy.shape[2]
-    rows = (act.shape[2] * 2 + mixed.shape[2]) // parts
+def other_bit(index, bit, const):
+    own = (index // (1 << bit)) % 2
+    return 1 - own if (const >> bit) & 1 else own
+
+
+def xor(index, const, bits):
+    return sum(other_bit(index, b, const) * (1 << b) for b in range(bits))
+
+
+def middle_kernel(
+    parts,
+    mix_ref,
+    rl_ref,
+    atoms_ref,
+    dy_ref,
+    small_ref,
+    bias_ref,
+    out_w,
+    inner_w,
+    outer_w,
+    out_ref,
+    a_keep,
+    a_send,
+    b_keep,
+    b_send,
+    c_keep,
+    c_send,
+    dm_ref,
+    nm_ref,
+    dmt_ref,
+    dmid_ref,
+    vec_ref,
+    ow,
+    iw,
+    uw,
+    act,
+    dpre,
+    dpre_in,
+    inner,
+    mixed,
+    branch,
+    branch_in,
+    dyh,
+    dy_in,
+    grads,
+    load_sem,
+    send_sem,
+    recv_sem,
+):
+    here, width = atoms_ref.shape
+    half = width // 2
+    blocks = act.shape[1]
+    slots, _, rows = dmt_ref.shape
+    bits = parts.bit_length() - 1
+    row = lax.axis_index("rows")
+    dp = lax.axis_index("dp")
+    core = row % 2
+    y = row // 2
+    sibling = (dp, row + 1 - 2 * core)
+
+    loads = [
+        pltpu.make_async_copy(hbm, vmem, load_sem.at[i])
+        for i, (hbm, vmem) in enumerate(((out_w, ow), (inner_w, iw), (outer_w, uw)))
+    ]
+    for copy in loads:
+        copy.start()
+    barrier = pltpu.get_barrier_semaphore()
+    pl.semaphore_signal(barrier, inc=1, device_id=sibling, device_id_type=pl.DeviceIdType.MESH)
+    pl.semaphore_wait(barrier, 1)
+    sent = []
+
+    def send(source, target):
+        n = len(sent)
+        copy = pltpu.make_async_remote_copy(
+            src_ref=source,
+            dst_ref=target,
+            send_sem=send_sem.at[n],
+            recv_sem=recv_sem.at[n],
+            device_id=sibling,
+            device_id_type=pl.DeviceIdType.MESH,
+        )
+        copy.start()
+        sent.append(copy)
+
+    dy = dy_ref[...]
+    dyh[0] = dy[:, :half]
+    dyh[1] = dy[:, half:]
+    send(dyh.at[1 - core], dy_in)
+    mix = mix_ref[...]
+    mixed[0] = mix.astype(bf16)
+    send(mixed.at[0], mixed.at[1])
+    loads[0].wait()
+    middle = atoms_ref[...].astype(f32) + matmul(mixed[0], ow[...]) + small_ref[0:1, :]
+    standard, inverse = standardize(middle)
+    gain = small_ref[1:2, :]
+    inner[0] = (standard * gain + small_ref[2:3, :]).astype(bf16)
+    send(inner.at[0], inner.at[1])
+    loads[1].wait()
+    loads[2].wait()
+    result = middle + small_ref[3:4, :]
+    grad_inner = jnp.zeros((here, width), f32)
+    for b in range(blocks):
+        cols = slice(width * b, width * (b + 1))
+        pre = matmul(inner[0], iw[:, cols]) + bias_ref[:, cols]
+        cdf = 0.5 + 0.5 * lax.erf(pre * (0.5**0.5))
+        low = (pre * cdf).astype(bf16)
+        act[0, b] = low
+        send(act.at[0, b], act.at[1, b])
+        slope = cdf + pre * (jnp.exp(-0.5 * pre * pre) * 0.3989422804014327)
+        grad = (times_transposed(dy, uw[cols, :]) * slope).astype(bf16)
+        dpre[b] = grad
+        result = result + matmul(low, uw[cols, :])
+        grad_inner = grad_inner + times_transposed(grad, iw[:, cols])
+        vec_ref[b : b + 1, :] = jnp.sum(grad.astype(f32), axis=0, keepdims=True)
+    for i in range(blocks // 2):
+        send(dpre.at[(blocks // 2) * (1 - core) + i], dpre_in.at[i])
+    out_ref[...] = result.astype(bf16)
+    dy_wide = dy.astype(f32)
+    grad_middle = dy_wide + norm_back(grad_inner * gain, standard, inverse)
+    dmid_ref[...] = grad_middle
+    low = grad_middle.astype(bf16)
+    branch[0] = low[:, :half]
+    branch[1] = low[:, half:]
+    send(branch.at[1 - core], branch_in)
+    down = lambda value: jnp.sum(value, axis=0, keepdims=True)
+    vec_ref[blocks : blocks + 1, :] = down(low.astype(f32))
+    vec_ref[blocks + 1 : blocks + 2, :] = down(grad_inner * standard)
+    vec_ref[blocks + 2 : blocks + 3, :] = down(grad_inner)
+    vec_ref[blocks + 3 : blocks + 4, :] = down(dy_wide)
+    scaled = times_transposed(low, ow[...]).astype(bf16).astype(f32) * rl_ref[...]
+    nm_ref[...] = (-scaled * mix).astype(bf16)
+    scaled = scaled.astype(bf16)
+    dm_ref[...] = scaled
+    for s in range(slots):
+        dmt_ref[s] = scaled[rows * s : rows * (s + 1)].astype(f32).T.astype(bf16)
+
+    for copy in sent:
+        copy.wait()
+    tall, short = blocks * width // parts, width // parts
+    dy_own = dyh[core]
+    for b in range(blocks):
+        grads[width * b : width * (b + 1), :] = outer_sum(act[0, b], dy_own) + outer_sum(act[1, b], dy_in[...])
+    base = blocks * width
+    for i in range(blocks // 2):
+        grad = outer_sum(inner[0], dpre[(blocks // 2) * core + i]) + outer_sum(inner[1], dpre_in[i])
+        for k in range(2):
+            grads[base + width * (2 * i + k) : base + width * (2 * i + k + 1), :] = grad[:, half * k : half * (k + 1)]
+    last = base + width * blocks
+    grads[last:, :] = outer_sum(mixed[0], branch[core]) + outer_sum(mixed[1], branch_in[...])
+    at = lambda start, n: grads[pl.ds(pl.multiple_of(start, 8), n), :]
+    long, rest = tall // 8 * 3, tall // 4
+    for p in range(parts):
+        j = xor(dp, p, bits)
+        ref = a_send if p & 1 else a_keep
+        for r in range(2):
+            h = other_bit(y, 0, r)
+            ref[p >> 1, r] = at(j * tall + h * long, long).astype(ref.dtype)
+        for r, ref in ((0, b_keep), (1, b_send)):
+            h = other_bit(y, 0, r)
+            for k in range(2):
+                ref[p, short * k : short * (k + 1), :] = at(
+                    base + width * (2 * h + k) + short * j, short
+                ).astype(ref.dtype)
+        ref = c_send if p & 2 else c_keep
+        for r in range(2):
+            h = other_bit(y, 0, r)
+            start = h * (last + short * j) + (1 - h) * (j * tall + 2 * long)
+            ref[(p >> 2) * 2 + (p & 1), r] = at(start, rest).astype(ref.dtype)
+
+
+def middle(parts, mix, rl, atoms, dy, small, bias, out_w, inner_w, outer_w, slots):
+    here, width = atoms.shape
+    hidden = inner_w.shape[1]
+    blocks, half, rows = hidden // width, width // 2, here // slots
+    tall, short = hidden // parts, width // parts
+    long, rest = tall // 8 * 3, tall // 4
+    assert hidden == 4 * width and rest == short
     vm = pl.BlockSpec(memory_space=pltpu.VMEM)
+    hbm = pl.BlockSpec(memory_space=pl.ANY)
+    like = jax.ShapeDtypeStruct
+    out_shape = [
+        like((here, width), bf16),
+        like((parts // 2, 2, long, half), f32),
+        like((parts // 2, 2, long, half), bf16),
+        like((parts, 2 * short, half), f32),
+        like((parts, 2 * short, half), bf16),
+        like((parts // 2, 2, rest, half), f32),
+        like((parts // 2, 2, rest, half), bf16),
+        like((here, width), bf16),
+        like((here, width), bf16),
+        like((slots, width, rows), bf16),
+        like((here, width), f32),
+        like((blocks + 4, width), f32),
+    ]
+    transfers = 3 + blocks + blocks // 2 + 1
     return pl.pallas_call(
-        ffn_grad_kernel,
-        in_specs=[pl.BlockSpec(memory_space=pltpu.SMEM)] + [vm] * 6,
-        out_specs=vm,
-        out_shape=jax.ShapeDtypeStruct((parts, rows, half), bf16),
-        name="ffn_grads",
-        cost_estimate=pl.CostEstimate(flops=2 * 384 * 2304 * 512, transcendentals=0, bytes_accessed=6 << 20),
-        compiler_params=pltpu.CompilerParams(vmem_limit_bytes=40 << 20),
-    )(me, act, dy, inner, dpre, mixed, branch)
+        functools.partial(middle_kernel, parts),
+        in_specs=[vm] * 6 + [hbm] * 3,
+        out_specs=[vm] * len(out_shape),
+        out_shape=out_shape,
+        scratch_shapes=[
+            pltpu.VMEM((width, width), bf16),
+            pltpu.VMEM((width, hidden), bf16),
+            pltpu.VMEM((hidden, width), bf16),
+            pltpu.VMEM((2, blocks, here, width), bf16),
+            pltpu.VMEM((blocks, here, width), bf16),
+            pltpu.VMEM((blocks // 2, here, width), bf16),
+            pltpu.VMEM((2, here, width), bf16),
+            pltpu.VMEM((2, here, width), bf16),
+            pltpu.VMEM((2, here, half), bf16),
+            pltpu.VMEM((here, half), bf16),
+            pltpu.VMEM((2, here, half), bf16),
+            pltpu.VMEM((here, half), bf16),
+            pltpu.VMEM((2 * hidden + width, half), f32),
+            pltpu.SemaphoreType.DMA((3,)),
+            pltpu.SemaphoreType.DMA((transfers,)),
+            pltpu.SemaphoreType.DMA((transfers,)),
+        ],
+        name="middle",
+        cost_estimate=pl.CostEstimate(
+            flops=12 * here * width * hidden, transcendentals=2 * here * hidden, bytes_accessed=12 << 20
+        ),
+        compiler_params=pltpu.CompilerParams(
+            vmem_limit_bytes=40 << 20, collective_id=1, has_side_effects=True
+        ),
+    )(mix, rl, atoms, dy, small, bias, out_w, inner_w, outer_w)
 
 
 def attn_grad_kernel(scale, me_ref, normed_ref, own_ref, dq_ref, dkt_ref, dvt_ref, vec_ref, out_ref):
@@ -360,7 +549,6 @@
     order = jnp.arange(group, dtype=jnp.int32) ^ row
     atoms_all = jnp.take(stack, order, axis=0)
     atoms_all = jnp.swapaxes(atoms_all, 0, 1).reshape(slots, full, width)
-    top_other = swap(atoms_cotangent, row_bit=0)
 
     cumulative = jnp.cumsum(mol_counts, axis=1)
     position = jnp.arange(full, dtype=jnp.int32)
@@ -372,7 +560,6 @@
 
     gain_one = attn_gain.astype(f32)
     shift_one = attn_shift.astype(f32)
-    gain_two = ffn_gain.astype(f32)
     atoms_flat = atoms.astype(f32).reshape(here, width)
     standard_one, inverse_one = standardize(atoms_flat)
     normed = (standard_one * gain_one + shift_one).astype(bf16)
@@ -390,45 +577,81 @@
     pair_out, weights, mixed_wide, inverse_sum = attention_forward(
         queries, turn(keys), values, pair_bias, mask
     )
-    mixed = mixed_wide.reshape(here, width).astype(bf16)
-    middle = atoms_flat + matmul(mixed, out_weight) + out_bias.astype(f32)
-    standard_two, inverse_two = standardize(middle)
-    inner = (standard_two * gain_two + ffn_shift.astype(f32)).astype(bf16)
-    pre = matmul(inner, inner_weight) + inner_bias.astype(f32)
-    activation, gelu_back = jax.vjp(lambda u: jax.nn.gelu(u, approximate=False), pre)
-    act_low = activation.astype(bf16)
-    result = middle + matmul(act_low, outer_weight) + outer_bias.astype(f32)
-    atoms_out = result.astype(bf16).reshape(slots, part_rows, width)
-    grad_top = atoms_cotangent.reshape(here, width)
-    grad_act = times_transposed(grad_top, outer_weight)
-    grad_pre = gelu_back(grad_act)[0].astype(bf16)
-    grad_inner = times_transposed(grad_pre, inner_weight)
-    grad_middle = grad_top.astype(f32) + norm_back(grad_inner * gain_two, standard_two, inverse_two)
-    grad_branch = grad_middle.astype(bf16)
-    grad_mixed = times_transposed(grad_branch, out_weight).astype(bf16)
+    small = jnp.stack([out_bias, ffn_gain, ffn_shift, outer_bias]).astype(f32)
+    (
+        atoms_out,
+        a_keep,
+        a_send,
+        b_keep,
+        b_send,
+        c_keep,
+        c_send,
+        scaled,
+        centre,
+        scaled_turned,
+        grad_middle,
+        middle_vectors,
+    ) = middle(
+        parts,
+        mixed_wide.reshape(here, width),
+        inverse_sum.reshape(here, width),
+        atoms.reshape(here, width),
+        atoms_cotangent.reshape(here, width),
+        small,
+        inner_bias.astype(f32).reshape(1, hidden),
+        out_weight,
+        inner_weight,
+        outer_weight,
+        slots,
+    )
+    atoms_out = atoms_out.reshape(slots, part_rows, width)
+
+    nbits = len(dp_bits)
+    names = ["d%d" % b for b in reversed(dp_bits)] + ["y"]
+
+    def tagged(array, used):
+        left = [n for n in names if n != used]
+        return array.reshape((2,) * len(left) + array.shape[-2:]), left
+
+    def partner(array, name):
+        return swap(array, row_bit=1) if name == "y" else swap(array, dp_bit=int(name[1:]))
+
+    def stage(array, left, name):
+        axis = left.index(name)
+        keep = lax.index_in_dim(array, 0, axis, keepdims=False)
+        send = lax.index_in_dim(array, 1, axis, keepdims=False).astype(bf16)
+        return keep.astype(f32) + partner(send, name).astype(f32), [n for n in left if n != name]
+
+    def begin(keep, send, name):
+        array, left = tagged(keep, name)
+        got, _ = tagged(partner(send, name), name)
+        return array + got.astype(f32), left
+
+    def finish(array, left, order):
+        for name in order:
+            array, left = stage(array, left, name)
+        other = swap(array.astype(bf16), row_bit=1).astype(f32)
+        return jnp.where(y == 0, jnp.stack([array, other]), jnp.stack([other, array]))
+
+    a_part, a_left = begin(a_keep, a_send, "d0")
+    b_part, b_left = begin(
+        b_keep.reshape((parts,) + b_keep.shape[1:]), b_send.reshape((parts,) + b_send.shape[1:]), "y"
+    )
+    c_part, c_left = begin(c_keep, c_send, "d1")
+    more = ["d%d" % b for b in dp_bits[2:]]
+    a_total = finish(a_part, a_left, ["y", "d1"] + more)
+    b_total = finish(b_part, b_left, ["d1", "d0"] + more)
+    c_total = finish(c_part, c_left, ["d0", "y"] + more)
 
     def pick(array, which):
         return lax.dynamic_slice_in_dim(array, which * (array.shape[1] // 2), array.shape[1] // 2, 1)
 
     pair_of = lambda own, send: jnp.stack([own, swap(send, row_bit=0)])
-    act_two = pair_of(act_low, act_low)
-    inner_two = pair_of(inner, inner)
-    mixed_two = pair_of(mixed, mixed)
-    pre_two = pair_of(pick(grad_pre, core), pick(grad_pre, 1 - core))
-    branch_two = pair_of(pick(grad_branch, core), pick(grad_branch, 1 - core))
-    top_two = jnp.stack([pick(grad_top, core), pick(top_other.reshape(here, width), core)])
-    ffn_packed = ffn_grads(me, parts, act_two, top_two, inner_two, pre_two, mixed_two, branch_two)
-    cut = hidden // parts
-    ffn_first = ffn_packed[:, :cut]
-    ffn_second = ffn_packed[:, cut:]
-    first_total = reduce_x_first(swap, ffn_first, dp_bits)
-    second_total = reduce_y_first(swap, ffn_second, dp_bits, y)
-
-    scaled = grad_mixed.astype(f32) * inverse_sum.reshape(here, width)
-    centre = (-scaled * mixed_wide.reshape(here, width)).astype(bf16).reshape(queries.shape)
-    scaled = scaled.astype(bf16).reshape(queries.shape)
+
+    scaled = scaled.reshape(queries.shape)
+    centre = centre.reshape(queries.shape)
     pair_grad, grad_queries, dkt, dvt = attention_backward(
-        turn(queries), scaled, turn(scaled), centre, keys, values_turned, weights, pair_cotangent
+        turn(queries), scaled, scaled_turned, centre, keys, values_turned, weights, pair_cotangent
     )
     grad_queries = grad_queries.reshape(here, width)
 
@@ -451,13 +674,13 @@
         jnp.sum(grad_normed, axis=0),
         jnp.sum(grad_queries.astype(f32), axis=0) * scale,
         jnp.sum(dvt.astype(f32), axis=(0, 2)),
-        jnp.sum(grad_branch.astype(f32), axis=0),
-        jnp.sum(grad_inner * standard_two, axis=0),
-        jnp.sum(grad_inner, axis=0),
-        jnp.sum(grad_top.astype(f32), axis=0),
+        middle_vectors[4],
+        middle_vectors[5],
+        middle_vectors[6],
+        middle_vectors[7],
     )
     vectors = jnp.concatenate(
-        [v.reshape(parts, -1) for v in short] + [jnp.sum(grad_pre.astype(f32), axis=0).reshape(parts, -1)],
+        [v.reshape(parts, -1) for v in short] + [middle_vectors[:4].reshape(parts, -1)],
         axis=1,
     )
     vectors = vectors + swap(vectors, row_bit=0)
@@ -482,7 +705,8 @@
     third_total = reduce_x_first(swap, attn_packed[:, : attn_packed.shape[1] // 2], dp_bits)
     fourth_total = reduce_y_first(swap, attn_packed[:, attn_packed.shape[1] // 2 :], dp_bits, y)
 
-    total = jnp.concatenate([first_total, second_total, third_total, fourth_total], axis=0)
+    first = jnp.concatenate([a_total.reshape(-1, half), c_total[0]], axis=0)
+    total = jnp.concatenate([first, b_total.reshape(-1, half), c_total[1], third_total, fourth_total], axis=0)
     other = swap(total, row_bit=0)
     left = jnp.where(core == 0, total, other)
     right = jnp.where(core == 0, other, total)

time: 211 us -> 159 us (0.75)
  other arithmetic: 48.3 us -> 26.7 us
  matrix products: 21.4 us -> 4.89 us
  local copies, waits for them, and re-layouts: 48.6 us -> 35.6 us
  waiting for transfers between devices: 32.1 us -> 22.2 us
  Pallas kernels: 24.2 us -> 31.4 us
  starting transfers between devices: 32.1 us -> 35.2 us
    ppermute x34, waiting for transfers between devices: 32.1 us -> 22.2 us  [swap(): return lax.ppermute(array, ('dp', 'rows'), pairs)]
    another operation x9 -> x3, other arithmetic: 11.3 us -> 2.15 us  [local(): pair_of = lambda own, send: jnp.stack([own, swap(send, row_bit=0)])]
    dot_general x4 -> x1, matrix products: 8.08 us -> 0.32 us  [times_transposed(): lax.dot_general(left, right, (((1,), (1,)), ((), ())), preferred_element_...]
    convert_element_type x10 -> x1, other arithmetic: 7.59 us -> 0.02 us  [local(): small = jnp.stack([out_bias, ffn_gain, ffn_shift, outer_bias]).astype(f32)]
    pallas_call x1, Pallas kernels: 1.53 us -> 8.7 us  [middle(): pl.pallas_call(functools.partial(middle_kernel, parts), in_specs=[vm] * 6...]
    dot_general x6 -> x3, matrix products: 10 us -> 3.32 us  [matmul(): return jnp.dot(left, right, preferred_element_type=f32)]
    add x2 -> x9, other arithmetic: 0.04 us -> 6.39 us  [the longest x6 3.99 us: stage(): keep.astype(f32) + partner(send, name).astype(f32)]
    convert_element_type x7 -> x4, other arithmetic: 5.5 us -> 0.25 us  [add_low(): return (left.astype(f32) + right.astype(f32)).astype(bf16)]
  transfers between devices with their start and end apart: 34 -> 34, of which waited for: 11 -> 13; matrix products, arithmetic and copies ran while one was open for 39% -> 22% of each run, Pallas kernels for 7% -> 0%
where the time goes in v2:
time: 159 us; the launch traced here: 158 us
  local copies, waits for them, and re-layouts  35.6 us (22%)
  starting transfers between devices  35.2 us (22%)
  Pallas kernels  31.4 us (20%)
  other arithmetic  26.7 us (17%)
  waiting for transfers between devices  22.2 us (14%)
  matrix products  4.89 us (3%)
  between operations  1.87 us (1%)
    ppermute x34, starting transfers between devices, swap(): return lax.ppermute(array, ('dp', 'rows'), pairs)  35.2 us
    ppermute x34, waiting for transfers between devices, swap(): return lax.ppermute(array, ('dp', 'rows'), pairs)  22.2 us
    unnamed x134, local copies, waits for them, and re-layouts  14.3 us
    pallas_call x1, Pallas kernels, attention_backward(): pl.pallas_call(backward_kernel, grid=(slots, heads // step), in_specs=[tu...  11.7 us
    pallas_call x1, Pallas kernels, attention_forward(): pl.pallas_call(forward_kernel, grid=(slots, heads // step), in_specs=[nat...  10.2 us
    pallas_call x1, Pallas kernels, middle(): pl.pallas_call(functools.partial(middle_kernel, parts), in_specs=[vm] * 6...  8.7 us
    add x6, other arithmetic, stage(): keep.astype(f32) + partner(send, name).astype(f32)  3.99 us
    dot_general x3, matrix products, matmul(): return jnp.dot(left, right, preferred_element_type=f32)  3.32 us
  transfers between devices with their start and end apart: 34, of which 13 were waited for; matrix products, arithmetic and copies ran while one was open for 22% of the time, Pallas kernels for 0%

profile of v2, /device:TPU:0, one launch (start us, length us, event | category | flops | bytes accessed | tf_op | source)
XLA Modules:
  0.0 157.7 jit_solution(15033347782198863825)
XLA Ops:
  1.2 2.6 %collective-permute-start.1 = (bf16[3,64,512]{2,1,0:T(8,128)(2,1)}, bf16[3,64,512]{2,1,0:T(8,128)(2,1)S(1)}, u32[]{:S(2)}, u32[]{:S(2)}) collective-permute-start(bf16[3,64,512]{2,1,0:T(8,128)(2,1)} %param.22), channel_id=1, source_target_pairs={{0,2},{1,3},{2,0},{3,1},{4,6},{5,7},{6,4},{7,5},{8,10},{9,11},{10,... | collective-permute-start | bytes 589832 | tf_op jit(solution)/shard_map/ppermute | solution.py:455
  4.4 1.0 convert_reduce_fusion.3
  5.5 1.1 multiply_reduce_fusion.4
  6.6 1.0 convert_element_type.319
  15.4 1.0 fusion.27
  23.3 1.2 copy-done.20
  26.9 2.5 %add_convert_fusion.1 = bf16[768,512]{1,0:T(8,128)(2,1)} fusion(bf16[768,512]{1,0:T(8,128)(2,1)S(1)} %copy-done.39, bf16[512,512]{1,0:T(8,128)(2,1)} %param.30, f32[512]{0:T(512)S(1)} %convert_element_type.331), kind=kOutput, calls=%fused_computation.16 | convolution fusion | flops 403439616 | bytes 2099200 | tf_op jit(solution)/shard_map/dot_general | solution.py:32
  29.3 1.4 copy.194
  30.8 1.1 copy-done.6
  31.9 10.2 %attention_forward.1 = (bf16[3,64,64,256]{3,2,1,0:T(8,128)(2,1)}, bf16[3,64,64,256]{3,2,1,0:T(8,128)(2,1)}, f32[3,64,512]{2,1,0:T(8,128)S(1)}, f32[3,64,512]{2,1,0:T(8,128)S(1)}) custom-call(bf16[3,64,512]{2,1,0:T(8,128)(2,1)S(1)} %bitcast.347, bf16[3,512,256]{2,1,0:T(8,128)(2,1)S(1)} %copy.192.kt_ref, bf16[3,256,512]{2,1,0:T(8,128)(2,1)S(1)} %bitcast.345, ...), custom_call_target="tpu_custom_call" | custom-call | flops 3221225472 | bytes 18874368 | tf_op jit(solution)/shard_map/attention_forward/pallas_call | solution.py:81
  42.1 8.7 %middle.1 = (bf16[192,512]{1,0:T(8,128)(2,1)S(1)}, f32[4,2,96,256]{3,2,1,0:T(8,128)S(1)}, bf16[4,2,96,256]{3,2,1,0:T(8,128)(2,1)}, f32[8,128,256]{2,1,0:T(8,128)...) custom-call(f32[192,512]{1,0:T(8,128)S(1)} %bitcast.353, ...), custom_call_target="tpu_custom_call" | custom-call | flops 2415919104 | bytes 12582912 | tf_op jit(solution)/shard_map/middle/pallas_call | solution.py:378
  50.8 1.0 copy-done.4
  54.2 11.7 %attention_backward.1 = (bf16[3,64,64,256]{3,2,1,0:T(8,128)(2,1)}, bf16[3,64,512]{2,1,0:T(8,128)(2,1)S(1)}, bf16[3,512,256]{2,1,0:T(8,128)(2,1)S(1)}, bf16[3,512,256]{2,1,0:T(8,128)(2,1)S(1)}) custom-call(bf16[3,512,64]{2,1,0:T(8,128)(2,1)S(1)} %bitcast.348, bf16[3,64,512]{2,1,0:T(8,128)(2,1)S(1)} %bitcast.355, ...), custom_call_target="tpu_custom_call" | custom-call | flops 4831838208 | bytes 18874368 | tf_op jit(solution)/shard_map/attention_backward/pallas_call | solution.py:155
  70.6 1.6 collective-permute-start.10
  72.2 1.5 collective-permute-start.5
  74.8 1.8 %gather_fusion.2 = bf16[4,3,64,512]{3,2,1,0:T(8,128)(2,1)} fusion(bf16[4,3,64,512]{3,2,0,1:T(8,128)(2,1)S(1)} %bitcast.359, s32[1024]{0:T(1024)} %copy-done.58), kind=kCustom, calls=%fused_computation.1.clone | custom fusion | bytes 1572880 | tf_op jit(solution)/shard_map/jit(_take)/gather | solution.py:662
  80.4 1.2 collective-permute-start.11
  83.1 3.5 %collective-permute-done.11 = bf16[2,2,64,256]{3,2,1,0:T(8,128)(2,1)} collective-permute-done((bf16[2,2,64,256]{3,2,1,0:T(8,128)(2,1)}, bf16[2,2,64,256]{3,2,1,0:T(8,128)(2,1)}, u32[]{:S(2)}, u32[]{:S(2)}) %collective-permute-start.11) | collective-permute-done | bytes 131104 | tf_op jit(solution)/shard_map/ppermute | solution.py:455
  87.5 1.6 %collective-permute-start.12 = (bf16[2,64,256]{2,1,0:T(8,128)(2,1)S(1)}, bf16[2,64,256]{2,1,0:T(8,128)(2,1)S(1)}, u32[]{:S(2)}, u32[]{:S(2)}) collective-permute-start(bf16[2,64,256]{2,1,0:T(8,128)(2,1)S(1)} %fusion.48), channel_id=1, source_target_pairs={{0,2},{1,3},{2,0},{3,1},{4,6},{5,7},{6,4},{7,5},{8,10},{9,11},{10,... | collective-permute-start | bytes 196616 | tf_op jit(solution)/shard_map/ppermute | solution.py:455
  89.1 1.1 convert_add_fusion.2
  91.7 1.6 %collective-permute-start.4 = (bf16[3,64,512]{2,1,0:T(8,128)(2,1)S(1)}, bf16[3,64,512]{2,1,0:T(8,128)(2,1)S(1)}, u32[]{:S(2)}, u32[]{:S(2)}) collective-permute-start(bf16[3,64,512]{2,1,0:T(8,128)(2,1)S(1)} %slice_bitcast_fusion.9), channel_id=1, source_target_pairs={{0,2},{1,3},{2,0},{3,1},{4,6},{5,7},{6,4},{7,5},{8,10},{9,11},{10,... | collective-permute-start | bytes 589832 | tf_op jit(solution)/shard_map/ppermute | solution.py:455
  93.3 1.2 pad_maximum_fusion.1.dkt_ref
  94.5 2.6 %collective-permute-start.13 = (bf16[64,256]{1,0:T(8,128)(2,1)S(1)}, bf16[64,256]{1,0:T(8,128)(2,1)S(1)}, u32[]{:S(2)}, u32[]{:S(2)}) collective-permute-start(bf16[64,256]{1,0:T(8,128)(2,1)S(1)} %fusion.60), channel_id=1, source_target_pairs={{0,16},{1,17},{2,18},{3,19},{4,20},{5,21},{6,22},{7,23},{8,24},{9,... | collective-permute-start | bytes 98312 | tf_op jit(solution)/shard_map/ppermute | solution.py:455
  97.2 2.4 %collective-permute-done.13 = bf16[64,256]{1,0:T(8,128)(2,1)S(1)} collective-permute-done((bf16[64,256]{1,0:T(8,128)(2,1)S(1)}, bf16[64,256]{1,0:T(8,128)(2,1)S(1)}, u32[]{:S(2)}, u32[]{:S(2)}) %collective-permute-start.13) | collective-permute-done | bytes 32800 | tf_op jit(solution)/shard_map/ppermute | solution.py:455
  100.2 1.2 convert_add_fusion
  102.5 1.1 collective-permute-done.14
  105.7 1.1 fusion.18
  110.2 1.5 collective-permute-start.24
  111.6 1.3 collective-permute-done.7
  113.9 2.4 %collective-permute-start.8 = (bf16[96,256]{1,0:T(8,128)(2,1)S(1)}, bf16[96,256]{1,0:T(8,128)(2,1)S(1)}, u32[]{:S(2)}, u32[]{:S(2)}) collective-permute-start(bf16[96,256]{1,0:T(8,128)(2,1)S(1)} %fusion.57), channel_id=1, source_target_pairs={{0,16},{1,17},{2,18},{3,19},{4,20},{5,21},{6,22},{7,23},{8,24},{9,... | collective-permute-start | bytes 147464 | tf_op jit(solution)/shard_map/ppermute | solution.py:455
  117.1 2.4 %collective-permute-done.8 = bf16[96,256]{1,0:T(8,128)(2,1)S(1)} collective-permute-done((bf16[96,256]{1,0:T(8,128)(2,1)S(1)}, bf16[96,256]{1,0:T(8,128)(2,1)S(1)}, u32[]{:S(2)}, u32[]{:S(2)}) %collective-permute-start.8) | collective-permute-done | bytes 49184 | tf_op jit(solution)/shard_map/ppermute | solution.py:455
  119.9 1.0 fusion.12
  121.0 1.6 %collective-permute-start.17 = (bf16[2,128,256]{2,1,0:T(8,128)(2,1)S(1)}, bf16[2,128,256]{2,1,0:T(8,128)(2,1)S(1)}, u32[]{:S(2)}, u32[]{:S(2)}) collective-permute-start(bf16[2,128,256]{2,1,0:T(8,128)(2,1)S(1)} %fusion.38), channel_id=1, source_target_pairs={{0,4},{1,5},{2,6},{3,7},{4,0},{5,1},{6,2},{7,3},{8,12},{9,13},{10,... | collective-permute-start | bytes 393224 | tf_op jit(solution)/shard_map/ppermute | solution.py:455
  122.6 1.4 collective-permute-done.9
  125.5 1.4 collective-permute-start.29
  126.9 2.0 %collective-permute-start.18 = (bf16[128,256]{1,0:T(8,128)(2,1)S(1)}, bf16[128,256]{1,0:T(8,128)(2,1)S(1)}, u32[]{:S(2)}, u32[]{:S(2)}) collective-permute-start(bf16[128,256]{1,0:T(8,128)(2,1)S(1)} %fusion.49), channel_id=1, source_target_pairs={{0,16},{1,17},{2,18},{3,19},{4,20},{5,21},{6,22},{7,23},{8,24},{9,... | collective-permute-start | bytes 196616 | tf_op jit(solution)/shard_map/ppermute | solution.py:455
  128.9 1.4 collective-permute-done.29
  130.4 1.4 collective-permute-start.30
  131.9 1.5 collective-permute-start.26
  133.4 1.8 %collective-permute-done.30 = bf16[2,52,256]{2,1,0:T(8,128)(2,1)S(1)} collective-permute-done((bf16[2,52,256]{2,1,0:T(8,128)(2,1)S(1)}, bf16[2,52,256]{2,1,0:T(8,128)(2,1)S(1)}, u32[]{:S(2)}, u32[]{:S(2)}) %collective-permute-start.30) | collective-permute-done | bytes 53280 | tf_op jit(solution)/shard_map/ppermute | solution.py:455
  135.3 1.3 collective-permute-start.31
  136.6 1.7 %collective-permute-start.19 = (bf16[128,256]{1,0:T(8,128)(2,1)S(1)}, bf16[128,256]{1,0:T(8,128)(2,1)S(1)}, u32[]{:S(2)}, u32[]{:S(2)}) collective-permute-start(bf16[128,256]{1,0:T(8,128)(2,1)S(1)} %get-tuple-element.85), channel_id=1, source_target_pairs={{0,2},{1,3},{2,0},{3,1},{4,6},{5,7},{6,4},{7,5},{8,10},{9,11},{10,... | collective-permute-start | bytes 196616 | tf_op jit(solution)/shard_map/ppermute | solution.py:455
  138.3 1.8 %collective-permute-done.31 = bf16[1,52,256]{2,1,0:T(8,128)(2,1)S(1)} collective-permute-done((bf16[1,52,256]{2,1,0:T(8,128)(2,1)S(1)}, bf16[1,52,256]{2,1,0:T(8,128)(2,1)S(1)}, u32[]{:S(2)}, u32[]{:S(2)}) %collective-permute-start.31) | collective-permute-done | bytes 26656 | tf_op jit(solution)/shard_map/ppermute | solution.py:455
  140.1 1.3 collective-permute-start.32
  142.3 1.8 %collective-permute-done.32 = bf16[52,256]{1,0:T(8,128)(2,1)S(1)} collective-permute-done((bf16[52,256]{1,0:T(8,128)(2,1)S(1)}, bf16[52,256]{1,0:T(8,128)(2,1)S(1)}, u32[]{:S(2)}, u32[]{:S(2)}) %collective-permute-start.32) | collective-permute-done | bytes 26656 | tf_op jit(solution)/shard_map/ppermute | solution.py:455
  144.2 1.4 collective-permute-done.27
  146.6 1.4 collective-permute-done.33
  153.3 1.1 reshape.647
  (309 shorter events, 54.7 us)
Async XLA Ops:
  0.7 24.2 %copy-start = (bf16[512,512]{1,0:T(8,128)(2,1)S(1)}, bf16[512,512]{1,0:T(8,128)(2,1)}, u32[]{:S(2)}) copy-start(bf16[512,512]{1,0:T(8,128)(2,1)} %param.29) | copy-start | bytes 1572868
  0.7 15.8 %copy-start.32 = (bf16[512,512]{1,0:T(8,128)(2,1)S(1)}, bf16[512,512]{1,0:T(8,128)(2,1)}, u32[]{:S(2)}) copy-start(bf16[512,512]{1,0:T(8,128)(2,1)} %param.27) | copy-start | bytes 1572868
  0.7 17.2 %collective-permute-start = (bf16[3,64,512]{2,1,0:T(8,128)(2,1)}, bf16[3,64,512]{2,1,0:T(8,128)(2,1)S(1)}, u32[]{:S(2)}, u32[]{:S(2)}) collective-permute-start(bf16[3,64,512]{2,1,0:T(8,128)(2,1)} %param.22), channel_id=1, source_target_pairs={{0,1},{1,0},{2,3},{3,2},{4,5},{5,4},{6,7},{7,6},{8,9},{9,8},{10,11... | collective-permute-start | bytes 589832 | tf_op jit(solution)/shard_map/ppermute | solution.py:455
  1.2 17.2 %collective-permute-start.1 = (bf16[3,64,512]{2,1,0:T(8,128)(2,1)}, bf16[3,64,512]{2,1,0:T(8,128)(2,1)S(1)}, u32[]{:S(2)}, u32[]{:S(2)}) collective-permute-start(bf16[3,64,512]{2,1,0:T(8,128)(2,1)} %param.22), channel_id=1, source_target_pairs={{0,2},{1,3},{2,0},{3,1},{4,6},{5,7},{6,4},{7,5},{8,10},{9,11},{10,... | collective-permute-start | bytes 589832 | tf_op jit(solution)/shard_map/ppermute | solution.py:455
  3.8 19.1 %copy-start.56 = (pred[4]{0:T(512)(128)(4,1)}, pred[4]{0:T(512)(128)(4,1)S(1)}, u32[]{:S(2)}) copy-start(pred[4]{0:T(512)(128)(4,1)S(1)} %compare_and_fusion) | copy-start | bytes 16
  5.5 13.2 %copy-start.48 = (f32[192]{0:T(256)}, f32[192]{0:T(256)S(1)}, u32[]{:S(2)}) copy-start(f32[192]{0:T(256)S(1)} %div.41) | copy-start | bytes 2308
  8.3 15.0 %copy-start.43 = (f32[512]{0:T(512)}, f32[512]{0:T(512)S(1)}, u32[]{:S(2)}) copy-start(f32[512]{0:T(512)S(1)} %convert_element_type.320) | copy-start | bytes 6148
  9.0 14.3 %copy-start.46 = (f32[512]{0:T(512)}, f32[512]{0:T(512)S(1)}, u32[]{:S(2)}) copy-start(f32[512]{0:T(512)S(1)} %convert_element_type.321) | copy-start | bytes 6148
  18.5 1.5 collective-permute-start.2
  31.9 10.2 %copy-start.16 = (bf16[512,2048]{1,0:T(8,128)(2,1)S(1)}, bf16[512,2048]{1,0:T(8,128)(2,1)}, u32[]{:S(2)}) copy-start(bf16[512,2048]{1,0:T(8,128)(2,1)} %inner_w.1) | copy-start | bytes 6291460
  31.9 10.2 %copy-start.17 = (bf16[2048,512]{1,0:T(8,128)(2,1)S(1)}, bf16[2048,512]{1,0:T(8,128)(2,1)}, u32[]{:S(2)}) copy-start(bf16[2048,512]{1,0:T(8,128)(2,1)} %outer_w.1) | copy-start | bytes 6291460
  31.9 10.2 %copy-start.18 = (bf16[512,512]{1,0:T(8,128)(2,1)S(1)}, bf16[512,512]{1,0:T(8,128)(2,1)}, u32[]{:S(2)}) copy-start(bf16[512,512]{1,0:T(8,128)(2,1)} %out_w.1) | copy-start | bytes 1572868
  31.9 10.2 %copy-start.19 = (bf16[3,64,512]{2,1,0:T(8,128)(2,1)S(1)}, bf16[3,64,512]{2,1,0:T(8,128)(2,1)}, u32[]{:S(2)}) copy-start(bf16[3,64,512]{2,1,0:T(8,128)(2,1)} %param.40) | copy-start | bytes 589828
  42.1 12.1 %copy-start.11 = (bf16[3,64,512]{1,2,0:T(8,128)(2,1)S(1)}, bf16[3,64,512]{1,2,0:T(8,128)(2,1)}, u32[]{:S(2)}) copy-start(bf16[3,64,512]{1,2,0:T(8,128)(2,1)} %copy.193) | copy-start | bytes 589828
  54.2 11.7 %copy-start.12 = (f32[192,512]{1,0:T(8,128)}, f32[192,512]{1,0:T(8,128)S(1)}, u32[]{:S(2)}) copy-start(f32[192,512]{1,0:T(8,128)S(1)} %get-tuple-element.44) | copy-start | bytes 1179652
  70.4 11.7 %collective-permute-start.20 = (bf16[192,256]{1,0:T(8,128)(2,1)}, bf16[192,256]{1,0:T(8,128)(2,1)}, u32[]{:S(2)}, u32[]{:S(2)}) collective-permute-start(bf16[192,256]{1,0:T(8,128)(2,1)} %get-tuple-element.91), channel_id=1, source_target_pairs={{0,1},{1,0},{2,3},{3,2},{4,5},{5,4},{6,7},{7,6},{8,9},{9,8},{10,11... | collective-permute-start | bytes 294920 | tf_op jit(solution)/shard_map/ppermute | solution.py:455
  70.6 9.0 %collective-permute-start.10 = (bf16[4,2,64,256]{3,2,1,0:T(8,128)(2,1)}, bf16[4,2,64,256]{3,2,1,0:T(8,128)(2,1)S(1)}, u32[]{:S(2)}, u32[]{:S(2)}) collective-permute-start(bf16[4,2,64,256]{3,2,1,0:T(8,128)(2,1)} %get-tuple-element.56), channel_id=1, source_target_pairs={{0,8},{1,9},{2,10},{3,11},{4,12},{5,13},{6,14},{7,15},{8,0},{9,1},... | collective-permute-start | bytes 786440 | tf_op jit(solution)/shard_map/ppermute | solution.py:455
  72.2 15.4 %collective-permute-start.5 = (bf16[4,2,96,256]{3,2,1,0:T(8,128)(2,1)}, bf16[4,2,96,256]{3,2,1,0:T(8,128)(2,1)}, u32[]{:S(2)}, u32[]{:S(2)}) collective-permute-start(bf16[4,2,96,256]{3,2,1,0:T(8,128)(2,1)} %get-tuple-element.54), channel_id=1, source_target_pairs={{0,4},{1,5},{2,6},{3,7},{4,0},{5,1},{6,2},{7,3},{8,12},{9,13},{10,... | collective-permute-start | bytes 1179656 | tf_op jit(solution)/shard_map/ppermute | solution.py:455
  73.7 26.5 %collective-permute-start.15 = (bf16[8,128,256]{2,1,0:T(8,128)(2,1)}, bf16[8,128,256]{2,1,0:T(8,128)(2,1)}, u32[]{:S(2)}, u32[]{:S(2)}) collective-permute-start(bf16[8,128,256]{2,1,0:T(8,128)(2,1)} %get-tuple-element.58), channel_id=1, source_target_pairs={{0,2},{1,3},{2,0},{3,1},{4,6},{5,7},{6,4},{7,5},{8,10},{9,11},{10,... | collective-permute-start | bytes 1572872 | tf_op jit(solution)/shard_map/ppermute | solution.py:455
  74.2 17.5 %collective-permute-start.21 = (bf16[3,256,256]{2,1,0:T(8,128)(2,1)}, bf16[3,256,256]{2,1,0:T(8,128)(2,1)}, u32[]{:S(2)}, u32[]{:S(2)}) collective-permute-start(bf16[3,256,256]{2,1,0:T(8,128)(2,1)} %get-tuple-element.83), channel_id=1, source_target_pairs={{0,1},{1,0},{2,3},{3,2},{4,5},{5,4},{6,7},{7,6},{8,9},{9,8},{10,11... | collective-permute-start | bytes 1179656 | tf_op jit(solution)/shard_map/ppermute | solution.py:455
  80.4 6.2 %collective-permute-start.11 = (bf16[2,2,64,256]{3,2,1,0:T(8,128)(2,1)}, bf16[2,2,64,256]{3,2,1,0:T(8,128)(2,1)}, u32[]{:S(2)}, u32[]{:S(2)}) collective-permute-start(bf16[2,2,64,256]{3,2,1,0:T(8,128)(2,1)} %fusion.37), channel_id=1, source_target_pairs={{0,4},{1,5},{2,6},{3,7},{4,0},{5,1},{6,2},{7,3},{8,12},{9,13},{10,... | collective-permute-start | bytes 393224 | tf_op jit(solution)/shard_map/ppermute | solution.py:455
  82.1 15.0 %collective-permute-start.22 = (bf16[3,256,256]{2,1,0:T(8,128)(2,1)}, bf16[3,256,256]{2,1,0:T(8,128)(2,1)S(1)}, u32[]{:S(2)}, u32[]{:S(2)}) collective-permute-start(bf16[3,256,256]{2,1,0:T(8,128)(2,1)} %get-tuple-element.81), channel_id=1, source_target_pairs={{0,1},{1,0},{2,3},{3,2},{4,5},{5,4},{6,7},{7,6},{8,9},{9,8},{10,11... | collective-permute-start | bytes 1179656 | tf_op jit(solution)/shard_map/ppermute | solution.py:455
  86.6 4.5 %collective-permute-start.3 = (bf16[2,3,64,512]{3,2,1,0:T(8,128)(2,1)}, bf16[2,3,64,512]{3,2,1,0:T(8,128)(2,1)S(1)}, u32[]{:S(2)}, u32[]{:S(2)}) collective-permute-start(bf16[2,3,64,512]{3,2,1,0:T(8,128)(2,1)} %slice_bitcast_fusion.2), channel_id=1, source_target_pairs={{0,1},{1,0},{2,3},{3,2},{4,5},{5,4},{6,7},{7,6},{8,9},{9,8},{10,11... | collective-permute-start | bytes 1179656 | tf_op jit(solution)/shard_map/ppermute | solution.py:455
  87.5 6.9 %collective-permute-start.12 = (bf16[2,64,256]{2,1,0:T(8,128)(2,1)S(1)}, bf16[2,64,256]{2,1,0:T(8,128)(2,1)S(1)}, u32[]{:S(2)}, u32[]{:S(2)}) collective-permute-start(bf16[2,64,256]{2,1,0:T(8,128)(2,1)S(1)} %fusion.48), channel_id=1, source_target_pairs={{0,2},{1,3},{2,0},{3,1},{4,6},{5,7},{6,4},{7,5},{8,10},{9,11},{10,... | collective-permute-start | bytes 196616 | tf_op jit(solution)/shard_map/ppermute | solution.py:455
  91.1 14.7 %collective-permute-start.6 = (bf16[2,2,96,256]{3,2,1,0:T(8,128)(2,1)}, bf16[2,2,96,256]{3,2,1,0:T(8,128)(2,1)}, u32[]{:S(2)}, u32[]{:S(2)}) collective-permute-start(bf16[2,2,96,256]{3,2,1,0:T(8,128)(2,1)} %fusion.33), channel_id=1, source_target_pairs={{0,2},{1,3},{2,0},{3,1},{4,6},{5,7},{6,4},{7,5},{8,10},{9,11},{10,... | collective-permute-start | bytes 589832 | tf_op jit(solution)/shard_map/ppermute | solution.py:455
  91.7 12.6 %collective-permute-start.4 = (bf16[3,64,512]{2,1,0:T(8,128)(2,1)S(1)}, bf16[3,64,512]{2,1,0:T(8,128)(2,1)S(1)}, u32[]{:S(2)}, u32[]{:S(2)}) collective-permute-start(bf16[3,64,512]{2,1,0:T(8,128)(2,1)S(1)} %slice_bitcast_fusion.9), channel_id=1, source_target_pairs={{0,2},{1,3},{2,0},{3,1},{4,6},{5,7},{6,4},{7,5},{8,10},{9,11},{10,... | collective-permute-start | bytes 589832 | tf_op jit(solution)/shard_map/ppermute | solution.py:455
  94.5 5.1 %collective-permute-start.13 = (bf16[64,256]{1,0:T(8,128)(2,1)S(1)}, bf16[64,256]{1,0:T(8,128)(2,1)S(1)}, u32[]{:S(2)}, u32[]{:S(2)}) collective-permute-start(bf16[64,256]{1,0:T(8,128)(2,1)S(1)} %fusion.60), channel_id=1, source_target_pairs={{0,16},{1,17},{2,18},{3,19},{4,20},{5,21},{6,22},{7,23},{8,24},{9,... | collective-permute-start | bytes 98312 | tf_op jit(solution)/shard_map/ppermute | solution.py:455
  99.6 4.0 %collective-permute-start.14 = (bf16[64,256]{1,0:T(8,128)(2,1)S(1)}, bf16[64,256]{1,0:T(8,128)(2,1)S(1)}, u32[]{:S(2)}, u32[]{:S(2)}) collective-permute-start(bf16[64,256]{1,0:T(8,128)(2,1)S(1)} %get-tuple-element.95), channel_id=1, source_target_pairs={{0,2},{1,3},{2,0},{3,1},{4,6},{5,7},{6,4},{7,5},{8,10},{9,11},{10,... | collective-permute-start | bytes 98312 | tf_op jit(solution)/shard_map/ppermute | solution.py:455
  102.3 17.7 %collective-permute-start.16 = (bf16[2,2,128,256]{3,2,1,0:T(8,128)(2,1)}, bf16[2,2,128,256]{3,2,1,0:T(8,128)(2,1)}, u32[]{:S(2)}, u32[]{:S(2)}) collective-permute-start(bf16[2,2,128,256]{3,2,1,0:T(8,128)(2,1)} %fusion.28), channel_id=1, source_target_pairs={{0,8},{1,9},{2,10},{3,11},{4,12},{5,13},{6,14},{7,15},{8,0},{9,1},... | collective-permute-start | bytes 786440 | tf_op jit(solution)/shard_map/ppermute | solution.py:455
  105.7 2.7 %collective-permute-start.23 = (f32[8,768]{1,0:T(8,128)S(1)}, f32[8,768]{1,0:T(8,128)S(1)}, u32[]{:S(2)}, u32[]{:S(2)}) collective-permute-start(f32[8,768]{1,0:T(8,128)S(1)} %concatenate.9), channel_id=1, source_target_pairs={{0,1},{1,0},{2,3},{3,2},{4,5},{5,4},{6,7},{7,6},{8,9},{9,8},{10,11... | collective-permute-start | bytes 73736 | tf_op jit(solution)/shard_map/ppermute | solution.py:455
  107.6 5.4 %collective-permute-start.7 = (bf16[2,96,256]{2,1,0:T(8,128)(2,1)S(1)}, bf16[2,96,256]{2,1,0:T(8,128)(2,1)}, u32[]{:S(2)}, u32[]{:S(2)}) collective-permute-start(bf16[2,96,256]{2,1,0:T(8,128)(2,1)S(1)} %fusion.44), channel_id=1, source_target_pairs={{0,8},{1,9},{2,10},{3,11},{4,12},{5,13},{6,14},{7,15},{8,0},{9,1},... | collective-permute-start | bytes 294920 | tf_op jit(solution)/shard_map/ppermute | solution.py:455
  110.2 13.9 %collective-permute-start.24 = (bf16[4,104,256]{2,1,0:T(8,128)(2,1)S(1)}, bf16[4,104,256]{2,1,0:T(8,128)(2,1)S(1)}, u32[]{:S(2)}, u32[]{:S(2)}) collective-permute-start(bf16[4,104,256]{2,1,0:T(8,128)(2,1)S(1)} %slice_bitcast_fusion.6), channel_id=1, source_target_pairs={{0,4},{1,5},{2,6},{3,7},{4,0},{5,1},{6,2},{7,3},{8,12},{9,13},{10,... | collective-permute-start | bytes 638984 | tf_op jit(solution)/shard_map/ppermute | solution.py:455
  113.9 5.6 %collective-permute-start.8 = (bf16[96,256]{1,0:T(8,128)(2,1)S(1)}, bf16[96,256]{1,0:T(8,128)(2,1)S(1)}, u32[]{:S(2)}, u32[]{:S(2)}) collective-permute-start(bf16[96,256]{1,0:T(8,128)(2,1)S(1)} %fusion.57), channel_id=1, source_target_pairs={{0,16},{1,17},{2,18},{3,19},{4,20},{5,21},{6,22},{7,23},{8,24},{9,... | collective-permute-start | bytes 147464 | tf_op jit(solution)/shard_map/ppermute | solution.py:455
  116.3 8.6 %collective-permute-start.28 = (bf16[8,52,256]{2,0,1:T(8,128)(2,1)S(1)}, bf16[8,52,256]{2,0,1:T(8,128)(2,1)S(1)}, u32[]{:S(2)}, u32[]{:S(2)}) collective-permute-start(bf16[8,52,256]{2,0,1:T(8,128)(2,1)S(1)} %dynamic-slice_bitcast_fusion.2), channel_id=1, source_target_pairs={{0,2},{1,3},{2,0},{3,1},{4,6},{5,7},{6,4},{7,5},{8,10},{9,11},{10,... | collective-permute-start | bytes 638984 | tf_op jit(solution)/shard_map/ppermute | solution.py:455
  119.5 4.5 %collective-permute-start.9 = (bf16[96,256]{1,0:T(8,128)(2,1)S(1)}, bf16[96,256]{1,0:T(8,128)(2,1)S(1)}, u32[]{:S(2)}, u32[]{:S(2)}) collective-permute-start(bf16[96,256]{1,0:T(8,128)(2,1)S(1)} %get-tuple-element.87), channel_id=1, source_target_pairs={{0,2},{1,3},{2,0},{3,1},{4,6},{5,7},{6,4},{7,5},{8,10},{9,11},{10,... | collective-permute-start | bytes 147464 | tf_op jit(solution)/shard_map/ppermute | solution.py:455
  121.0 5.8 %collective-permute-start.17 = (bf16[2,128,256]{2,1,0:T(8,128)(2,1)S(1)}, bf16[2,128,256]{2,1,0:T(8,128)(2,1)S(1)}, u32[]{:S(2)}, u32[]{:S(2)}) collective-permute-start(bf16[2,128,256]{2,1,0:T(8,128)(2,1)S(1)} %fusion.38), channel_id=1, source_target_pairs={{0,4},{1,5},{2,6},{3,7},{4,0},{5,1},{6,2},{7,3},{8,12},{9,13},{10,... | collective-permute-start | bytes 393224 | tf_op jit(solution)/shard_map/ppermute | solution.py:455
  124.2 7.6 %collective-permute-start.25 = (bf16[2,104,256]{2,1,0:T(8,128)(2,1)S(1)}, bf16[2,104,256]{2,1,0:T(8,128)(2,1)S(1)}, u32[]{:S(2)}, u32[]{:S(2)}) collective-permute-start(bf16[2,104,256]{2,1,0:T(8,128)(2,1)S(1)} %slice_bitcast_fusion.13), channel_id=1, source_target_pairs={{0,8},{1,9},{2,10},{3,11},{4,12},{5,13},{6,14},{7,15},{8,0},{9,1},... | collective-permute-start | bytes 319496 | tf_op jit(solution)/shard_map/ppermute | solution.py:455
  125.5 4.9 %collective-permute-start.29 = (bf16[4,52,256]{2,1,0:T(8,128)(2,1)S(1)}, bf16[4,52,256]{2,1,0:T(8,128)(2,1)S(1)}, u32[]{:S(2)}, u32[]{:S(2)}) collective-permute-start(bf16[4,52,256]{2,1,0:T(8,128)(2,1)S(1)} %bitcast.396), channel_id=1, source_target_pairs={{0,4},{1,5},{2,6},{3,7},{4,0},{5,1},{6,2},{7,3},{8,12},{9,13},{10,... | collective-permute-start | bytes 319496 | tf_op jit(solution)/shard_map/ppermute | solution.py:455
  126.9 9.7 %collective-permute-start.18 = (bf16[128,256]{1,0:T(8,128)(2,1)S(1)}, bf16[128,256]{1,0:T(8,128)(2,1)S(1)}, u32[]{:S(2)}, u32[]{:S(2)}) collective-permute-start(bf16[128,256]{1,0:T(8,128)(2,1)S(1)} %fusion.49), channel_id=1, source_target_pairs={{0,16},{1,17},{2,18},{3,19},{4,20},{5,21},{6,22},{7,23},{8,24},{9,... | collective-permute-start | bytes 196616 | tf_op jit(solution)/shard_map/ppermute | solution.py:455
  130.4 15.4 %copy-start.13 = (f32[192,512]{1,0:T(8,128)S(1)}, f32[192,512]{1,0:T(8,128)}, u32[]{:S(2)}) copy-start(f32[192,512]{1,0:T(8,128)} %copy-done.12) | copy-start | bytes 1179652
  130.4 15.4 %copy-start.25 = (f32[192,512]{1,0:T(8,128)S(1)}, f32[192,512]{1,0:T(8,128)}, u32[]{:S(2)}) copy-start(f32[192,512]{1,0:T(8,128)} %copy-done.24) | copy-start | bytes 1179652
  130.4 4.8 %collective-permute-start.30 = (bf16[2,52,256]{2,1,0:T(8,128)(2,1)S(1)}, bf16[2,52,256]{2,1,0:T(8,128)(2,1)S(1)}, u32[]{:S(2)}, u32[]{:S(2)}) collective-permute-start(bf16[2,52,256]{2,1,0:T(8,128)(2,1)S(1)} %slice_bitcast_fusion.19), channel_id=1, source_target_pairs={{0,8},{1,9},{2,10},{3,11},{4,12},{5,13},{6,14},{7,15},{8,0},{9,1},... | collective-permute-start | bytes 159752 | tf_op jit(solution)/shard_map/ppermute | solution.py:455
  131.9 9.5 %collective-permute-start.26 = (bf16[1,104,256]{2,1,0:T(8,128)(2,1)S(1)}, bf16[1,104,256]{2,1,0:T(8,128)(2,1)S(1)}, u32[]{:S(2)}, u32[]{:S(2)}) collective-permute-start(bf16[1,104,256]{2,1,0:T(8,128)(2,1)S(1)} %slice_bitcast_fusion.21), channel_id=1, source_target_pairs={{0,16},{1,17},{2,18},{3,19},{4,20},{5,21},{6,22},{7,23},{8,24},{9,... | collective-permute-start | bytes 159752 | tf_op jit(solution)/shard_map/ppermute | solution.py:455
  135.3 4.8 %collective-permute-start.31 = (bf16[1,52,256]{2,1,0:T(8,128)(2,1)S(1)}, bf16[1,52,256]{2,1,0:T(8,128)(2,1)S(1)}, u32[]{:S(2)}, u32[]{:S(2)}) collective-permute-start(bf16[1,52,256]{2,1,0:T(8,128)(2,1)S(1)} %slice_bitcast_fusion.23), channel_id=1, source_target_pairs={{0,16},{1,17},{2,18},{3,19},{4,20},{5,21},{6,22},{7,23},{8,24},{9,... | collective-permute-start | bytes 79880 | tf_op jit(solution)/shard_map/ppermute | solution.py:455
  136.6 7.5 %collective-permute-start.19 = (bf16[128,256]{1,0:T(8,128)(2,1)S(1)}, bf16[128,256]{1,0:T(8,128)(2,1)S(1)}, u32[]{:S(2)}, u32[]{:S(2)}) collective-permute-start(bf16[128,256]{1,0:T(8,128)(2,1)S(1)} %get-tuple-element.85), channel_id=1, source_target_pairs={{0,2},{1,3},{2,0},{3,1},{4,6},{5,7},{6,4},{7,5},{8,10},{9,11},{10,... | collective-permute-start | bytes 196616 | tf_op jit(solution)/shard_map/ppermute | solution.py:455
  140.1 3.9 %collective-permute-start.32 = (bf16[52,256]{1,0:T(8,128)(2,1)S(1)}, bf16[52,256]{1,0:T(8,128)(2,1)S(1)}, u32[]{:S(2)}, u32[]{:S(2)}) collective-permute-start(bf16[52,256]{1,0:T(8,128)(2,1)S(1)} %fusion.61), channel_id=1, source_target_pairs={{0,2},{1,3},{2,0},{3,1},{4,6},{5,7},{6,4},{7,5},{8,10},{9,11},{10,... | collective-permute-start | bytes 79880 | tf_op jit(solution)/shard_map/ppermute | solution.py:455
  141.4 4.2 %collective-permute-start.27 = (bf16[104,256]{1,0:T(8,128)(2,1)S(1)}, bf16[104,256]{1,0:T(8,128)(2,1)S(1)}, u32[]{:S(2)}, u32[]{:S(2)}) collective-permute-start(bf16[104,256]{1,0:T(8,128)(2,1)S(1)} %fusion.56), channel_id=1, source_target_pairs={{0,2},{1,3},{2,0},{3,1},{4,6},{5,7},{6,4},{7,5},{8,10},{9,11},{10,... | collective-permute-start | bytes 159752 | tf_op jit(solution)/shard_map/ppermute | solution.py:455
  145.6 2.4 %collective-permute-start.33 = (f32[784,256]{1,0:T(8,128)S(1)}, f32[784,256]{1,0:T(8,128)S(1)}, u32[]{:S(2)}, u32[]{:S(2)}) collective-permute-start(f32[784,256]{1,0:T(8,128)S(1)} %convert_dynamic-update-slice_fusion), channel_id=1, source_target_pairs={{0,1},{1,0},{2,3},{3,2},{4,5},{5,4},{6,7},{7,6},{8,9},{9,8},{10,11... | collective-permute-start | bytes 2408456 | tf_op jit(solution)/shard_map/ppermute | solution.py:455
  (46 other events, 160.3 us)

commit v3 on v2

v3 whole, which is shorter than its diff:
```python
import functools

import jax
import jax.numpy as jnp
from jax import lax
from jax.experimental import pallas as pl
from jax.experimental.pallas import tpu as pltpu
from jax.sharding import PartitionSpec as P

f32, bf16 = jnp.float32, jnp.bfloat16
BIG = 1e9
HPL = 16
CHUNK = 8
STEP = 32
VMEM_PAIR = 24 << 20
MESH = pl.DeviceIdType.MESH


def standardize(value):
    centred = value - jnp.mean(value, axis=-1, keepdims=True)
    inverse = lax.rsqrt(jnp.mean(centred * centred, axis=-1, keepdims=True) + 1e-05)
    return (centred * inverse, inverse)


def norm_back(grad_normed, standard, inverse):
    return inverse * (
        grad_normed
        - jnp.mean(grad_normed, axis=-1, keepdims=True)
        - standard * jnp.mean(grad_normed * standard, axis=-1, keepdims=True)
    )


def matmul(left, right):
    return jnp.dot(left, right, preferred_element_type=f32)


def times_transposed(left, right):
    return lax.dot_general(left, right, (((1,), (1,)), ((), ())), preferred_element_type=f32)


def outer_sum(left, right):
    return lax.dot_general(left, right, (((0,), (0,)), ((), ())), preferred_element_type=f32)


def other_bit(index, bit, const):
    own = (index // (1 << bit)) % 2
    return 1 - own if (const >> bit) & 1 else own


def xor(index, const, bits):
    return sum(other_bit(index, b, const) * (1 << b) for b in range(bits))


def remote(source, target, send_sem, recv_sem, device):
    copy = pltpu.make_async_remote_copy(
        src_ref=source, dst_ref=target, send_sem=send_sem, recv_sem=recv_sem, device_id=device, device_id_type=MESH
    )
    copy.start()
    return copy


def meet(devices):
    barrier = pltpu.get_barrier_semaphore()
    for device in devices:
        pl.semaphore_signal(barrier, inc=1, device_id=device, device_id_type=MESH)
    pl.semaphore_wait(barrier, len(devices))


def front_kernel(
    scale,
    atoms_ref,
    counts_ref,
    small_ref,
    query_w,
    key_w,
    value_w,
    all_ref,
    mask_ref,
    q_ref,
    qt_ref,
    k_ref,
    kt_ref,
    v_ref,
    vt_ref,
    qw,
    kw,
    vw,
    gathered,
    load_sem,
    send_sem,
    recv_sem,
):
    slots, rows, width = atoms_ref.shape
    full = mask_ref.shape[2]
    row, dp = lax.axis_index("rows"), lax.axis_index("dp")
    core, y = row % 2, row // 2
    beside, across = row + 1 - 2 * core, row + 2 - 4 * y
    loads = [
        pltpu.make_async_copy(hbm, vmem, load_sem.at[i])
        for i, (hbm, vmem) in enumerate(((query_w, qw), (key_w, kw), (value_w, vw)))
    ]
    for copy in loads:
        copy.start()
    meet([(dp, beside), (dp, across)])
    far = [
        remote(atoms_ref.at[s], gathered.at[row, s], send_sem.at[s], recv_sem.at[s], (dp, across))
        for s in range(slots)
    ]
    near = [
        remote(atoms_ref.at[s], gathered.at[row, s], send_sem.at[slots + s], recv_sem.at[slots + s], (dp, beside))
        for s in range(slots)
    ]
    gain, shift = small_ref[0:1, :], small_ref[1:2, :]
    for s in range(slots):
        gathered[row, s] = atoms_ref[s]
        ends = [counts_ref[s, 0]]
        for m in range(1, counts_ref.shape[1]):
            ends.append(ends[-1] + counts_ref[s, m])
        keys_at = lax.broadcasted_iota(jnp.int32, (rows, full), 1)
        queries_at = lax.broadcasted_iota(jnp.int32, (rows, full), 0) + row * rows
        count = lambda at: sum((end <= at).astype(jnp.int32) for end in ends)
        mask_ref[s] = jnp.where(count(keys_at) == count(queries_at), 0.0, -BIG)
    own = atoms_ref[...].reshape(slots * rows, width).astype(f32)
    normed = (standardize(own)[0] * gain + shift).astype(bf16)
    loads[0].wait()
    queries = ((matmul(normed, qw[...]) + small_ref[2:3, :]) * scale).astype(bf16)
    for s in range(slots):
        part = queries[rows * s : rows * (s + 1)]
        q_ref[s] = part
        qt_ref[s] = part.T
    loads[1].wait()
    loads[2].wait()
    forward = []
    for s in range(slots):
        far[s].wait()
        n = 2 * slots + s
        forward.append(
            remote(gathered.at[across, s], gathered.at[across, s], send_sem.at[n], recv_sem.at[n], (dp, beside))
        )
    for s in range(slots):
        near[s].wait()
        forward[s].wait()
        whole = jnp.concatenate([gathered[i, s] for i in range(full // rows)], axis=0)
        all_ref[s] = whole
        normed = (standardize(whole.astype(f32))[0] * gain + shift).astype(bf16)
        keys = matmul(normed, kw[...]).astype(bf16)
        k_ref[s] = keys
        kt_ref[s] = keys.T
        values = (matmul(normed, vw[...]) + small_ref[3:4, :]).astype(bf16)
        v_ref[s] = values
        vt_ref[s] = values.T


def front(scale, full, atoms, counts, small, query_w, key_w, value_w):
    slots, rows, width = atoms.shape
    vm = pl.BlockSpec(memory_space=pltpu.VMEM)
    hbm = pl.BlockSpec(memory_space=pl.ANY)
    like = lambda *shape: jax.ShapeDtypeStruct(shape, bf16)
    out_shape = [
        like(slots, full, width),
        jax.ShapeDtypeStruct((slots, rows, full), f32),
        like(slots, rows, width),
        like(slots, width, rows),
        like(slots, full, width),
        like(slots, width, full),
        like(slots, full, width),
        like(slots, width, full),
    ]
    return pl.pallas_call(
        functools.partial(front_kernel, scale),
        in_specs=[vm, pl.BlockSpec(memory_space=pltpu.SMEM), vm, hbm, hbm, hbm],
        out_specs=[vm] * len(out_shape),
        out_shape=out_shape,
        scratch_shapes=[pltpu.VMEM((width, width), bf16)] * 3
        + [
            pltpu.VMEM((full // rows, slots, rows, width), bf16),
            pltpu.SemaphoreType.DMA((3,)),
            pltpu.SemaphoreType.DMA((3 * slots,)),
            pltpu.SemaphoreType.DMA((3 * slots,)),
        ],
        name="front",
        cost_estimate=pl.CostEstimate(
            flops=4 * slots * full * width * width, transcendentals=0, bytes_accessed=8 << 20
        ),
        compiler_params=pltpu.CompilerParams(vmem_limit_bytes=32 << 20, collective_id=0, has_side_effects=True),
    )(atoms, counts, small, query_w, key_w, value_w)


def forward_kernel(q_ref, kt_ref, v_ref, bias_ref, mask_ref, out_ref, e_ref, mix_ref, rl_ref):
    _, heads, rows, full = bias_ref.shape
    lane_head = lax.broadcasted_iota(jnp.int32, (rows, 128), 1) // 8
    mask = mask_ref[0]
    ones = jnp.ones((full, 128), bf16)
    for b in range(heads // HPL):
        cols = slice(128 * b, 128 * b + 128)
        q = q_ref[0, :, cols].astype(f32)
        kt = kt_ref[0, cols, :]
        v = jnp.concatenate([v_ref[0, :, cols], ones], axis=1)
        mixed = jnp.zeros((rows, 128), f32)
        total = jnp.zeros((rows, 128), f32)
        for c in range(HPL // CHUNK):
            own = [lane_head == CHUNK * c + i for i in range(CHUNK)]
            left = jnp.concatenate([jnp.where(o, q, 0.0).astype(bf16) for o in own], axis=0)
            scores = matmul(left, kt).reshape(CHUNK, rows, full)
            hs = slice(HPL * b + CHUNK * c, HPL * b + CHUNK * (c + 1))
            scores = scores + bias_ref[0, hs].astype(f32)
            out_ref[0, hs] = scores.astype(bf16)
            scores = scores + mask[None]
            highest = jnp.max(scores, axis=-1, keepdims=True)
            e = jnp.exp(scores - highest).astype(bf16)
            e_ref[0, hs] = e
            sums = matmul(e.reshape(CHUNK * rows, full), v)
            for i, o in enumerate(own):
                mixed = jnp.where(o, sums[rows * i : rows * (i + 1), :128], mixed)
                total = jnp.where(o, sums[rows * i : rows * (i + 1), 128:], total)
        inverse = 1.0 / total
        mix_ref[0, :, cols] = mixed * inverse
        rl_ref[0, :, cols] = inverse


def attention_forward(q, kt, v, bias, mask):
    slots, heads, rows, full = bias.shape
    step = min(STEP, heads)
    width = step * 8
    natural = lambda n: pl.BlockSpec((1, n, width), lambda s, h: (s, 0, h))
    pair = pl.BlockSpec((1, step, rows, full), lambda s, h: (s, h, 0, 0))
    return pl.pallas_call(
        forward_kernel,
        grid=(slots, heads // step),
        in_specs=[
            natural(rows),
            pl.BlockSpec((1, width, full), lambda s, h: (s, h, 0)),
            natural(full),
            pair,
            pl.BlockSpec((1, rows, full), lambda s, h: (s, 0, 0)),
        ],
        out_specs=[pair, pair, natural(rows), natural(rows)],
        out_shape=[
            jax.ShapeDtypeStruct(bias.shape, bf16),
            jax.ShapeDtypeStruct(bias.shape, bf16),
            jax.ShapeDtypeStruct(q.shape, f32),
            jax.ShapeDtypeStruct(q.shape, f32),
        ],
        name="attention_forward",
        cost_estimate=pl.CostEstimate(
            flops=2 * bias.size * 512, transcendentals=bias.size, bytes_accessed=bias.size * 6
        ),
        compiler_params=pltpu.CompilerParams(vmem_limit_bytes=VMEM_PAIR),
    )(q, kt, v, bias, mask)


def backward_kernel(
    qt_ref, dm_ref, dmt_ref, nm_ref, k_ref, vt_ref, e_ref, cot_ref, pg_ref, dq_ref, dkt_ref, dvt_ref
):
    _, heads, rows, full = cot_ref.shape
    lane_head = lax.broadcasted_iota(jnp.int32, (rows, 128), 1) // 8
    shape = (8 * CHUNK, CHUNK * rows)
    same = lax.broadcasted_iota(jnp.int32, shape, 0) // 8 == lax.broadcasted_iota(jnp.int32, shape, 1) // rows
    ones = jnp.ones((128, full), bf16)
    for b in range(heads // HPL):
        cols = slice(128 * b, 128 * b + 128)
        dm = dm_ref[0, :, cols].astype(f32)
        nm = nm_ref[0, :, cols].astype(f32)
        vt = jnp.concatenate([vt_ref[0, cols, :], ones], axis=0)
        k = k_ref[0, :, cols]
        dq = jnp.zeros((rows, 128), f32)
        for c in range(HPL // CHUNK):
            own = [lane_head == CHUNK * c + i for i in range(CHUNK)]
            left = jnp.concatenate(
                [
                    jnp.concatenate([jnp.where(o, dm, 0.0), jnp.where(o, nm, 0.0)], axis=1).astype(bf16)
                    for o in own
                ],
                axis=0,
            )
            centred = matmul(left, vt).reshape(CHUNK, rows, full)
            hs = slice(HPL * b + CHUNK * c, HPL * b + CHUNK * (c + 1))
            e = e_ref[0, hs]
            grad = (e.astype(f32) * centred + cot_ref[0, hs].astype(f32)).astype(bf16)
            pg_ref[0, hs] = grad
            grad = grad.reshape(CHUNK * rows, full)
            sums = matmul(grad, k)
            for i, o in enumerate(own):
                dq = jnp.where(o, sums[rows * i : rows * (i + 1)], dq)
            rs = slice(hs.start * 8, hs.stop * 8)
            spread = lambda ref: jnp.where(
                same, jnp.concatenate([ref[0, rs, :].astype(f32)] * CHUNK, axis=1), 0.0
            ).astype(bf16)
            dkt_ref[0, rs, :] = matmul(spread(qt_ref), grad).astype(bf16)
            dvt_ref[0, rs, :] = matmul(spread(dmt_ref), e.reshape(CHUNK * rows, full)).astype(bf16)
        dq_ref[0, :, cols] = dq.astype(bf16)


def attention_backward(qt, dm, dmt, nm, k, vt, e, cot):
    slots, heads, rows, full = cot.shape
    step = min(STEP, heads)
    width = step * 8
    natural = lambda n: pl.BlockSpec((1, n, width), lambda s, h: (s, 0, h))
    turned = lambda n: pl.BlockSpec((1, width, n), lambda s, h: (s, h, 0))
    pair = pl.BlockSpec((1, step, rows, full), lambda s, h: (s, h, 0, 0))
    return pl.pallas_call(
        backward_kernel,
        grid=(slots, heads // step),
        in_specs=[
            turned(rows),
            natural(rows),
            turned(rows),
            natural(rows),
            natural(full),
            turned(full),
            pair,
            pair,
        ],
        out_specs=[pair, natural(rows), turned(full), turned(full)],
        out_shape=[
            jax.ShapeDtypeStruct(cot.shape, bf16),
            jax.ShapeDtypeStruct(dm.shape, bf16),
            jax.ShapeDtypeStruct(vt.shape, bf16),
            jax.ShapeDtypeStruct(vt.shape, bf16),
        ],
        name="attention_backward",
        cost_estimate=pl.CostEstimate(
            flops=2 * cot.size * 768, transcendentals=0, bytes_accessed=cot.size * 6
        ),
        compiler_params=pltpu.CompilerParams(vmem_limit_bytes=VMEM_PAIR),
    )(qt, dm, dmt, nm, k, vt, e, cot)


def middle_kernel(
    parts,
    mix_ref,
    rl_ref,
    atoms_ref,
    dy_ref,
    small_ref,
    bias_ref,
    out_w,
    inner_w,
    outer_w,
    out_ref,
    a_keep,
    a_send,
    b_keep,
    b_send,
    c_keep,
    c_send,
    dm_ref,
    nm_ref,
    dmt_ref,
    dmid_ref,
    vec_ref,
    ow,
    iw,
    uw,
    act,
    dpre,
    dpre_in,
    inner,
    mixed,
    branch,
    branch_in,
    dyh,
    dy_in,
    grads,
    load_sem,
    send_sem,
    recv_sem,
):
    here, width = atoms_ref.shape
    half = width // 2
    blocks = act.shape[1]
    slots, _, rows = dmt_ref.shape
    bits = parts.bit_length() - 1
    row = lax.axis_index("rows")
    dp = lax.axis_index("dp")
    core = row % 2
    y = row // 2
    sibling = (dp, row + 1 - 2 * core)

    loads = [
        pltpu.make_async_copy(hbm, vmem, load_sem.at[i])
        for i, (hbm, vmem) in enumerate(((out_w, ow), (inner_w, iw), (outer_w, uw)))
    ]
    for copy in loads:
        copy.start()
    barrier = pltpu.get_barrier_semaphore()
    pl.semaphore_signal(barrier, inc=1, device_id=sibling, device_id_type=pl.DeviceIdType.MESH)
    pl.semaphore_wait(barrier, 1)
    sent = []

    def send(source, target):
        n = len(sent)
        copy = pltpu.make_async_remote_copy(
            src_ref=source,
            dst_ref=target,
            send_sem=send_sem.at[n],
            recv_sem=recv_sem.at[n],
            device_id=sibling,
            device_id_type=pl.DeviceIdType.MESH,
        )
        copy.start()
        sent.append(copy)

    dy = dy_ref[...]
    dyh[0] = dy[:, :half]
    dyh[1] = dy[:, half:]
    send(dyh.at[1 - core], dy_in)
    mix = mix_ref[...]
    mixed[0] = mix.astype(bf16)
    send(mixed.at[0], mixed.at[1])
    loads[0].wait()
    middle = atoms_ref[...].astype(f32) + matmul(mixed[0], ow[...]) + small_ref[4:5, :]
    standard, inverse = standardize(middle)
    gain = small_ref[5:6, :]
    inner[0] = (standard * gain + small_ref[6:7, :]).astype(bf16)
    send(inner.at[0], inner.at[1])
    loads[1].wait()
    loads[2].wait()
    result = middle + small_ref[7:8, :]
    grad_inner = jnp.zeros((here, width), f32)
    for b in range(blocks):
        cols = slice(width * b, width * (b + 1))
        pre = matmul(inner[0], iw[:, cols]) + bias_ref[:, cols]
        cdf = 0.5 + 0.5 * lax.erf(pre * (0.5**0.5))
        low = (pre * cdf).astype(bf16)
        act[0, b] = low
        send(act.at[0, b], act.at[1, b])
        slope = cdf + pre * (jnp.exp(-0.5 * pre * pre) * 0.3989422804014327)
        grad = (times_transposed(dy, uw[cols, :]) * slope).astype(bf16)
        dpre[b] = grad
        result = result + matmul(low, uw[cols, :])
        grad_inner = grad_inner + times_transposed(grad, iw[:, cols])
        vec_ref[b : b + 1, :] = jnp.sum(grad.astype(f32), axis=0, keepdims=True)
    for i in range(blocks // 2):
        send(dpre.at[(blocks // 2) * (1 - core) + i], dpre_in.at[i])
    out_ref[...] = result.astype(bf16)
    dy_wide = dy.astype(f32)
    grad_middle = dy_wide + norm_back(grad_inner * gain, standard, inverse)
    dmid_ref[...] = grad_middle
    low = grad_middle.astype(bf16)
    branch[0] = low[:, :half]
    branch[1] = low[:, half:]
    send(branch.at[1 - core], branch_in)
    down = lambda value: jnp.sum(value, axis=0, keepdims=True)
    vec_ref[blocks : blocks + 1, :] = down(low.astype(f32))
    vec_ref[blocks + 1 : blocks + 2, :] = down(grad_inner * standard)
    vec_ref[blocks + 2 : blocks + 3, :] = down(grad_inner)
    vec_ref[blocks + 3 : blocks + 4, :] = down(dy_wide)
    scaled = times_transposed(low, ow[...]).astype(bf16).astype(f32) * rl_ref[...]
    nm_ref[...] = (-scaled * mix).astype(bf16)
    scaled = scaled.astype(bf16)
    dm_ref[...] = scaled
    for s in range(slots):
        dmt_ref[s] = scaled[rows * s : rows * (s + 1)].astype(f32).T.astype(bf16)

    for copy in sent:
        copy.wait()
    tall, short = blocks * width // parts, width // parts
    dy_own = dyh[core]
    for b in range(blocks):
        grads[width * b : width * (b + 1), :] = outer_sum(act[0, b], dy_own) + outer_sum(act[1, b], dy_in[...])
    base = blocks * width
    for i in range(blocks // 2):
        grad = outer_sum(inner[0], dpre[(blocks // 2) * core + i]) + outer_sum(inner[1], dpre_in[i])
        for k in range(2):
            grads[base + width * (2 * i + k) : base + width * (2 * i + k + 1), :] = grad[:, half * k : half * (k + 1)]
    last = base + width * blocks
    grads[last:, :] = outer_sum(mixed[0], branch[core]) + outer_sum(mixed[1], branch_in[...])

    def at(start, n, h):
        return grads[pl.ds(pl.multiple_of(start, 8), n), pl.ds(pl.multiple_of(h * 128, 128), 128)]

    rest = tall // 4
    long = tall - rest
    for p in range(parts):
        j = xor(dp, p, bits)
        for r in range(2):
            h = other_bit(y, 0, r)
            ref = a_send if p & 1 else a_keep
            ref[2 * (p >> 1) + r] = at(j * tall, long, h).astype(ref.dtype)
            ref = b_send if r else b_keep
            for k in range(blocks):
                ref[p, short * k : short * (k + 1)] = at(base + width * k + short * j, short, h).astype(ref.dtype)
            ref = c_send if p & 2 else c_keep
            q = 2 * ((p >> 2) * 2 + (p & 1)) + r
            ref[q, :rest] = at(j * tall + long, rest, h).astype(ref.dtype)
            ref[q, rest:] = at(last + short * j, short, h).astype(ref.dtype)


def middle(parts, mix, rl, atoms, dy, small, bias, out_w, inner_w, outer_w, slots):
    here, width = atoms.shape
    hidden = inner_w.shape[1]
    blocks, half, rows = hidden // width, width // 2, here // slots
    tall, short = hidden // parts, width // parts
    rest = tall // 4
    long = tall - rest
    assert hidden == 4 * width
    vm = pl.BlockSpec(memory_space=pltpu.VMEM)
    hbm = pl.BlockSpec(memory_space=pl.ANY)
    like = jax.ShapeDtypeStruct
    out_shape = [
        like((here, width), bf16),
        like((parts, long, 128), f32),
        like((parts, long, 128), bf16),
        like((parts, blocks * short, 128), f32),
        like((parts, blocks * short, 128), bf16),
        like((parts, rest + short, 128), f32),
        like((parts, rest + short, 128), bf16),
        like((here, width), bf16),
        like((here, width), bf16),
        like((slots, width, rows), bf16),
        like((here, width), f32),
        like((blocks + 4, width), f32),
    ]
    transfers = 3 + blocks + blocks // 2 + 1
    return pl.pallas_call(
        functools.partial(middle_kernel, parts),
        in_specs=[vm] * 6 + [hbm] * 3,
        out_specs=[vm] * len(out_shape),
        out_shape=out_shape,
        scratch_shapes=[
            pltpu.VMEM((width, width), bf16),
            pltpu.VMEM((width, hidden), bf16),
            pltpu.VMEM((hidden, width), bf16),
            pltpu.VMEM((2, blocks, here, width), bf16),
            pltpu.VMEM((blocks, here, width), bf16),
            pltpu.VMEM((blocks // 2, here, width), bf16),
            pltpu.VMEM((2, here, width), bf16),
            pltpu.VMEM((2, here, width), bf16),
            pltpu.VMEM((2, here, half), bf16),
            pltpu.VMEM((here, half), bf16),
            pltpu.VMEM((2, here, half), bf16),
            pltpu.VMEM((here, half), bf16),
            pltpu.VMEM((2 * hidden + width, half), f32),
            pltpu.SemaphoreType.DMA((3,)),
            pltpu.SemaphoreType.DMA((transfers,)),
            pltpu.SemaphoreType.DMA((transfers,)),
        ],
        name="middle",
        cost_estimate=pl.CostEstimate(
            flops=12 * here * width * hidden, transcendentals=2 * here * hidden, bytes_accessed=12 << 20
        ),
        compiler_params=pltpu.CompilerParams(
            vmem_limit_bytes=40 << 20, collective_id=1, has_side_effects=True
        ),
    )(mix, rl, atoms, dy, small, bias, out_w, inner_w, outer_w)


class Part:
    def __init__(self, names, order, rows, dtype=bf16):
        self.names, self.order, self.rows, self.dtype = names, order, rows, dtype
        self.steps, left = [], list(names)
        for name in order:
            others = [n for n in left if n != name]
            spots = []
            for q in range(1 << len(others)):
                base = sum(
                    self.stride(n) for i, n in enumerate(others) if (q >> (len(others) - 1 - i)) & 1
                )
                spots.append((base, base + self.stride(name)))
            self.steps.append((name, spots))
            left = others

    def stride(self, name):
        return 1 << (len(self.names) - 1 - self.names.index(name))

    def scratch(self):
        shapes = [pltpu.VMEM((1 << len(self.names), self.rows, 128), f32)]
        for _, spots in self.steps:
            shapes += [pltpu.VMEM((len(spots), self.rows, 128), self.dtype)] * 2
        shapes += [pltpu.VMEM((self.rows, 128), self.dtype)] * 2
        n = len(self.steps) + 1
        return shapes + [pltpu.SemaphoreType.DMA((n,)), pltpu.SemaphoreType.DMA((n,))]

    def bind(self, refs, partner):
        self.state, self.sends, self.recvs = refs[0], refs[1:-2:2], refs[2:-2:2]
        self.send_sem, self.recv_sem, self.partner = refs[-2], refs[-1], partner

    def go(self, n):
        name, spots = self.steps[n]
        for q, (_, far) in enumerate(spots):
            self.sends[n][q] = self.state[far].astype(self.dtype)
        self.copy = remote(
            self.sends[n], self.recvs[n], self.send_sem.at[n], self.recv_sem.at[n], self.partner(name)
        )

    def come(self, n):
        self.copy.wait()
        for q, (near, _) in enumerate(self.steps[n][1]):
            self.state[near] = self.state[near] + self.recvs[n][q].astype(f32)

    def share(self, total, core, y, row):
        n = len(self.steps)
        low = self.state[0].astype(self.dtype)
        self.sends[n][...] = low
        self.copy = remote(
            self.sends[n], self.recvs[n], self.send_sem.at[n], self.recv_sem.at[n], self.partner("y")
        )
        self.put(total, core, y, row, low)

    def shared(self, total, core, y, row):
        self.copy.wait()
        self.put(total, core, 1 - y, row, self.recvs[len(self.steps)][...])

    def put(self, total, core, y, row, value):
        total[core, row : row + self.rows, pl.ds(pl.multiple_of(y * 128, 128), 128)] = value.astype(f32)


def make_parts(parts, width, hidden):
    bits = ["d%d" % b for b in range(parts.bit_length() - 1)]
    high = bits[::-1]
    tall, short = hidden // parts, width // parts
    rest = tall // 4
    without = lambda name: [n for n in high if n != name]
    a = Part(without("d0") + ["y"], ["y", "d1"] + bits[2:], tall - rest)
    b = Part(high, ["d1", "d0"] + bits[2:], hidden // width * short)
    c = Part(without("d1") + ["y"], ["d0", "y"] + bits[2:], rest + short)
    q = Part(high + ["y"], ["d0", "y", "d1"] + bits[2:], short)
    k = Part(high + ["y"], ["y", "d1", "d0"] + bits[2:], short)
    v = Part(high + ["y"], ["d1", "d0", "y"] + bits[2:], short)
    s = Part(high + ["y"], ["d1", "d0", "y"] + bits[2:], 16, f32)
    return a, b, c, q, k, v, s


def tail_kernel(parts, scale, hidden, *refs):
    (
        dkt_in, dvt_in, dq_in, all_in, query_w, key_w, value_w, dmid_in, small_ref, vec_ref,
        a_keep, a_got, b_keep, b_got, c_keep, c_got, out_ref, total,
        dkt, dvt, dq, atoms, qw, kw, vw, dmid, ak, ag, bk, bg, ck, cg,
        dk_in, dv_in, dqh, dqh_in, vec_own, vec_in, standard, normed, partial, beside_send, beside_recv,
        across_send, across_recv, grads, vec_all, load_sem, send_sem, recv_sem,
    ) = refs[:50]
    slots, width, full = dkt.shape
    here = dq.shape[0]
    rows, half = here // slots, width // 2
    bits = parts.bit_length() - 1
    short, tall = width // parts, hidden // parts
    row, dp = lax.axis_index("rows"), lax.axis_index("dp")
    core, y = row % 2, row // 2
    beside, across = (dp, row + 1 - 2 * core), (dp, row + 2 - 4 * y)

    def partner(name):
        if name == "y":
            return across
        b = int(name[1:])
        return (xor(dp, 1 << b, bits), row)

    pieces = make_parts(parts, width, hidden)
    at = 50
    for piece in pieces:
        n = len(piece.scratch())
        piece.bind(refs[at : at + n], partner)
        at += n
    pa, pb, pc, pq, pk, pv, ps = pieces

    pairs = (
        (ak, a_keep), (ag, a_got), (bk, b_keep), (bg, b_got), (ck, c_keep), (cg, c_got), (dq, dq_in),
        (dkt, dkt_in), (dvt, dvt_in), (atoms, all_in), (kw, key_w), (vw, value_w), (qw, query_w), (dmid, dmid_in),
    )
    loads = {}
    for i, (vmem, hbm) in enumerate(pairs):
        loads[id(vmem)] = pltpu.make_async_copy(hbm, vmem, load_sem.at[i])
        loads[id(vmem)].start()
    ready = lambda *which: [loads[id(ref)].wait() for ref in which]
    meet([beside, across] + [partner("d%d" % b) for b in range(bits)])
    other = pl.ds(pl.multiple_of((1 - core) * half, half), half)
    mine = pl.ds(pl.multiple_of(core * half, half), half)
    ready(dkt, dvt, dq)
    to_sibling = [
        remote(dkt.at[:, other, :], dk_in, send_sem.at[0], recv_sem.at[0], beside),
        remote(dvt.at[:, other, :], dv_in, send_sem.at[1], recv_sem.at[1], beside),
    ]
    dq_low = dq[...]
    dqh[0] = dq_low[:, :half]
    dqh[1] = dq_low[:, half:]
    to_sibling.append(remote(dqh.at[1 - core], dqh_in, send_sem.at[2], recv_sem.at[2], beside))
    ready(ak, ag, bk, bg, ck, cg)
    for piece, keep, got in ((pa, ak, ag), (pb, bk, bg), (pc, ck, cg)):
        piece.state[...] = keep[...] + got[...].astype(f32)
        piece.go(0)

    gain, shift = small_ref[0:1, :], small_ref[1:2, :]
    down = lambda value: jnp.sum(value, axis=0, keepdims=True)
    ready(atoms, kw, vw)
    gain_grad = shift_grad = value_bias = 0.0
    send_on = []
    for s in range(slots):
        standard[s] = standardize(atoms[s].astype(f32))[0]
        normed[s] = (standard[s] * gain + shift).astype(bf16)
        dv = dvt[s].T
        grad = times_transposed(dkt[s].T, kw[...]) + times_transposed(dv, vw[...])
        value_bias = value_bias + down(dv.astype(f32))
        gain_grad = gain_grad + down(grad * standard[s])
        shift_grad = shift_grad + down(grad)
        for i in range(full // rows):
            to = xor(row, i, 2)
            partial[to, s] = grad[rows * i : rows * (i + 1)]
        beside_send[s, 0] = partial[1, s].astype(bf16)
        beside_send[s, 1] = partial[3, s].astype(bf16)
        send_on.append(remote(beside_send.at[s], beside_recv.at[s], send_sem.at[3 + s], recv_sem.at[3 + s], beside))
    ready(qw)
    own = pl.ds(pl.multiple_of(row * rows, rows), rows)
    next_to = pl.ds(pl.multiple_of((row + 1 - 2 * core) * rows, rows), rows)
    rows_of = lambda ref, which: jnp.concatenate([ref[s, which, :] for s in range(slots)], axis=0)
    standard_own = rows_of(standard, own)
    query_grad = times_transposed(dq_low, qw[...]) * scale
    vec_own[0:1, :] = gain_grad + down(query_grad * standard_own)
    vec_own[1:2, :] = shift_grad + down(query_grad)
    vec_own[2:3, :] = down(dq_low.astype(f32)) * scale
    vec_own[3:4, :] = value_bias
    vec_own[4:12, :] = vec_ref[...]
    vec_own[12:16, :] = jnp.zeros((4, width), f32)
    n = 3 + slots
    to_sibling.append(remote(vec_own, vec_in, send_sem.at[n], recv_sem.at[n], beside))

    for piece in (pa, pb, pc):
        piece.come(0)
        piece.go(1)

    for copy in to_sibling[:3]:
        copy.wait()
    grads[0] = (
        outer_sum(rows_of(normed, own), dqh[core]) + outer_sum(rows_of(normed, next_to), dqh_in[...])
    ) * scale
    key_total = value_total = 0.0
    add = lambda left, right: (left.astype(f32) + right.astype(f32)).astype(bf16)
    for s in range(slots):
        turned = normed[s].T
        key_total = key_total + times_transposed(turned, add(dkt[s, mine, :], dk_in[s]))
        value_total = value_total + times_transposed(turned, add(dvt[s, mine, :], dv_in[s]))
    grads[1] = key_total
    grads[2] = value_total
    to_sibling[3].wait()
    vec = vec_own[...] + vec_in[...]
    vec_all[...] = jnp.zeros_like(vec_all)
    for j in range(parts):
        vec_all[j, 0:4, :short] = vec[0:4, short * j : short * (j + 1)]
        vec_all[j, 4:8, :short] = vec[8:12, short * j : short * (j + 1)]
        start = tall * j
        vec_all[j, 8:9, :tall] = vec[4 + start // width : 5 + start // width, start % width : start % width + tall]
    for p in range(parts):
        j = xor(dp, p, bits)
        for r in range(2):
            lanes = pl.ds(pl.multiple_of(other_bit(y, 0, r) * 128, 128), 128)
            for i, piece in enumerate((pq, pk, pv)):
                piece.state[2 * p + r] = grads[i, pl.ds(pl.multiple_of(j * short, short), short), lanes]
            ps.state[2 * p + r] = vec_all[j, :, lanes]
    late = (pq, pk, pv, ps)
    for piece in late:
        piece.go(0)

    for s in range(slots):
        send_on[s].wait()
        across_send[s] = (partial[2, s] + beside_recv[s, 1].astype(f32)).astype(bf16)
    n = 4 + slots
    over = remote(across_send, across_recv, send_sem.at[n], recv_sem.at[n], across)

    steps = len(pa.steps)
    for piece in (pa, pb, pc):
        piece.come(1)
        piece.go(2)
    for piece in late:
        piece.come(0)
        piece.go(1)
    over.wait()
    ready(dmid)
    for s in range(slots):
        some = slice(rows * s, rows * (s + 1))
        grad = partial[0, s] + beside_recv[s, 0].astype(f32) + across_recv[s].astype(f32) + query_grad[some]
        stand, inverse = standardize(atoms[s, own, :].astype(f32))
        out_ref[some, :] = (dmid[some, :] + norm_back(grad * gain, stand, inverse)).astype(bf16)
    for n in range(2, steps):
        for piece in (pa, pb, pc):
            piece.come(n)
            if n + 1 < steps:
                piece.go(n + 1)
        for piece in late:
            piece.come(n - 1)
            piece.go(n)
    at = 0
    places = []
    for piece in (pa, pc, pb, pq, pk, pv, ps):
        places.append((piece, at))
        at += piece.rows
    for piece, at in places[:3]:
        piece.share(total, core, y, at)
    for n in range(steps - 1, len(pq.steps)):
        for piece in late:
            piece.come(n)
            if n + 1 < len(pq.steps):
                piece.go(n + 1)
    for piece, at in places[3:]:
        piece.share(total, core, y, at)
    for piece, at in places:
        piece.shared(total, core, y, at)
    n = 5 + slots
    remote(total.at[core], total.at[core], send_sem.at[n], recv_sem.at[n], beside).wait()


def tail(parts, scale, dkt, dvt, dq, all_atoms, query_w, key_w, value_w, dmid, small, vec, pieces):
    slots, width, full = dkt.shape
    here = dq.shape[0]
    hidden = width * 4
    rows, half = here // slots, width // 2
    vm = pl.BlockSpec(memory_space=pltpu.VMEM)
    hbm = pl.BlockSpec(memory_space=pl.ANY)
    kinds = make_parts(parts, width, hidden)
    count = sum(piece.rows for piece in kinds)
    same = lambda array: pltpu.VMEM(array.shape, array.dtype)
    loaded = [dkt, dvt, dq, all_atoms, query_w, key_w, value_w, dmid] + list(pieces)
    transfers = 6 + slots
    scratch = [same(array) for array in loaded] + [
        pltpu.VMEM((slots, half, full), bf16),
        pltpu.VMEM((slots, half, full), bf16),
        pltpu.VMEM((2, here, half), bf16),
        pltpu.VMEM((here, half), bf16),
        pltpu.VMEM((16, width), f32),
        pltpu.VMEM((16, width), f32),
        pltpu.VMEM((slots, full, width), f32),
        pltpu.VMEM((slots, full, width), bf16),
        pltpu.VMEM((4, slots, rows, width), f32),
        pltpu.VMEM((slots, 2, rows, width), bf16),
        pltpu.VMEM((slots, 2, rows, width), bf16),
        pltpu.VMEM((slots, rows, width), bf16),
        pltpu.VMEM((slots, rows, width), bf16),
        pltpu.VMEM((3, width, half), f32),
        pltpu.VMEM((parts, 16, half), f32),
        pltpu.SemaphoreType.DMA((len(loaded),)),
        pltpu.SemaphoreType.DMA((transfers,)),
        pltpu.SemaphoreType.DMA((transfers,)),
    ]
    for piece in kinds:
        scratch += piece.scratch()
    return pl.pallas_call(
        functools.partial(tail_kernel, parts, scale, hidden),
        in_specs=[hbm] * 8 + [vm, vm] + [hbm] * 6,
        out_specs=[vm, vm],
        out_shape=[
            jax.ShapeDtypeStruct((here, width), bf16),
            jax.ShapeDtypeStruct((2, count, half), f32),
        ],
        scratch_shapes=scratch,
        name="tail",
        cost_estimate=pl.CostEstimate(
            flops=10 * slots * full * width * width, transcendentals=0, bytes_accessed=12 << 20
        ),
        compiler_params=pltpu.CompilerParams(vmem_limit_bytes=48 << 20, collective_id=2, has_side_effects=True),
    )(dkt, dvt, dq, all_atoms, query_w, key_w, value_w, dmid, small, vec, *pieces)


def last_kernel(
    total, grad_ref, made_ref, grad_out, made_out, uw, ow, iw, qw, kw, vw, again, ashift, qb, vb, ob, fgain, fshift, ub, ib
):
    half = total.shape[2]
    grad_out[...] = grad_ref[...]
    made_out[...] = made_ref[...]
    short = ow.shape[0]
    at = 0
    for ref in (uw, ow):
        n = ref.shape[0]
        for c in range(2):
            ref[:, half * c : half * (c + 1)] = total[c, at : at + n, :]
        at += n
    blocks = iw.shape[1] // 2 // half
    for k in range(blocks):
        for c in range(2):
            n = c * blocks + k
            iw[:, half * n : half * (n + 1)] = total[c, at : at + short, :]
        at += short
    for ref in (qw, kw, vw):
        for c in range(2):
            ref[:, half * c : half * (c + 1)] = total[c, at : at + short, :]
        at += short
    vec = total[0, at : at + 16, :]
    for i, ref in enumerate((again, ashift, qb, vb, ob, fgain, fshift, ub)):
        ref[...] = vec[i : i + 1, :short]
    ib[...] = vec[8:9, : ib.shape[1]]


def last(parts, total, grad, made, hidden):
    here, width = grad.shape
    short, tall = width // parts, hidden // parts
    vm = pl.BlockSpec(memory_space=pltpu.VMEM)
    like = lambda *shape: jax.ShapeDtypeStruct(shape, f32)
    out_shape = [jax.ShapeDtypeStruct(grad.shape, bf16)] * 2
    out_shape += [like(tall, width), like(short, width), like(short, hidden)] + [like(short, width)] * 3
    out_shape += [like(1, short)] * 8 + [like(1, tall)]
    return pl.pallas_call(
        last_kernel,
        in_specs=[vm] * 3,
        out_specs=[vm] * len(out_shape),
        out_shape=out_shape,
        name="last",
        compiler_params=pltpu.CompilerParams(vmem_limit_bytes=16 << 20),
    )(total, grad, made)


def make_swap(parts, group):
    def swap(array, dp_bit=None, row_bit=None):
        pairs = []
        for d in range(parts):
            for r in range(group):
                e = d if dp_bit is None else d ^ (1 << dp_bit)
                t = r if row_bit is None else r ^ (1 << row_bit)
                pairs.append((d * group + r, e * group + t))
        return lax.ppermute(array, ("dp", "rows"), pairs)

    return swap


def local(
    parts,
    group,
    atoms,
    pair_bias,
    mol_counts,
    attn_gain,
    attn_shift,
    query_weight,
    query_bias,
    key_weight,
    value_weight,
    value_bias,
    out_weight,
    out_bias,
    ffn_gain,
    ffn_shift,
    inner_weight,
    inner_bias,
    outer_weight,
    outer_bias,
    atoms_cotangent,
    pair_cotangent,
):
    slots, part_rows, width = atoms.shape
    heads = pair_bias.shape[1]
    full = pair_bias.shape[3]
    scale = (width // heads) ** (-0.5)
    here = slots * part_rows
    hidden = inner_weight.shape[1]
    swap = make_swap(parts, group)
    flat = lambda array: array.reshape(here, width)
    small = jnp.stack(
        [attn_gain, attn_shift, query_bias, value_bias, out_bias, ffn_gain, ffn_shift, outer_bias]
    ).astype(f32)
    all_atoms, mask, q, qt, k, kt, v, vt = front(
        scale, full, atoms, mol_counts, small, query_weight, key_weight, value_weight
    )
    pair_out, weights, mixed, inverse_sum = attention_forward(q, kt, v, pair_bias, mask)
    atoms_out, a_keep, a_send, b_keep, b_send, c_keep, c_send, scaled, centre, scaled_turned, grad_middle, vec = middle(
        parts,
        flat(mixed),
        flat(inverse_sum),
        flat(atoms),
        flat(atoms_cotangent),
        small,
        inner_bias.astype(f32).reshape(1, hidden),
        out_weight,
        inner_weight,
        outer_weight,
        slots,
    )
    a_got, b_got, c_got = swap(a_send, dp_bit=0), swap(b_send, row_bit=1), swap(c_send, dp_bit=1)
    pair_grad, dq, dkt, dvt = attention_backward(
        qt, scaled.reshape(q.shape), scaled_turned, centre.reshape(q.shape), k, vt, weights, pair_cotangent
    )
    grad, total = tail(
        parts,
        scale,
        dkt,
        dvt,
        flat(dq),
        all_atoms,
        query_weight,
        key_weight,
        value_weight,
        grad_middle,
        small,
        vec,
        (a_keep, a_got, b_keep, b_got, c_keep, c_got),
    )
    grad, made, uw, ow, iw, qw, kw, vw, again, ashift, qb, vb, ob, fgain, fshift, ub, ib = last(
        parts, total, grad, atoms_out, hidden
    )
    line = lambda array: array.reshape(-1)
    return (
        made.reshape(atoms.shape),
        pair_out,
        grad.reshape(atoms.shape),
        pair_grad,
        line(again),
        line(ashift),
        qw,
        line(qb),
        kw,
        vw,
        line(vb),
        ow,
        line(ob),
        line(fgain),
        line(fshift),
        iw,
        line(ib),
        uw,
        line(ub),
    )


def solution(mesh):
    one, two = P("dp"), P("dp", None)
    atoms_spec, pair_spec = P("dp", "rows", None), P("dp", None, "rows", None)
    in_specs = (atoms_spec, pair_spec, two) + (P(),) * 15 + (atoms_spec, pair_spec)
    out_specs = (
        (atoms_spec, pair_spec, atoms_spec, pair_spec, one, one, two, one, two, two, one, two)
        + (one, one, one, two, one, two, one)
    )
    run = functools.partial(local, mesh.shape["dp"], mesh.shape["rows"])
    return jax.shard_map(run, mesh=mesh, in_specs=in_specs, out_specs=out_specs, check_vma=False)
```

time: 159 us -> 100 us (0.63)
  Pallas kernels: 31.4 us -> 72.8 us
  starting transfers between devices: 35.2 us -> 4.21 us
  other arithmetic: 26.7 us -> 0.7 us
  waiting for transfers between devices: 22.2 us -> 0.01 us
  local copies, waits for them, and re-layouts: 35.6 us -> 20.8 us
  matrix products: 4.89 us -> 0 us
    pallas_call x1 -> x3, Pallas kernels: 0.77 us -> 48.5 us  [the longest x1 35.4 us: tail(): pl.pallas_call(functools.partial(tail_kernel, parts, scale, hidden), in_s...]
    ppermute x34 -> x3, starting transfers between devices: 35.2 us -> 4.21 us  [swap(): return lax.ppermute(array, ('dp', 'rows'), pairs)]
    ppermute x34 -> x3, waiting for transfers between devices: 22.2 us -> 0.01 us  [swap(): return lax.ppermute(array, ('dp', 'rows'), pairs)]
    add x11 -> x0, other arithmetic: 6.44 us -> none  [the longest x6 3.99 us: stage(): keep.astype(f32) + partner(send, name).astype(f32)]
    convert_element_type x17 -> x1, other arithmetic: 5.93 us -> 0.01 us  [local(): small = jnp.stack([attn_gain, attn_shift, query_bias, value_bias, out_bia...]
    another operation x13 -> x0, other arithmetic: 4.91 us -> none  [the longest x3 2.15 us: local(): pair_of = lambda own, send: jnp.stack([own, swap(send, row_bit=0)])]
    dot_general x6 -> x0, matrix products: 4.89 us -> none  [the longest x3 3.32 us: matmul(): return jnp.dot(left, right, preferred_element_type=f32)]
    reduce_sum x10 -> x0, other arithmetic: 4.3 us -> none  [the longest x3 1.73 us: standardize(): jnp.mean(centred * centred, axis=-1, keepdims=True) + 1e-05]
  transfers between devices with their start and end apart: 34 -> 3, of which waited for: 13 -> 0; matrix products, arithmetic and copies ran while one was open for 22% -> 0% of each run, Pallas kernels for 0% -> 9%
where the time goes in v3:
time: 100 us; the launch traced here: 99.5 us
  Pallas kernels  72.8 us (73%)
  local copies, waits for them, and re-layouts  20.8 us (21%)
  starting transfers between devices  4.21 us (4%)
    pallas_call x1, Pallas kernels, tail(): pl.pallas_call(functools.partial(tail_kernel, parts, scale, hidden), in_s...  35.4 us
    unnamed x42, local copies, waits for them, and re-layouts  15.3 us
    pallas_call x1, Pallas kernels, front(): pl.pallas_call(functools.partial(front_kernel, scale), in_specs=[vm, pl.B...  11.6 us
    pallas_call x1, Pallas kernels, attention_backward(): pl.pallas_call(backward_kernel, grid=(slots, heads // step), in_specs=[tu...  9.35 us
    pallas_call x1, Pallas kernels, middle(): pl.pallas_call(functools.partial(middle_kernel, parts), in_specs=[vm] * 6...  7.85 us
    pallas_call x1, Pallas kernels, attention_forward(): pl.pallas_call(forward_kernel, grid=(slots, heads // step), in_specs=[nat...  7.14 us
    another operation x9, local copies, waits for them, and re-layouts, local(): jnp.stack([attn_gain, attn_shift, query_bias, value_bias, out_bias, ffn_g...  5.49 us
    ppermute x3, starting transfers between devices, swap(): return lax.ppermute(array, ('dp', 'rows'), pairs)  4.21 us
  transfers between devices with their start and end apart: 3, of which 0 were waited for; matrix products, arithmetic and copies ran while one was open for 0% of the time, Pallas kernels for 9%

profile of v3, /device:TPU:0, one launch (start us, length us, event | category | flops | bytes accessed | tf_op | source)
XLA Modules:
  0.0 99.5 jit_solution(15279210995031396617)
XLA Ops:
  0.7 0.7 stack.27
  1.3 0.7 stack.28
  2.0 0.7 stack.29
  2.7 0.7 stack.30
  3.4 0.7 stack.31
  4.1 0.7 stack.32
  4.7 0.7 stack.33
  5.4 0.7 stack.34
  6.2 0.7 reshape.117
  6.9 0.0 copy-start.4
  6.9 1.0 %copy-done.4 = bf16[512,512]{1,0:T(8,128)(2,1)S(1)} copy-done((bf16[512,512]{1,0:T(8,128)(2,1)S(1)}, bf16[512,512]{1,0:T(8,128)(2,1)}, u32[]{:S(2)}) %copy-start.4) | copy-done | bytes 524312
  7.9 0.0 copy-start.6
  7.9 1.0 %copy-done.6 = bf16[512,512]{1,0:T(8,128)(2,1)S(1)} copy-done((bf16[512,512]{1,0:T(8,128)(2,1)S(1)}, bf16[512,512]{1,0:T(8,128)(2,1)}, u32[]{:S(2)}) %copy-start.6) | copy-done | bytes 524312
  8.9 1.0 %copy-done.8 = bf16[512,512]{1,0:T(8,128)(2,1)S(1)} copy-done((bf16[512,512]{1,0:T(8,128)(2,1)S(1)}, bf16[512,512]{1,0:T(8,128)(2,1)}, u32[]{:S(2)}) %copy-start.8) | copy-done | bytes 524312
  10.0 0.9 copy-done.15
  10.9 0.7 copy-done.18
  11.6 11.6 %front.1 = (bf16[3,256,512]{2,1,0:T(8,128)(2,1)S(1)}, f32[3,64,256]{2,1,0:T(8,128)S(1)}, bf16[3,64,512]{2,1,0:T(8,128)(2,1)S(1)}, bf16[3,512,64]{2,1,0:T(8,128)(...) custom-call(bf16[3,64,512]{2,1,0:T(8,128)(2,1)S(1)} %copy-done.15, ...), custom_call_target="tpu_custom_call" | custom-call | flops 805306368 | bytes 8388608 | tf_op jit(solution)/shard_map/front/pallas_call | solution.py:169
  23.2 0.0 copy-start.2
  23.2 0.9 copy-done.2
  24.1 2.8 %copy-done.10 = bf16[3,64,64,256]{3,2,1,0:T(8,128)(2,1)S(1)} copy-done((bf16[3,64,64,256]{3,2,1,0:T(8,128)(2,1)S(1)}, bf16[3,64,64,256]{3,2,1,0:T(8,128)(2,1)}, u32[]{:S(2)}) %copy-start.10) | copy-done | bytes 6291480
  26.9 7.1 %attention_forward.1 = (bf16[3,64,64,256]{3,2,1,0:T(8,128)(2,1)}, bf16[3,64,64,256]{3,2,1,0:T(8,128)(2,1)S(1)}, f32[3,64,512]{2,1,0:T(8,128)S(1)}, f32[3,64,512]{2,1,0:T(8,128)S(1)}) custom-call(bf16[3,64,512]{2,1,0:T(8,128)(2,1)S(1)} %get-tuple-element.67.q_ref, bf16[3,512,256]{2,1,0:T(8,128)(2,1)S(1)} %get-tuple-element.68.kt_ref, ...), custom_call_target="tpu_custom_call" | custom-call | flops 3221225472 | bytes 18874368 | tf_op jit(solution)/shard_map/attention_forward/pallas_call | solution.py:227
  34.0 2.7 %copy-done.19 = bf16[3,64,64,256]{3,2,1,0:T(8,128)(2,1)} copy-done((bf16[3,64,64,256]{3,2,1,0:T(8,128)(2,1)}, bf16[3,64,64,256]{3,2,1,0:T(8,128)(2,1)S(1)}, u32[]{:S(2)}) %copy-start.19) | copy-done | bytes 6291480
  36.7 0.0 copy-done.12
  36.7 0.0 copy-done.14
  36.8 0.0 copy-done.16
  36.8 0.0 copy-done.13
  36.8 0.0 copy-done.17
  36.8 7.8 %middle.1 = (bf16[192,512]{1,0:T(8,128)(2,1)S(1)}, f32[8,192,128]{2,1,0:T(8,128)S(1)}, bf16[8,192,128]{2,1,0:T(8,128)(2,1)S(1)}, f32[8,256,128]{2,1,0:T(8,128)S(...) custom-call(f32[192,512]{1,0:T(8,128)S(1)} %bitcast.23, ...), custom_call_target="tpu_custom_call" | custom-call | flops 2415919104 | bytes 12582912 | tf_op jit(solution)/shard_map/middle/pallas_call | solution.py:516
  44.6 0.0 copy-start.1
  44.6 0.0 copy-start.3
  44.7 1.1 %collective-permute-start.1 = (bf16[8,256,128]{2,1,0:T(8,128)(2,1)S(1)}, bf16[8,256,128]{2,1,0:T(8,128)(2,1)S(1)}, u32[]{:S(2)}, u32[]{:S(2)}) collective-permute-start(bf16[8,256,128]{2,1,0:T(8,128)(2,1)S(1)} %get-tuple-element.88), channel_id=1, source_target_pairs={{0,2},{1,3},{2,0},{3,1},{4,6},{5,7},{6,4},{7,5},{8,10},{9,11},{10,... | collective-permute-start | bytes 1572872 | tf_op jit(solution)/shard_map/ppermute | solution.py:906
  45.8 1.6 %collective-permute-start.2 = (bf16[8,128,128]{2,1,0:T(8,128)(2,1)S(1)}, bf16[8,128,128]{2,1,0:T(8,128)(2,1)S(1)}, u32[]{:S(2)}, u32[]{:S(2)}) collective-permute-start(bf16[8,128,128]{2,1,0:T(8,128)(2,1)S(1)} %get-tuple-element.90), channel_id=1, source_target_pairs={{0,8},{1,9},{2,10},{3,11},{4,12},{5,13},{6,14},{7,15},{8,0},{9,1},... | collective-permute-start | bytes 786440 | tf_op jit(solution)/shard_map/ppermute | solution.py:906
  47.4 1.5 %collective-permute-start = (bf16[8,192,128]{2,1,0:T(8,128)(2,1)S(1)}, bf16[8,192,128]{2,1,0:T(8,128)(2,1)S(1)}, u32[]{:S(2)}, u32[]{:S(2)}) collective-permute-start(bf16[8,192,128]{2,1,0:T(8,128)(2,1)S(1)} %get-tuple-element.86), channel_id=1, source_target_pairs={{0,4},{1,5},{2,6},{3,7},{4,0},{5,1},{6,2},{7,3},{8,12},{9,13},{10,... | collective-permute-start | bytes 1179656 | tf_op jit(solution)/shard_map/ppermute | solution.py:906
  48.9 0.0 copy-done.11
  48.9 2.8 %copy-done.20 = bf16[3,64,64,256]{3,2,1,0:T(8,128)(2,1)S(1)} copy-done((bf16[3,64,64,256]{3,2,1,0:T(8,128)(2,1)S(1)}, bf16[3,64,64,256]{3,2,1,0:T(8,128)(2,1)}, u32[]{:S(2)}) %copy-start.20) | copy-done | bytes 6291480
  51.7 9.3 %attention_backward.1 = (bf16[3,64,64,256]{3,2,1,0:T(8,128)(2,1)}, bf16[3,64,512]{2,1,0:T(8,128)(2,1)S(1)}, bf16[3,512,256]{2,1,0:T(8,128)(2,1)S(1)}, bf16[3,512,256]{2,1,0:T(8,128)(2,1)S(1)}) custom-call(bf16[3,512,64]{2,1,0:T(8,128)(2,1)S(1)} %get-tuple-element.66.qt_ref, bf16[3,64,512]{2,1,0:T(8,128)(2,1)S(1)} %bitcast.25, ...), custom_call_target="tpu_custom_call" | custom-call | flops 4831838208 | bytes 18874368 | tf_op jit(solution)/shard_map/attention_backward/pallas_call | solution.py:301
  61.0 0.0 copy-done.1
  61.0 0.0 copy-done.3
  61.0 0.0 collective-permute-done.2.refs_15_
  61.0 0.0 collective-permute-done.refs_11_
  61.0 0.0 collective-permute-done.1.refs_13_
  61.0 0.0 copy-done.5
  61.0 0.0 copy-done.7
  61.1 0.0 copy-done.9
  61.1 35.4 %tail.1 = (bf16[192,512]{1,0:T(8,128)(2,1)S(1)}, f32[2,784,256]{2,1,0:T(8,128)}) custom-call(bf16[3,512,256]{2,1,0:T(8,128)(2,1)S(1)} %get-tuple-element.79.refs_0_, bf16[3,512,256]{2,1,0:T(8,128)(2,1)S(1)} %get-tuple-element.80.refs_1_, bf16[192,512]{1,0:T(8,128)(2,1)S(1)} %bitcast.19, bf16[3,256,512]{2,1,0:T(8,128)(2,1)} %copy-done.2, ...), custom_call_target="tpu_custom_call" | custom-call | flops 2013265920 | bytes 12582912 | tf_op jit(solution)/shard_map/tail/pallas_call | solution.py:834
  96.5 0.0 copy-start
  96.5 1.4 %copy-done = f32[2,784,256]{2,1,0:T(8,128)S(1)} copy-done((f32[2,784,256]{2,1,0:T(8,128)S(1)}, f32[2,784,256]{2,1,0:T(8,128)}, u32[]{:S(2)}) %copy-start) | copy-done | bytes 1605656
  97.9 1.4 %last.1 = (bf16[192,512]{1,0:T(8,128)(2,1)}, bf16[192,512]{1,0:T(8,128)(2,1)}, f32[256,512]{1,0:T(8,128)}, f32[64,512]{1,0:T(8,128)}, f32[64,2048]{1,0:T(8,128)}...) custom-call(f32[2,784,256]{2,1,0:T(8,128)S(1)} %copy-done, ...), custom_call_target="tpu_custom_call" | custom-call | tf_op jit(solution)/shard_map/last/pallas_call | solution.py:888
  (17 shorter events, 0.1 us)
Async XLA Ops:
  6.9 1.0 %copy-start.4 = (bf16[512,512]{1,0:T(8,128)(2,1)S(1)}, bf16[512,512]{1,0:T(8,128)(2,1)}, u32[]{:S(2)}) copy-start(bf16[512,512]{1,0:T(8,128)(2,1)} %refs_4_.1) | copy-start | bytes 1572868
  7.9 1.0 %copy-start.6 = (bf16[512,512]{1,0:T(8,128)(2,1)S(1)}, bf16[512,512]{1,0:T(8,128)(2,1)}, u32[]{:S(2)}) copy-start(bf16[512,512]{1,0:T(8,128)(2,1)} %refs_5_.1) | copy-start | bytes 1572868
  8.9 1.0 %copy-start.8 = (bf16[512,512]{1,0:T(8,128)(2,1)S(1)}, bf16[512,512]{1,0:T(8,128)(2,1)}, u32[]{:S(2)}) copy-start(bf16[512,512]{1,0:T(8,128)(2,1)} %refs_6_.1) | copy-start | bytes 1572868
  10.0 0.9 copy-start.15
  10.9 0.7 copy-start.18
  11.6 25.2 %copy-start.12 = (bf16[512,2048]{1,0:T(8,128)(2,1)S(1)}, bf16[512,2048]{1,0:T(8,128)(2,1)}, u32[]{:S(2)}) copy-start(bf16[512,2048]{1,0:T(8,128)(2,1)} %inner_w.1) | copy-start | bytes 6291460
  11.6 25.2 %copy-start.14 = (bf16[512,512]{1,0:T(8,128)(2,1)S(1)}, bf16[512,512]{1,0:T(8,128)(2,1)}, u32[]{:S(2)}) copy-start(bf16[512,512]{1,0:T(8,128)(2,1)} %out_w.1) | copy-start | bytes 1572868
  11.6 25.2 %copy-start.16 = (bf16[3,64,512]{2,1,0:T(8,128)(2,1)S(1)}, bf16[3,64,512]{2,1,0:T(8,128)(2,1)}, u32[]{:S(2)}) copy-start(bf16[3,64,512]{2,1,0:T(8,128)(2,1)} %atoms_ref.1) | copy-start | bytes 589828
  23.2 0.9 copy-start.2
  24.1 2.8 %copy-start.10 = (bf16[3,64,64,256]{3,2,1,0:T(8,128)(2,1)S(1)}, bf16[3,64,64,256]{3,2,1,0:T(8,128)(2,1)}, u32[]{:S(2)}) copy-start(bf16[3,64,64,256]{3,2,1,0:T(8,128)(2,1)} %bias_ref.1) | copy-start | bytes 18874372
  26.9 9.9 %copy-start.13 = (bf16[2048,512]{1,0:T(8,128)(2,1)S(1)}, bf16[2048,512]{1,0:T(8,128)(2,1)}, u32[]{:S(2)}) copy-start(bf16[2048,512]{1,0:T(8,128)(2,1)} %outer_w.1) | copy-start | bytes 6291460
  26.9 9.9 %copy-start.17 = (bf16[3,64,512]{2,1,0:T(8,128)(2,1)S(1)}, bf16[3,64,512]{2,1,0:T(8,128)(2,1)}, u32[]{:S(2)}) copy-start(bf16[3,64,512]{2,1,0:T(8,128)(2,1)} %param.38) | copy-start | bytes 589828
  34.0 2.7 %copy-start.19 = (bf16[3,64,64,256]{3,2,1,0:T(8,128)(2,1)}, bf16[3,64,64,256]{3,2,1,0:T(8,128)(2,1)S(1)}, u32[]{:S(2)}) copy-start(bf16[3,64,64,256]{3,2,1,0:T(8,128)(2,1)S(1)} %get-tuple-element.78.e_ref) | copy-start | bytes 18874372
  36.7 12.1 %copy-start.11 = (bf16[3,64,64,256]{3,2,1,0:T(8,128)(2,1)S(1)}, bf16[3,64,64,256]{3,2,1,0:T(8,128)(2,1)}, u32[]{:S(2)}) copy-start(bf16[3,64,64,256]{3,2,1,0:T(8,128)(2,1)} %cot_ref.1) | copy-start | bytes 18874372
  44.6 16.4 %copy-start.1 = (f32[8,256,128]{2,1,0:T(8,128)}, f32[8,256,128]{2,1,0:T(8,128)S(1)}, u32[]{:S(2)}) copy-start(f32[8,256,128]{2,1,0:T(8,128)S(1)} %get-tuple-element.87.refs_12_) | copy-start | bytes 3145732
  44.6 16.4 %copy-start.3 = (f32[8,192,128]{2,1,0:T(8,128)}, f32[8,192,128]{2,1,0:T(8,128)S(1)}, u32[]{:S(2)}) copy-start(f32[8,192,128]{2,1,0:T(8,128)S(1)} %get-tuple-element.85.refs_10_) | copy-start | bytes 2359300
  44.7 16.4 %collective-permute-start.1 = (bf16[8,256,128]{2,1,0:T(8,128)(2,1)S(1)}, bf16[8,256,128]{2,1,0:T(8,128)(2,1)S(1)}, u32[]{:S(2)}, u32[]{:S(2)}) collective-permute-start(bf16[8,256,128]{2,1,0:T(8,128)(2,1)S(1)} %get-tuple-element.88), channel_id=1, source_target_pairs={{0,2},{1,3},{2,0},{3,1},{4,6},{5,7},{6,4},{7,5},{8,10},{9,11},{10,... | collective-permute-start | bytes 1572872 | tf_op jit(solution)/shard_map/ppermute | solution.py:906
  45.8 15.2 %collective-permute-start.2 = (bf16[8,128,128]{2,1,0:T(8,128)(2,1)S(1)}, bf16[8,128,128]{2,1,0:T(8,128)(2,1)S(1)}, u32[]{:S(2)}, u32[]{:S(2)}) collective-permute-start(bf16[8,128,128]{2,1,0:T(8,128)(2,1)S(1)} %get-tuple-element.90), channel_id=1, source_target_pairs={{0,8},{1,9},{2,10},{3,11},{4,12},{5,13},{6,14},{7,15},{8,0},{9,1},... | collective-permute-start | bytes 786440 | tf_op jit(solution)/shard_map/ppermute | solution.py:906
  47.4 13.6 %collective-permute-start = (bf16[8,192,128]{2,1,0:T(8,128)(2,1)S(1)}, bf16[8,192,128]{2,1,0:T(8,128)(2,1)S(1)}, u32[]{:S(2)}, u32[]{:S(2)}) collective-permute-start(bf16[8,192,128]{2,1,0:T(8,128)(2,1)S(1)} %get-tuple-element.86), channel_id=1, source_target_pairs={{0,4},{1,5},{2,6},{3,7},{4,0},{5,1},{6,2},{7,3},{8,12},{9,13},{10,... | collective-permute-start | bytes 1179656 | tf_op jit(solution)/shard_map/ppermute | solution.py:906
  48.9 2.8 %copy-start.20 = (bf16[3,64,64,256]{3,2,1,0:T(8,128)(2,1)S(1)}, bf16[3,64,64,256]{3,2,1,0:T(8,128)(2,1)}, u32[]{:S(2)}) copy-start(bf16[3,64,64,256]{3,2,1,0:T(8,128)(2,1)} %copy-done.19) | copy-start | bytes 18874372
  51.7 9.4 %copy-start.5 = (bf16[512,512]{1,0:T(8,128)(2,1)S(1)}, bf16[512,512]{1,0:T(8,128)(2,1)}, u32[]{:S(2)}) copy-start(bf16[512,512]{1,0:T(8,128)(2,1)} %refs_4_.1) | copy-start | bytes 1572868
  51.7 9.4 %copy-start.7 = (bf16[512,512]{1,0:T(8,128)(2,1)S(1)}, bf16[512,512]{1,0:T(8,128)(2,1)}, u32[]{:S(2)}) copy-start(bf16[512,512]{1,0:T(8,128)(2,1)} %refs_5_.1) | copy-start | bytes 1572868
  51.7 9.4 %copy-start.9 = (bf16[512,512]{1,0:T(8,128)(2,1)S(1)}, bf16[512,512]{1,0:T(8,128)(2,1)}, u32[]{:S(2)}) copy-start(bf16[512,512]{1,0:T(8,128)(2,1)} %refs_6_.1) | copy-start | bytes 1572868
  96.5 1.4 %copy-start = (f32[2,784,256]{2,1,0:T(8,128)S(1)}, f32[2,784,256]{2,1,0:T(8,128)}, u32[]{:S(2)}) copy-start(f32[2,784,256]{2,1,0:T(8,128)} %get-tuple-element.91.total) | copy-start | bytes 4816900

commit v4 on v3

--- a/solution.py
+++ b/solution.py
@@ -12,7 +12,7 @@
 HPL = 16
 CHUNK = 8
 STEP = 32
-VMEM_PAIR = 24 << 20
+VMEM_PAIR = 16 << 20
 MESH = pl.DeviceIdType.MESH
 
 
@@ -66,11 +66,18 @@
     pl.semaphore_wait(barrier, len(devices))
 
 
+def wide(ref):
+    return ref[...].astype(f32).reshape(1, -1)
+
+
 def front_kernel(
     scale,
     atoms_ref,
     counts_ref,
-    small_ref,
+    gain_ref,
+    shift_ref,
+    query_b,
+    value_b,
     query_w,
     key_w,
     value_w,
@@ -85,7 +92,6 @@
     qw,
     kw,
     vw,
-    gathered,
     load_sem,
     send_sem,
     recv_sem,
@@ -102,59 +108,67 @@
     for copy in loads:
         copy.start()
     meet([(dp, beside), (dp, across)])
-    far = [
-        remote(atoms_ref.at[s], gathered.at[row, s], send_sem.at[s], recv_sem.at[s], (dp, across))
+    at = lambda r: pl.ds(pl.multiple_of(r * rows, rows), rows)
+    here = lambda s: all_ref.at[s, at(row), :]
+    there = lambda s: all_ref.at[s, at(across), :]
+    far = [remote(atoms_ref.at[s], here(s), send_sem.at[s], recv_sem.at[s], (dp, across)) for s in range(slots)]
+    near = [
+        remote(atoms_ref.at[s], here(s), send_sem.at[slots + s], recv_sem.at[slots + s], (dp, beside))
         for s in range(slots)
     ]
-    near = [
-        remote(atoms_ref.at[s], gathered.at[row, s], send_sem.at[slots + s], recv_sem.at[slots + s], (dp, beside))
-        for s in range(slots)
-    ]
-    gain, shift = small_ref[0:1, :], small_ref[1:2, :]
+    gain, shift = wide(gain_ref), wide(shift_ref)
+    bias = wide(value_b)
     for s in range(slots):
-        gathered[row, s] = atoms_ref[s]
-        ends = [counts_ref[s, 0]]
-        for m in range(1, counts_ref.shape[1]):
-            ends.append(ends[-1] + counts_ref[s, m])
-        keys_at = lax.broadcasted_iota(jnp.int32, (rows, full), 1)
-        queries_at = lax.broadcasted_iota(jnp.int32, (rows, full), 0) + row * rows
-        count = lambda at: sum((end <= at).astype(jnp.int32) for end in ends)
-        mask_ref[s] = jnp.where(count(keys_at) == count(queries_at), 0.0, -BIG)
+        all_ref[s, at(row), :] = atoms_ref[s]
     own = atoms_ref[...].reshape(slots * rows, width).astype(f32)
     normed = (standardize(own)[0] * gain + shift).astype(bf16)
     loads[0].wait()
-    queries = ((matmul(normed, qw[...]) + small_ref[2:3, :]) * scale).astype(bf16)
+    queries = ((matmul(normed, qw[...]) + wide(query_b)) * scale).astype(bf16)
     for s in range(slots):
         part = queries[rows * s : rows * (s + 1)]
         q_ref[s] = part
         qt_ref[s] = part.T
     loads[1].wait()
     loads[2].wait()
+
+    def project(s, chip):
+        some = pl.ds(pl.multiple_of(chip * 2 * rows, 2 * rows), 2 * rows)
+        normed = (standardize(all_ref[s, some, :].astype(f32))[0] * gain + shift).astype(bf16)
+        keys = matmul(normed, kw[...]).astype(bf16)
+        k_ref[s, some, :] = keys
+        kt_ref[s, :, some] = keys.T
+        values = (matmul(normed, vw[...]) + bias).astype(bf16)
+        v_ref[s, some, :] = values
+        vt_ref[s, :, some] = values.T
+
+    def masks(s):
+        ends = [counts_ref[s, 0]]
+        for m in range(1, counts_ref.shape[1]):
+            ends.append(ends[-1] + counts_ref[s, m])
+        keys_at = lax.broadcasted_iota(jnp.int32, (1, full), 1)
+        queries_at = lax.broadcasted_iota(jnp.int32, (rows, 1), 0) + row * rows
+        count = lambda at: sum((end <= at).astype(jnp.int32) for end in ends)
+        mask_ref[s] = jnp.where(count(keys_at) == count(queries_at), 0.0, -BIG)
+
     forward = []
     for s in range(slots):
+        near[s].wait()
+        project(s, y)
         far[s].wait()
         n = 2 * slots + s
-        forward.append(
-            remote(gathered.at[across, s], gathered.at[across, s], send_sem.at[n], recv_sem.at[n], (dp, beside))
-        )
-    for s in range(slots):
-        near[s].wait()
-        forward[s].wait()
-        whole = jnp.concatenate([gathered[i, s] for i in range(full // rows)], axis=0)
-        all_ref[s] = whole
-        normed = (standardize(whole.astype(f32))[0] * gain + shift).astype(bf16)
-        keys = matmul(normed, kw[...]).astype(bf16)
-        k_ref[s] = keys
-        kt_ref[s] = keys.T
-        values = (matmul(normed, vw[...]) + small_ref[3:4, :]).astype(bf16)
-        v_ref[s] = values
-        vt_ref[s] = values.T
-
-
-def front(scale, full, atoms, counts, small, query_w, key_w, value_w):
+        forward.append(remote(there(s), there(s), send_sem.at[n], recv_sem.at[n], (dp, beside)))
+        masks(s)
+        if s:
+            forward[s - 1].wait()
+            project(s - 1, 1 - y)
+    forward[-1].wait()
+    project(slots - 1, 1 - y)
+
+
+def front(scale, full, atoms, counts, vectors, query_w, key_w, value_w):
     slots, rows, width = atoms.shape
     vm = pl.BlockSpec(memory_space=pltpu.VMEM)
-    hbm = pl.BlockSpec(memory_space=pl.ANY)
+    hbm = pl.BlockSpec(memory_space=pltpu.HBM)
     like = lambda *shape: jax.ShapeDtypeStruct(shape, bf16)
     out_shape = [
         like(slots, full, width),
@@ -168,22 +182,21 @@
     ]
     return pl.pallas_call(
         functools.partial(front_kernel, scale),
-        in_specs=[vm, pl.BlockSpec(memory_space=pltpu.SMEM), vm, hbm, hbm, hbm],
+        in_specs=[vm, pl.BlockSpec(memory_space=pltpu.SMEM)] + [vm] * 4 + [hbm] * 3,
         out_specs=[vm] * len(out_shape),
         out_shape=out_shape,
         scratch_shapes=[pltpu.VMEM((width, width), bf16)] * 3
         + [
-            pltpu.VMEM((full // rows, slots, rows, width), bf16),
             pltpu.SemaphoreType.DMA((3,)),
             pltpu.SemaphoreType.DMA((3 * slots,)),
             pltpu.SemaphoreType.DMA((3 * slots,)),
         ],
         name="front",
         cost_estimate=pl.CostEstimate(
-            flops=4 * slots * full * width * width, transcendentals=0, bytes_accessed=8 << 20
+            flops=48 * slots * full * width * width, transcendentals=0, bytes_accessed=32 << 20
         ),
-        compiler_params=pltpu.CompilerParams(vmem_limit_bytes=32 << 20, collective_id=0, has_side_effects=True),
-    )(atoms, counts, small, query_w, key_w, value_w)
+        compiler_params=pltpu.CompilerParams(vmem_limit_bytes=18 << 20, collective_id=0, has_side_effects=True),
+    )(*(pltpu.with_memory_space_constraint(array, pltpu.HBM) for array in (atoms, counts, *vectors, query_w, key_w, value_w)))
 
 
 def forward_kernel(q_ref, kt_ref, v_ref, bias_ref, mask_ref, out_ref, e_ref, mix_ref, rl_ref):
@@ -332,7 +345,10 @@
     rl_ref,
     atoms_ref,
     dy_ref,
-    small_ref,
+    out_b,
+    gain_ref,
+    shift_ref,
+    outer_b,
     bias_ref,
     out_w,
     inner_w,
@@ -409,18 +425,19 @@
     mixed[0] = mix.astype(bf16)
     send(mixed.at[0], mixed.at[1])
     loads[0].wait()
-    middle = atoms_ref[...].astype(f32) + matmul(mixed[0], ow[...]) + small_ref[4:5, :]
+    middle = atoms_ref[...].astype(f32) + matmul(mixed[0], ow[...]) + wide(out_b)
     standard, inverse = standardize(middle)
-    gain = small_ref[5:6, :]
-    inner[0] = (standard * gain + small_ref[6:7, :]).astype(bf16)
+    gain = wide(gain_ref)
+    inner[0] = (standard * gain + wide(shift_ref)).astype(bf16)
     send(inner.at[0], inner.at[1])
     loads[1].wait()
     loads[2].wait()
-    result = middle + small_ref[7:8, :]
+    result = middle + wide(outer_b)
+    bias = wide(bias_ref)
     grad_inner = jnp.zeros((here, width), f32)
     for b in range(blocks):
         cols = slice(width * b, width * (b + 1))
-        pre = matmul(inner[0], iw[:, cols]) + bias_ref[:, cols]
+        pre = matmul(inner[0], iw[:, cols]) + bias[:, cols]
         cdf = 0.5 + 0.5 * lax.erf(pre * (0.5**0.5))
         low = (pre * cdf).astype(bf16)
         act[0, b] = low
@@ -487,7 +504,7 @@
             ref[q, rest:] = at(last + short * j, short, h).astype(ref.dtype)
 
 
-def middle(parts, mix, rl, atoms, dy, small, bias, out_w, inner_w, outer_w, slots):
+def middle(parts, mix, rl, atoms, dy, vectors, out_w, inner_w, outer_w, slots):
     here, width = atoms.shape
     hidden = inner_w.shape[1]
     blocks, half, rows = hidden // width, width // 2, here // slots
@@ -496,7 +513,7 @@
     long = tall - rest
     assert hidden == 4 * width
     vm = pl.BlockSpec(memory_space=pltpu.VMEM)
-    hbm = pl.BlockSpec(memory_space=pl.ANY)
+    hbm = pl.BlockSpec(memory_space=pltpu.HBM)
     like = jax.ShapeDtypeStruct
     out_shape = [
         like((here, width), bf16),
@@ -515,7 +532,7 @@
     transfers = 3 + blocks + blocks // 2 + 1
     return pl.pallas_call(
         functools.partial(middle_kernel, parts),
-        in_specs=[vm] * 6 + [hbm] * 3,
+        in_specs=[vm] * 9 + [hbm] * 3,
         out_specs=[vm] * len(out_shape),
         out_shape=out_shape,
         scratch_shapes=[
@@ -541,9 +558,9 @@
             flops=12 * here * width * hidden, transcendentals=2 * here * hidden, bytes_accessed=12 << 20
         ),
         compiler_params=pltpu.CompilerParams(
-            vmem_limit_bytes=40 << 20, collective_id=1, has_side_effects=True
+            vmem_limit_bytes=20 << 20, collective_id=1, has_side_effects=True
         ),
-    )(mix, rl, atoms, dy, small, bias, out_w, inner_w, outer_w)
+    )(mix, rl, atoms, dy, *vectors, out_w, inner_w, outer_w)
 
 
 class Part:
@@ -624,12 +641,12 @@
 
 def tail_kernel(parts, scale, hidden, *refs):
     (
-        dkt_in, dvt_in, dq_in, all_in, query_w, key_w, value_w, dmid_in, small_ref, vec_ref,
+        dkt_in, dvt_in, dq_in, all_in, query_w, key_w, value_w, dmid_in, gain_ref, shift_ref, vec_ref,
         a_keep, a_got, b_keep, b_got, c_keep, c_got, out_ref, total,
         dkt, dvt, dq, atoms, qw, kw, vw, dmid, ak, ag, bk, bg, ck, cg,
         dk_in, dv_in, dqh, dqh_in, vec_own, vec_in, standard, normed, partial, beside_send, beside_recv,
         across_send, across_recv, grads, vec_all, load_sem, send_sem, recv_sem,
-    ) = refs[:50]
+    ) = refs[:51]
     slots, width, full = dkt.shape
     here = dq.shape[0]
     rows, half = here // slots, width // 2
@@ -646,7 +663,7 @@
         return (xor(dp, 1 << b, bits), row)
 
     pieces = make_parts(parts, width, hidden)
-    at = 50
+    at = 51
     for piece in pieces:
         n = len(piece.scratch())
         piece.bind(refs[at : at + n], partner)
@@ -679,7 +696,7 @@
         piece.state[...] = keep[...] + got[...].astype(f32)
         piece.go(0)
 
-    gain, shift = small_ref[0:1, :], small_ref[1:2, :]
+    gain, shift = wide(gain_ref), wide(shift_ref)
     down = lambda value: jnp.sum(value, axis=0, keepdims=True)
     ready(atoms, kw, vw)
     gain_grad = shift_grad = value_bias = 0.0
@@ -797,13 +814,14 @@
     remote(total.at[core], total.at[core], send_sem.at[n], recv_sem.at[n], beside).wait()
 
 
-def tail(parts, scale, dkt, dvt, dq, all_atoms, query_w, key_w, value_w, dmid, small, vec, pieces):
+def tail(parts, scale, dkt, dvt, dq, all_atoms, query_w, key_w, value_w, dmid, vectors, vec, pieces):
     slots, width, full = dkt.shape
     here = dq.shape[0]
     hidden = width * 4
     rows, half = here // slots, width // 2
     vm = pl.BlockSpec(memory_space=pltpu.VMEM)
     hbm = pl.BlockSpec(memory_space=pl.ANY)
+    far = pl.BlockSpec(memory_space=pltpu.HBM)
     kinds = make_parts(parts, width, hidden)
     count = sum(piece.rows for piece in kinds)
     same = lambda array: pltpu.VMEM(array.shape, array.dtype)
@@ -833,7 +851,7 @@
         scratch += piece.scratch()
     return pl.pallas_call(
         functools.partial(tail_kernel, parts, scale, hidden),
-        in_specs=[hbm] * 8 + [vm, vm] + [hbm] * 6,
+        in_specs=[hbm] * 4 + [far] * 3 + [hbm] + [vm] * 3 + [hbm] * 6,
         out_specs=[vm, vm],
         out_shape=[
             jax.ShapeDtypeStruct((here, width), bf16),
@@ -844,8 +862,8 @@
         cost_estimate=pl.CostEstimate(
             flops=10 * slots * full * width * width, transcendentals=0, bytes_accessed=12 << 20
         ),
-        compiler_params=pltpu.CompilerParams(vmem_limit_bytes=48 << 20, collective_id=2, has_side_effects=True),
-    )(dkt, dvt, dq, all_atoms, query_w, key_w, value_w, dmid, small, vec, *pieces)
+        compiler_params=pltpu.CompilerParams(vmem_limit_bytes=26 << 20, collective_id=2, has_side_effects=True),
+    )(dkt, dvt, dq, all_atoms, query_w, key_w, value_w, dmid, *vectors, vec, *pieces)
 
 
 def last_kernel(
@@ -940,11 +958,8 @@
     hidden = inner_weight.shape[1]
     swap = make_swap(parts, group)
     flat = lambda array: array.reshape(here, width)
-    small = jnp.stack(
-        [attn_gain, attn_shift, query_bias, value_bias, out_bias, ffn_gain, ffn_shift, outer_bias]
-    ).astype(f32)
     all_atoms, mask, q, qt, k, kt, v, vt = front(
-        scale, full, atoms, mol_counts, small, query_weight, key_weight, value_weight
+        scale, full, atoms, mol_counts, (attn_gain, attn_shift, query_bias, value_bias), query_weight, key_weight, value_weight
     )
     pair_out, weights, mixed, inverse_sum = attention_forward(q, kt, v, pair_bias, mask)
     atoms_out, a_keep, a_send, b_keep, b_send, c_keep, c_send, scaled, centre, scaled_turned, grad_middle, vec = middle(
@@ -953,8 +968,7 @@
         flat(inverse_sum),
         flat(atoms),
         flat(atoms_cotangent),
-        small,
-        inner_bias.astype(f32).reshape(1, hidden),
+        (out_bias, ffn_gain, ffn_shift, outer_bias, inner_bias),
         out_weight,
         inner_weight,
         outer_weight,
@@ -975,7 +989,7 @@
         key_weight,
         value_weight,
         grad_middle,
-        small,
+        (attn_gain, attn_shift),
         vec,
         (a_keep, a_got, b_keep, b_got, c_keep, c_got),
     )

time: 100 us -> 79.5 us (0.80)
  local copies, waits for them, and re-layouts: 20.8 us -> 0.11 us
    unnamed x42 -> x36, local copies, waits for them, and re-layouts: 15.3 us -> 0.11 us
    another operation x9 -> x0, local copies, waits for them, and re-layouts: 5.49 us -> none  [local(): jnp.stack([attn_gain, attn_shift, query_bias, value_bias, out_bias, ffn_g...]
  transfers between devices with their start and end apart: 3 -> 3, of which waited for: 0 -> 0; matrix products, arithmetic and copies ran while one was open for 0% -> 0% of each run, Pallas kernels for 9% -> 12%
where the time goes in v4:
time: 79.5 us; the launch traced here: 79.3 us
  Pallas kernels  73.4 us (92%)
  starting transfers between devices  4.73 us (6%)
  between operations  1.07 us (1%)
    pallas_call x1, Pallas kernels, tail(): pl.pallas_call(functools.partial(tail_kernel, parts, scale, hidden), in_s...  35.9 us
    pallas_call x1, Pallas kernels, front(): pl.pallas_call(functools.partial(front_kernel, scale), in_specs=[vm, pl.B...  11.4 us
    pallas_call x1, Pallas kernels, attention_backward(): pl.pallas_call(backward_kernel, grid=(slots, heads // step), in_specs=[tu...  9.43 us
    pallas_call x1, Pallas kernels, middle(): pl.pallas_call(functools.partial(middle_kernel, parts), in_specs=[vm] * 9...  7.89 us
    pallas_call x1, Pallas kernels, attention_forward(): pl.pallas_call(forward_kernel, grid=(slots, heads // step), in_specs=[nat...  7.34 us
    ppermute x3, starting transfers between devices, swap(): return lax.ppermute(array, ('dp', 'rows'), pairs)  4.73 us
  transfers between devices with their start and end apart: 3, of which 0 were waited for; matrix products, arithmetic and copies ran while one was open for 0% of the time, Pallas kernels for 12%

profile of v4, /device:TPU:0, one launch (start us, length us, event | category | flops | bytes accessed | tf_op | source)
XLA Modules:
  0.0 79.3 jit_solution(10514130196905102246)
XLA Ops:
  0.7 0.0 copy-start.5
  0.7 11.4 %front.1 = (bf16[3,256,512]{2,1,0:T(8,128)(2,1)S(1)}, f32[3,64,256]{2,1,0:T(8,128)S(1)}, bf16[3,64,512]{2,1,0:T(8,128)(2,1)S(1)}, bf16[3,512,64]{2,1,0:T(8,128)(...) custom-call(bf16[3,64,512]{2,1,0:T(8,128)(2,1)} %atoms_ref.1, ...), custom_call_target="tpu_custom_call" | custom-call | flops 9663676416 | bytes 33554432 | tf_op jit(solution)/shard_map/front/pallas_call | solution.py:183
  12.0 0.0 copy-start.6
  12.1 0.0 copy-start.7
  12.1 0.0 copy-start.8
  12.1 0.0 copy-start.9
  12.1 0.0 copy-start.10
  12.1 0.0 copy-start.11
  12.1 0.0 copy-start.12
  12.1 0.0 copy-start.13
  12.1 0.0 copy-start.14
  12.2 0.0 copy-start.15
  12.2 0.0 slice-start
  12.2 0.0 copy-done.5
  12.2 0.0 slice-start.1
  12.2 7.3 %attention_forward.1 = (bf16[3,64,64,256]{3,2,1,0:T(8,128)(2,1)}, bf16[3,64,64,256]{3,2,1,0:T(8,128)(2,1)S(1)}, f32[3,64,512]{2,1,0:T(8,128)S(1)}, f32[3,64,512]{2,1,0:T(8,128)S(1)}) custom-call(bf16[3,64,512]{2,1,0:T(8,128)(2,1)S(1)} %get-tuple-element.67.q_ref, bf16[3,512,256]{2,1,0:T(8,128)(2,1)S(1)} %get-tuple-element.68.kt_ref, ...), custom_call_target="tpu_custom_call" | custom-call | flops 3221225472 | bytes 18874368 | tf_op jit(solution)/shard_map/attention_forward/pallas_call | solution.py:240
  19.5 0.0 copy-done.6
  19.5 0.0 copy-done.7
  19.6 0.0 copy-done.8
  19.6 0.0 copy-done.9
  19.6 0.0 copy-done.10
  19.6 0.0 copy-done.11
  19.6 0.0 copy-done.12
  19.6 0.0 copy-done.13
  19.6 0.0 copy-done.14
  19.6 0.0 copy-done.15
  19.6 7.9 %middle.1 = (bf16[192,512]{1,0:T(8,128)(2,1)S(1)}, f32[8,192,128]{2,1,0:T(8,128)S(1)}, bf16[8,192,128]{2,1,0:T(8,128)(2,1)S(1)}, f32[8,256,128]{2,1,0:T(8,128)S(...) custom-call(f32[192,512]{1,0:T(8,128)S(1)} %bitcast.23, ...), custom_call_target="tpu_custom_call" | custom-call | flops 2415919104 | bytes 12582912 | tf_op jit(solution)/shard_map/middle/pallas_call | solution.py:533
  27.5 1.6 %collective-permute-start.1 = (bf16[8,256,128]{2,1,0:T(8,128)(2,1)S(1)}, bf16[8,256,128]{2,1,0:T(8,128)(2,1)S(1)}, u32[]{:S(2)}, u32[]{:S(2)}) collective-permute-start(bf16[8,256,128]{2,1,0:T(8,128)(2,1)S(1)} %get-tuple-element.88), channel_id=1, source_target_pairs={{0,2},{1,3},{2,0},{3,1},{4,6},{5,7},{6,4},{7,5},{8,10},{9,11},{10,... | collective-permute-start | bytes 1572872 | tf_op jit(solution)/shard_map/ppermute | solution.py:924
  29.2 1.6 %collective-permute-start.2 = (bf16[8,128,128]{2,1,0:T(8,128)(2,1)S(1)}, bf16[8,128,128]{2,1,0:T(8,128)(2,1)S(1)}, u32[]{:S(2)}, u32[]{:S(2)}) collective-permute-start(bf16[8,128,128]{2,1,0:T(8,128)(2,1)S(1)} %get-tuple-element.90), channel_id=1, source_target_pairs={{0,8},{1,9},{2,10},{3,11},{4,12},{5,13},{6,14},{7,15},{8,0},{9,1},... | collective-permute-start | bytes 786440 | tf_op jit(solution)/shard_map/ppermute | solution.py:924
  30.8 1.5 %collective-permute-start = (bf16[8,192,128]{2,1,0:T(8,128)(2,1)S(1)}, bf16[8,192,128]{2,1,0:T(8,128)(2,1)S(1)}, u32[]{:S(2)}, u32[]{:S(2)}) collective-permute-start(bf16[8,192,128]{2,1,0:T(8,128)(2,1)S(1)} %get-tuple-element.86), channel_id=1, source_target_pairs={{0,4},{1,5},{2,6},{3,7},{4,0},{5,1},{6,2},{7,3},{8,12},{9,13},{10,... | collective-permute-start | bytes 1179656 | tf_op jit(solution)/shard_map/ppermute | solution.py:924
  32.2 0.0 slice-done
  32.3 0.0 slice-done.1
  32.3 0.0 copy-start
  32.3 0.0 copy-start.1
  32.3 0.0 copy-start.2
  32.3 0.0 copy-start.3
  32.3 0.0 copy-start.4
  32.3 9.4 %attention_backward.1 = (bf16[3,64,64,256]{3,2,1,0:T(8,128)(2,1)}, bf16[3,64,512]{2,1,0:T(8,128)(2,1)S(1)}, bf16[3,512,256]{2,1,0:T(8,128)(2,1)S(1)}, bf16[3,512,256]{2,1,0:T(8,128)(2,1)S(1)}) custom-call(bf16[3,512,64]{2,1,0:T(8,128)(2,1)S(1)} %get-tuple-element.66.qt_ref, bf16[3,64,512]{2,1,0:T(8,128)(2,1)S(1)} %bitcast.25, ...), custom_call_target="tpu_custom_call" | custom-call | flops 4831838208 | bytes 18874368 | tf_op jit(solution)/shard_map/attention_backward/pallas_call | solution.py:314
  41.7 0.0 collective-permute-done.2.refs_16_
  41.7 0.0 collective-permute-done.refs_12_
  41.7 0.0 collective-permute-done.1.refs_14_
  41.8 0.0 copy-done
  41.8 0.0 copy-done.1
  41.8 0.0 copy-done.2
  41.8 0.0 copy-done.3
  41.8 0.0 copy-done.4
  41.8 35.9 %tail.1 = (bf16[192,512]{1,0:T(8,128)(2,1)S(1)}, f32[2,784,256]{2,1,0:T(8,128)S(1)}) custom-call(bf16[3,512,256]{2,1,0:T(8,128)(2,1)S(1)} %get-tuple-element.79.refs_0_, bf16[3,512,256]{2,1,0:T(8,128)(2,1)S(1)} %get-tuple-element.80.refs_1_, bf16[192,512]{1,0:T(8,128)(2,1)S(1)} %bitcast.18, bf16[3,256,512]{2,1,0:T(8,128)(2,1)S(1)} %get-tuple-element.82.refs_3_, ...), custom_call_target="tpu_custom_call" | custom-call | flops 2013265920 | bytes 12582912 | tf_op jit(solution)/shard_map/tail/pallas_call | solution.py:852
  77.7 1.4 %last.1 = (bf16[192,512]{1,0:T(8,128)(2,1)}, bf16[192,512]{1,0:T(8,128)(2,1)}, f32[256,512]{1,0:T(8,128)}, f32[64,512]{1,0:T(8,128)}, f32[64,2048]{1,0:T(8,128)}...) custom-call(f32[2,784,256]{2,1,0:T(8,128)S(1)} %get-tuple-element.91, ...), custom_call_target="tpu_custom_call" | custom-call | tf_op jit(solution)/shard_map/last/pallas_call | solution.py:906
  (1 shorter events, 0.0 us)
Async XLA Ops:
  0.7 11.5 %copy-start.5 = (bf16[3,64,64,256]{3,2,1,0:T(8,128)(2,1)S(1)}, bf16[3,64,64,256]{3,2,1,0:T(8,128)(2,1)}, u32[]{:S(2)}) copy-start(bf16[3,64,64,256]{3,2,1,0:T(8,128)(2,1)} %bias_ref.2) | copy-start | bytes 18874372
  12.0 7.5 %copy-start.6 = (bf16[512,2048]{1,0:T(8,128)(2,1)S(1)}, bf16[512,2048]{1,0:T(8,128)(2,1)}, u32[]{:S(2)}) copy-start(bf16[512,2048]{1,0:T(8,128)(2,1)} %inner_w.1) | copy-start | bytes 6291460
  12.1 7.5 %copy-start.7 = (bf16[2048,512]{1,0:T(8,128)(2,1)S(1)}, bf16[2048,512]{1,0:T(8,128)(2,1)}, u32[]{:S(2)}) copy-start(bf16[2048,512]{1,0:T(8,128)(2,1)} %outer_w.1) | copy-start | bytes 6291460
  12.1 7.5 %copy-start.8 = (bf16[512,512]{1,0:T(8,128)(2,1)S(1)}, bf16[512,512]{1,0:T(8,128)(2,1)}, u32[]{:S(2)}) copy-start(bf16[512,512]{1,0:T(8,128)(2,1)} %out_w.1) | copy-start | bytes 1572868
  12.1 7.5 %copy-start.9 = (bf16[3,64,512]{2,1,0:T(8,128)(2,1)S(1)}, bf16[3,64,512]{2,1,0:T(8,128)(2,1)}, u32[]{:S(2)}) copy-start(bf16[3,64,512]{2,1,0:T(8,128)(2,1)} %atoms_ref.1) | copy-start | bytes 589828
  12.1 7.5 %copy-start.10 = (bf16[3,64,512]{2,1,0:T(8,128)(2,1)S(1)}, bf16[3,64,512]{2,1,0:T(8,128)(2,1)}, u32[]{:S(2)}) copy-start(bf16[3,64,512]{2,1,0:T(8,128)(2,1)} %param.38) | copy-start | bytes 589828
  12.1 7.5 %copy-start.11 = (bf16[2048]{0:T(1024)(128)(2,1)S(1)}, bf16[2048]{0:T(1024)(128)(2,1)}, u32[]{:S(2)}) copy-start(bf16[2048]{0:T(1024)(128)(2,1)} %bias_ref.3) | copy-start | bytes 12292
  12.1 7.5 %copy-start.12 = (bf16[512]{0:T(512)(128)(2,1)S(1)}, bf16[512]{0:T(512)(128)(2,1)}, u32[]{:S(2)}) copy-start(bf16[512]{0:T(512)(128)(2,1)} %out_b.1) | copy-start | bytes 3076
  12.1 7.5 %copy-start.13 = (bf16[512]{0:T(512)(128)(2,1)S(1)}, bf16[512]{0:T(512)(128)(2,1)}, u32[]{:S(2)}) copy-start(bf16[512]{0:T(512)(128)(2,1)} %gain_ref.3) | copy-start | bytes 3076
  12.1 7.5 %copy-start.14 = (bf16[512]{0:T(512)(128)(2,1)S(1)}, bf16[512]{0:T(512)(128)(2,1)}, u32[]{:S(2)}) copy-start(bf16[512]{0:T(512)(128)(2,1)} %shift_ref.3) | copy-start | bytes 3076
  12.2 7.5 %copy-start.15 = (bf16[512]{0:T(512)(128)(2,1)S(1)}, bf16[512]{0:T(512)(128)(2,1)}, u32[]{:S(2)}) copy-start(bf16[512]{0:T(512)(128)(2,1)} %outer_b.1) | copy-start | bytes 3076
  12.2 20.1 %slice-start = ((s8[6291456]{0:T(1024)(128)(4,1)}), s8[4194304]{0:T(1024)(128)(4,1)S(1)}, s32[]{:S(2)}) async-start(s8[6291456]{0:T(1024)(128)(4,1)} %bitcast.19), calls=%async_computation | async-start | bytes 8388608
  12.2 20.1 %slice-start.1 = ((s8[6291456]{0:T(1024)(128)(4,1)}), s8[2097152]{0:T(1024)(128)(4,1)S(1)}, s32[]{:S(2)}) async-start(s8[6291456]{0:T(1024)(128)(4,1)} %bitcast.19), calls=%async_computation.1 | async-start | bytes 4194304
  27.5 14.2 %collective-permute-start.1 = (bf16[8,256,128]{2,1,0:T(8,128)(2,1)S(1)}, bf16[8,256,128]{2,1,0:T(8,128)(2,1)S(1)}, u32[]{:S(2)}, u32[]{:S(2)}) collective-permute-start(bf16[8,256,128]{2,1,0:T(8,128)(2,1)S(1)} %get-tuple-element.88), channel_id=1, source_target_pairs={{0,2},{1,3},{2,0},{3,1},{4,6},{5,7},{6,4},{7,5},{8,10},{9,11},{10,... | collective-permute-start | bytes 1572872 | tf_op jit(solution)/shard_map/ppermute | solution.py:924
  29.2 12.6 %collective-permute-start.2 = (bf16[8,128,128]{2,1,0:T(8,128)(2,1)S(1)}, bf16[8,128,128]{2,1,0:T(8,128)(2,1)S(1)}, u32[]{:S(2)}, u32[]{:S(2)}) collective-permute-start(bf16[8,128,128]{2,1,0:T(8,128)(2,1)S(1)} %get-tuple-element.90), channel_id=1, source_target_pairs={{0,8},{1,9},{2,10},{3,11},{4,12},{5,13},{6,14},{7,15},{8,0},{9,1},... | collective-permute-start | bytes 786440 | tf_op jit(solution)/shard_map/ppermute | solution.py:924
  30.8 11.0 %collective-permute-start = (bf16[8,192,128]{2,1,0:T(8,128)(2,1)S(1)}, bf16[8,192,128]{2,1,0:T(8,128)(2,1)S(1)}, u32[]{:S(2)}, u32[]{:S(2)}) collective-permute-start(bf16[8,192,128]{2,1,0:T(8,128)(2,1)S(1)} %get-tuple-element.86), channel_id=1, source_target_pairs={{0,4},{1,5},{2,6},{3,7},{4,0},{5,1},{6,2},{7,3},{8,12},{9,13},{10,... | collective-permute-start | bytes 1179656 | tf_op jit(solution)/shard_map/ppermute | solution.py:924
  32.3 9.5 %copy-start = (bf16[512,512]{1,0:T(8,128)(2,1)S(1)}, bf16[512,512]{1,0:T(8,128)(2,1)}, u32[]{:S(2)}) copy-start(bf16[512,512]{1,0:T(8,128)(2,1)} %refs_4_.1) | copy-start | bytes 1572868
  32.3 9.5 %copy-start.1 = (bf16[512,512]{1,0:T(8,128)(2,1)S(1)}, bf16[512,512]{1,0:T(8,128)(2,1)}, u32[]{:S(2)}) copy-start(bf16[512,512]{1,0:T(8,128)(2,1)} %refs_5_.1) | copy-start | bytes 1572868
  32.3 9.5 %copy-start.2 = (bf16[512,512]{1,0:T(8,128)(2,1)S(1)}, bf16[512,512]{1,0:T(8,128)(2,1)}, u32[]{:S(2)}) copy-start(bf16[512,512]{1,0:T(8,128)(2,1)} %refs_6_.1) | copy-start | bytes 1572868
  32.3 9.5 %copy-start.3 = (bf16[512]{0:T(512)(128)(2,1)S(1)}, bf16[512]{0:T(512)(128)(2,1)}, u32[]{:S(2)}) copy-start(bf16[512]{0:T(512)(128)(2,1)} %refs_8_.1) | copy-start | bytes 3076
  32.3 9.5 %copy-start.4 = (bf16[512]{0:T(512)(128)(2,1)S(1)}, bf16[512]{0:T(512)(128)(2,1)}, u32[]{:S(2)}) copy-start(bf16[512]{0:T(512)(128)(2,1)} %refs_9_.1) | copy-start | bytes 3076

commit v5 on v4

--- a/solution.py
+++ b/solution.py
@@ -13,7 +13,16 @@
 CHUNK = 8
 STEP = 32
 VMEM_PAIR = 16 << 20
+VMEM_BACK = 26 << 20
 MESH = pl.DeviceIdType.MESH
+PIECES = (
+    ("d0", (("outer", 0), ("outer", 1))),
+    ("y", (("outer", 2),)),
+    ("d1", (("outer", 3),)),
+    ("d0", (("inner", 0),)),
+    ("y", (("inner", 1), ("inner", 2))),
+    ("d1", (("inner", 3), ("out", 0))),
+)
 
 
 def standardize(value):
@@ -262,81 +271,43 @@
     )(q, kt, v, bias, mask)
 
 
-def backward_kernel(
-    qt_ref, dm_ref, dmt_ref, nm_ref, k_ref, vt_ref, e_ref, cot_ref, pg_ref, dq_ref, dkt_ref, dvt_ref
-):
+def attention_backward(s, b, qt_ref, dm_ref, dmt_ref, nm_ref, k_ref, vt_ref, e_ref, cot_ref, pg_ref, dq_ref, dkt_ref, dvt_ref):
     _, heads, rows, full = cot_ref.shape
     lane_head = lax.broadcasted_iota(jnp.int32, (rows, 128), 1) // 8
     shape = (8 * CHUNK, CHUNK * rows)
     same = lax.broadcasted_iota(jnp.int32, shape, 0) // 8 == lax.broadcasted_iota(jnp.int32, shape, 1) // rows
     ones = jnp.ones((128, full), bf16)
-    for b in range(heads // HPL):
-        cols = slice(128 * b, 128 * b + 128)
-        dm = dm_ref[0, :, cols].astype(f32)
-        nm = nm_ref[0, :, cols].astype(f32)
-        vt = jnp.concatenate([vt_ref[0, cols, :], ones], axis=0)
-        k = k_ref[0, :, cols]
-        dq = jnp.zeros((rows, 128), f32)
-        for c in range(HPL // CHUNK):
-            own = [lane_head == CHUNK * c + i for i in range(CHUNK)]
-            left = jnp.concatenate(
-                [
-                    jnp.concatenate([jnp.where(o, dm, 0.0), jnp.where(o, nm, 0.0)], axis=1).astype(bf16)
-                    for o in own
-                ],
-                axis=0,
-            )
-            centred = matmul(left, vt).reshape(CHUNK, rows, full)
-            hs = slice(HPL * b + CHUNK * c, HPL * b + CHUNK * (c + 1))
-            e = e_ref[0, hs]
-            grad = (e.astype(f32) * centred + cot_ref[0, hs].astype(f32)).astype(bf16)
-            pg_ref[0, hs] = grad
-            grad = grad.reshape(CHUNK * rows, full)
-            sums = matmul(grad, k)
-            for i, o in enumerate(own):
-                dq = jnp.where(o, sums[rows * i : rows * (i + 1)], dq)
-            rs = slice(hs.start * 8, hs.stop * 8)
-            spread = lambda ref: jnp.where(
-                same, jnp.concatenate([ref[0, rs, :].astype(f32)] * CHUNK, axis=1), 0.0
-            ).astype(bf16)
-            dkt_ref[0, rs, :] = matmul(spread(qt_ref), grad).astype(bf16)
-            dvt_ref[0, rs, :] = matmul(spread(dmt_ref), e.reshape(CHUNK * rows, full)).astype(bf16)
-        dq_ref[0, :, cols] = dq.astype(bf16)
-
-
-def attention_backward(qt, dm, dmt, nm, k, vt, e, cot):
-    slots, heads, rows, full = cot.shape
-    step = min(STEP, heads)
-    width = step * 8
-    natural = lambda n: pl.BlockSpec((1, n, width), lambda s, h: (s, 0, h))
-    turned = lambda n: pl.BlockSpec((1, width, n), lambda s, h: (s, h, 0))
-    pair = pl.BlockSpec((1, step, rows, full), lambda s, h: (s, h, 0, 0))
-    return pl.pallas_call(
-        backward_kernel,
-        grid=(slots, heads // step),
-        in_specs=[
-            turned(rows),
-            natural(rows),
-            turned(rows),
-            natural(rows),
-            natural(full),
-            turned(full),
-            pair,
-            pair,
-        ],
-        out_specs=[pair, natural(rows), turned(full), turned(full)],
-        out_shape=[
-            jax.ShapeDtypeStruct(cot.shape, bf16),
-            jax.ShapeDtypeStruct(dm.shape, bf16),
-            jax.ShapeDtypeStruct(vt.shape, bf16),
-            jax.ShapeDtypeStruct(vt.shape, bf16),
-        ],
-        name="attention_backward",
-        cost_estimate=pl.CostEstimate(
-            flops=2 * cot.size * 768, transcendentals=0, bytes_accessed=cot.size * 6
-        ),
-        compiler_params=pltpu.CompilerParams(vmem_limit_bytes=VMEM_PAIR),
-    )(qt, dm, dmt, nm, k, vt, e, cot)
+    cols = pl.ds(pl.multiple_of(128 * b, 128), 128)
+    dm = dm_ref[s, :, cols].astype(f32)
+    nm = nm_ref[s, :, cols].astype(f32)
+    vt = jnp.concatenate([vt_ref[s, cols, :], ones], axis=0)
+    k = k_ref[s, :, cols]
+    dq = jnp.zeros((rows, 128), f32)
+    for c in range(HPL // CHUNK):
+        own = [lane_head == CHUNK * c + i for i in range(CHUNK)]
+        left = jnp.concatenate(
+            [
+                jnp.concatenate([jnp.where(o, dm, 0.0), jnp.where(o, nm, 0.0)], axis=1).astype(bf16)
+                for o in own
+            ],
+            axis=0,
+        )
+        centred = matmul(left, vt).reshape(CHUNK, rows, full)
+        hs = pl.ds(HPL * b + CHUNK * c, CHUNK)
+        e = e_ref[s, hs]
+        grad = (e.astype(f32) * centred + cot_ref[s, hs].astype(f32)).astype(bf16)
+        pg_ref[s, hs] = grad
+        grad = grad.reshape(CHUNK * rows, full)
+        sums = matmul(grad, k)
+        for i, o in enumerate(own):
+            dq = jnp.where(o, sums[rows * i : rows * (i + 1)], dq)
+        rs = pl.ds(pl.multiple_of(128 * b + 8 * CHUNK * c, 8 * CHUNK), 8 * CHUNK)
+        spread = lambda ref: jnp.where(
+            same, jnp.concatenate([ref[s, rs, :].astype(f32)] * CHUNK, axis=1), 0.0
+        ).astype(bf16)
+        dkt_ref[s, rs, :] = matmul(spread(qt_ref), grad).astype(bf16)
+        dvt_ref[s, rs, :] = matmul(spread(dmt_ref), e.reshape(CHUNK * rows, full)).astype(bf16)
+    dq_ref[s, :, cols] = dq.astype(bf16)
 
 
 def middle_kernel(
@@ -354,12 +325,10 @@
     inner_w,
     outer_w,
     out_ref,
-    a_keep,
-    a_send,
-    b_keep,
-    b_send,
-    c_keep,
-    c_send,
+    *refs,
+):
+    pieces, refs = refs[: 2 * len(PIECES)], refs[2 * len(PIECES) :]
+    (
     dm_ref,
     nm_ref,
     dmt_ref,
@@ -381,7 +350,7 @@
     load_sem,
     send_sem,
     recv_sem,
-):
+    ) = refs
     here, width = atoms_ref.shape
     half = width // 2
     blocks = act.shape[1]
@@ -487,21 +456,23 @@
     def at(start, n, h):
         return grads[pl.ds(pl.multiple_of(start, 8), n), pl.ds(pl.multiple_of(h * 128, 128), 128)]
 
-    rest = tall // 4
-    long = tall - rest
+    start = {"outer": (0, tall), "inner": (base, short), "out": (last, short)}
+    step = {"outer": short, "inner": width, "out": 0}
     for p in range(parts):
         j = xor(dp, p, bits)
         for r in range(2):
             h = other_bit(y, 0, r)
-            ref = a_send if p & 1 else a_keep
-            ref[2 * (p >> 1) + r] = at(j * tall, long, h).astype(ref.dtype)
-            ref = b_send if r else b_keep
-            for k in range(blocks):
-                ref[p, short * k : short * (k + 1)] = at(base + width * k + short * j, short, h).astype(ref.dtype)
-            ref = c_send if p & 2 else c_keep
-            q = 2 * ((p >> 2) * 2 + (p & 1)) + r
-            ref[q, :rest] = at(j * tall + long, rest, h).astype(ref.dtype)
-            ref[q, rest:] = at(last + short * j, short, h).astype(ref.dtype)
+            for n, (opening, parts_of) in enumerate(PIECES):
+                if opening == "y":
+                    gone, q = r, p
+                elif opening == "d0":
+                    gone, q = p & 1, 2 * (p >> 1) + r
+                else:
+                    gone, q = (p >> 1) & 1, 2 * ((p >> 2) * 2 + (p & 1)) + r
+                ref = pieces[2 * n + gone]
+                for i, (kind, k) in enumerate(parts_of):
+                    first, per = start[kind]
+                    ref[q, short * i : short * (i + 1)] = at(first + step[kind] * k + per * j, short, h).astype(ref.dtype)
 
 
 def middle(parts, mix, rl, atoms, dy, vectors, out_w, inner_w, outer_w, slots):
@@ -509,20 +480,13 @@
     hidden = inner_w.shape[1]
     blocks, half, rows = hidden // width, width // 2, here // slots
     tall, short = hidden // parts, width // parts
-    rest = tall // 4
-    long = tall - rest
     assert hidden == 4 * width
     vm = pl.BlockSpec(memory_space=pltpu.VMEM)
     hbm = pl.BlockSpec(memory_space=pltpu.HBM)
     like = jax.ShapeDtypeStruct
     out_shape = [
         like((here, width), bf16),
-        like((parts, long, 128), f32),
-        like((parts, long, 128), bf16),
-        like((parts, blocks * short, 128), f32),
-        like((parts, blocks * short, 128), bf16),
-        like((parts, rest + short, 128), f32),
-        like((parts, rest + short, 128), bf16),
+        *(like((parts, len(blocks_of) * short, 128), kind) for _, blocks_of in PIECES for kind in (f32, bf16)),
         like((here, width), bf16),
         like((here, width), bf16),
         like((slots, width, rows), bf16),
@@ -560,11 +524,15 @@
         compiler_params=pltpu.CompilerParams(
             vmem_limit_bytes=20 << 20, collective_id=1, has_side_effects=True
         ),
-    )(mix, rl, atoms, dy, *vectors, out_w, inner_w, outer_w)
+    )(
+        mix, rl, atoms, dy, *vectors,
+        *(pltpu.with_memory_space_constraint(array, pltpu.HBM) for array in (out_w, inner_w, outer_w)),
+    )
 
 
 class Part:
-    def __init__(self, names, order, rows, dtype=bf16):
+    def __init__(self, names, order, rows, dtype=bf16, opening=None):
+        self.opening = opening
         self.names, self.order, self.rows, self.dtype = names, order, rows, dtype
         self.steps, left = [], list(names)
         for name in order:
@@ -583,15 +551,27 @@
 
     def scratch(self):
         shapes = [pltpu.VMEM((1 << len(self.names), self.rows, 128), f32)]
+        if self.opening:
+            shapes.append(pltpu.VMEM((1 << len(self.names), self.rows, 128), self.dtype))
         for _, spots in self.steps:
             shapes += [pltpu.VMEM((len(spots), self.rows, 128), self.dtype)] * 2
-        shapes += [pltpu.VMEM((self.rows, 128), self.dtype)] * 2
         n = len(self.steps) + 1
         return shapes + [pltpu.SemaphoreType.DMA((n,)), pltpu.SemaphoreType.DMA((n,))]
 
     def bind(self, refs, partner):
-        self.state, self.sends, self.recvs = refs[0], refs[1:-2:2], refs[2:-2:2]
+        self.state, refs = refs[0], refs[1:]
+        if self.opening:
+            self.first, refs = refs[0], refs[1:]
+        self.sends, self.recvs = refs[0:-2:2], refs[1:-2:2]
         self.send_sem, self.recv_sem, self.partner = refs[-2], refs[-1], partner
+
+    def open(self, send):
+        n = len(self.steps)
+        self.copy = remote(send, self.first, self.send_sem.at[n], self.recv_sem.at[n], self.partner(self.opening))
+
+    def opened(self, keep):
+        self.copy.wait()
+        self.state[...] = keep[...] + self.first[...].astype(f32)
 
     def go(self, n):
         name, spots = self.steps[n]
@@ -606,50 +586,47 @@
         for q, (near, _) in enumerate(self.steps[n][1]):
             self.state[near] = self.state[near] + self.recvs[n][q].astype(f32)
 
-    def share(self, total, core, y, row):
-        n = len(self.steps)
-        low = self.state[0].astype(self.dtype)
-        self.sends[n][...] = low
-        self.copy = remote(
-            self.sends[n], self.recvs[n], self.send_sem.at[n], self.recv_sem.at[n], self.partner("y")
-        )
-        self.put(total, core, y, row, low)
-
-    def shared(self, total, core, y, row):
-        self.copy.wait()
-        self.put(total, core, 1 - y, row, self.recvs[len(self.steps)][...])
-
-    def put(self, total, core, y, row, value):
-        total[core, row : row + self.rows, pl.ds(pl.multiple_of(y * 128, 128), 128)] = value.astype(f32)
+    def share(self, ref):
+        ref[...] = self.state[0].astype(ref.dtype)
 
 
 def make_parts(parts, width, hidden):
     bits = ["d%d" % b for b in range(parts.bit_length() - 1)]
     high = bits[::-1]
-    tall, short = hidden // parts, width // parts
-    rest = tall // 4
+    short = width // parts
     without = lambda name: [n for n in high if n != name]
-    a = Part(without("d0") + ["y"], ["y", "d1"] + bits[2:], tall - rest)
-    b = Part(high, ["d1", "d0"] + bits[2:], hidden // width * short)
-    c = Part(without("d1") + ["y"], ["d0", "y"] + bits[2:], rest + short)
+    kinds = {
+        "d0": (without("d0") + ["y"], ["y", "d1"]),
+        "y": (high, ["d1", "d0"]),
+        "d1": (without("d1") + ["y"], ["d0", "y"]),
+    }
+    early = [
+        Part(kinds[opening][0], kinds[opening][1] + bits[2:], len(blocks) * short, opening=opening)
+        for opening, blocks in PIECES
+    ]
     q = Part(high + ["y"], ["d0", "y", "d1"] + bits[2:], short)
     k = Part(high + ["y"], ["y", "d1", "d0"] + bits[2:], short)
     v = Part(high + ["y"], ["d1", "d0", "y"] + bits[2:], short)
     s = Part(high + ["y"], ["d1", "d0", "y"] + bits[2:], 16, f32)
-    return a, b, c, q, k, v, s
-
-
-def tail_kernel(parts, scale, hidden, *refs):
+    return early, [q, k, v, s]
+
+
+def back_kernel(parts, scale, hidden, *refs):
     (
-        dkt_in, dvt_in, dq_in, all_in, query_w, key_w, value_w, dmid_in, gain_ref, shift_ref, vec_ref,
-        a_keep, a_got, b_keep, b_got, c_keep, c_got, out_ref, total,
-        dkt, dvt, dq, atoms, qw, kw, vw, dmid, ak, ag, bk, bg, ck, cg,
+        qt, dm, dmt, nm, k_ref, vt, e_ref, cot, atoms, dmid, gain_ref, shift_ref, vec_ref,
+        *refs,
+    ) = refs
+    made, refs = refs[: 2 * len(PIECES)], refs[2 * len(PIECES) :]
+    (
+        query_w, key_w, value_w,
+        pg, out_ref, total,
+        dkt, dvt, dq, qw, kw, vw,
         dk_in, dv_in, dqh, dqh_in, vec_own, vec_in, standard, normed, partial, beside_send, beside_recv,
         across_send, across_recv, grads, vec_all, load_sem, send_sem, recv_sem,
-    ) = refs[:51]
+        *refs,
+    ) = refs
     slots, width, full = dkt.shape
-    here = dq.shape[0]
-    rows, half = here // slots, width // 2
+    rows, half = dq.shape[1], width // 2
     bits = parts.bit_length() - 1
     short, tall = width // parts, hidden // parts
     row, dp = lax.axis_index("rows"), lax.axis_index("dp")
@@ -662,46 +639,60 @@
         b = int(name[1:])
         return (xor(dp, 1 << b, bits), row)
 
-    pieces = make_parts(parts, width, hidden)
-    at = 51
-    for piece in pieces:
+    early, late = make_parts(parts, width, hidden)
+    for piece in early + late:
         n = len(piece.scratch())
-        piece.bind(refs[at : at + n], partner)
-        at += n
-    pa, pb, pc, pq, pk, pv, ps = pieces
-
-    pairs = (
-        (ak, a_keep), (ag, a_got), (bk, b_keep), (bg, b_got), (ck, c_keep), (cg, c_got), (dq, dq_in),
-        (dkt, dkt_in), (dvt, dvt_in), (atoms, all_in), (kw, key_w), (vw, value_w), (qw, query_w), (dmid, dmid_in),
-    )
-    loads = {}
-    for i, (vmem, hbm) in enumerate(pairs):
-        loads[id(vmem)] = pltpu.make_async_copy(hbm, vmem, load_sem.at[i])
-        loads[id(vmem)].start()
-    ready = lambda *which: [loads[id(ref)].wait() for ref in which]
-    meet([beside, across] + [partner("d%d" % b) for b in range(bits)])
+        piece.bind(refs[:n], partner)
+        refs = refs[n:]
+    one, two = early[:3], early[3:]
+    steps, late_steps = len(early[0].steps), len(late[0].steps)
+
+    def opened(group):
+        for piece in group:
+            piece.opened(made[2 * early.index(piece)])
+            piece.go(0)
+
+    def advance(group, n):
+        for piece in group:
+            piece.come(n)
+            if n + 1 < len(piece.steps):
+                piece.go(n + 1)
+
+    loads = [
+        pltpu.make_async_copy(hbm, vmem, load_sem.at[i])
+        for i, (hbm, vmem) in enumerate(((query_w, qw), (key_w, kw), (value_w, vw)))
+    ]
+    for copy in loads:
+        copy.start()
+    corner = (dp, 3 - row)
+    meet([beside, across, corner] + [partner("d%d" % b) for b in range(bits)])
+    for n, piece in enumerate(early):
+        piece.open(made[2 * n + 1])
+
+    sent = 0
+
+    def send(source, target, device):
+        nonlocal sent
+        sent += 1
+        return remote(source, target, send_sem.at[sent - 1], recv_sem.at[sent - 1], device)
+
     other = pl.ds(pl.multiple_of((1 - core) * half, half), half)
     mine = pl.ds(pl.multiple_of(core * half, half), half)
-    ready(dkt, dvt, dq)
-    to_sibling = [
-        remote(dkt.at[:, other, :], dk_in, send_sem.at[0], recv_sem.at[0], beside),
-        remote(dvt.at[:, other, :], dv_in, send_sem.at[1], recv_sem.at[1], beside),
-    ]
-    dq_low = dq[...]
-    dqh[0] = dq_low[:, :half]
-    dqh[1] = dq_low[:, half:]
-    to_sibling.append(remote(dqh.at[1 - core], dqh_in, send_sem.at[2], recv_sem.at[2], beside))
-    ready(ak, ag, bk, bg, ck, cg)
-    for piece, keep, got in ((pa, ak, ag), (pb, bk, bg), (pc, ck, cg)):
-        piece.state[...] = keep[...] + got[...].astype(f32)
-        piece.go(0)
-
     gain, shift = wide(gain_ref), wide(shift_ref)
     down = lambda value: jnp.sum(value, axis=0, keepdims=True)
-    ready(atoms, kw, vw)
     gain_grad = shift_grad = value_bias = 0.0
-    send_on = []
+    send_on, to_sibling = [], []
     for s in range(slots):
+        def block(b, carry):
+            attention_backward(s, b, qt, dm, dmt, nm, k_ref, vt, e_ref, cot, pg, dq, dkt, dvt)
+            return carry
+
+        lax.fori_loop(0, width // 128, block, 0)
+        to_sibling.append(send(dkt.at[s, other, :], dk_in.at[s], beside))
+        to_sibling.append(send(dvt.at[s, other, :], dv_in.at[s], beside))
+        if s == 0:
+            for copy in loads:
+                copy.wait()
         standard[s] = standardize(atoms[s].astype(f32))[0]
         normed[s] = (standard[s] * gain + shift).astype(bf16)
         dv = dvt[s].T
@@ -710,31 +701,36 @@
         gain_grad = gain_grad + down(grad * standard[s])
         shift_grad = shift_grad + down(grad)
         for i in range(full // rows):
-            to = xor(row, i, 2)
-            partial[to, s] = grad[rows * i : rows * (i + 1)]
+            partial[xor(row, i, 2), s] = grad[rows * i : rows * (i + 1)]
         beside_send[s, 0] = partial[1, s].astype(bf16)
         beside_send[s, 1] = partial[3, s].astype(bf16)
-        send_on.append(remote(beside_send.at[s], beside_recv.at[s], send_sem.at[3 + s], recv_sem.at[3 + s], beside))
-    ready(qw)
+        send_on.append(send(beside_send.at[s], beside_recv.at[s], beside))
+        if s == slots - 2:
+            opened(one)
+    opened(two)
+    dq_low = jnp.concatenate([dq[s] for s in range(slots)], axis=0)
+    dqh[0] = dq_low[:, :half]
+    dqh[1] = dq_low[:, half:]
+    to_sibling.append(send(dqh.at[1 - core], dqh_in, beside))
     own = pl.ds(pl.multiple_of(row * rows, rows), rows)
     next_to = pl.ds(pl.multiple_of((row + 1 - 2 * core) * rows, rows), rows)
     rows_of = lambda ref, which: jnp.concatenate([ref[s, which, :] for s in range(slots)], axis=0)
-    standard_own = rows_of(standard, own)
     query_grad = times_transposed(dq_low, qw[...]) * scale
-    vec_own[0:1, :] = gain_grad + down(query_grad * standard_own)
+    vec_own[0:1, :] = gain_grad + down(query_grad * rows_of(standard, own))
     vec_own[1:2, :] = shift_grad + down(query_grad)
     vec_own[2:3, :] = down(dq_low.astype(f32)) * scale
     vec_own[3:4, :] = value_bias
     vec_own[4:12, :] = vec_ref[...]
     vec_own[12:16, :] = jnp.zeros((4, width), f32)
-    n = 3 + slots
-    to_sibling.append(remote(vec_own, vec_in, send_sem.at[n], recv_sem.at[n], beside))
-
-    for piece in (pa, pb, pc):
-        piece.come(0)
-        piece.go(1)
-
-    for copy in to_sibling[:3]:
+    vec_sent = send(vec_own, vec_in, beside)
+
+    advance(one, 0)
+    for s in range(slots):
+        send_on[s].wait()
+        across_send[s] = (partial[2, s] + beside_recv[s, 1].astype(f32)).astype(bf16)
+    over = send(across_send, across_recv, across)
+
+    for copy in to_sibling:
         copy.wait()
     grads[0] = (
         outer_sum(rows_of(normed, own), dqh[core]) + outer_sum(rows_of(normed, next_to), dqh_in[...])
@@ -747,7 +743,7 @@
         value_total = value_total + times_transposed(turned, add(dvt[s, mine, :], dv_in[s]))
     grads[1] = key_total
     grads[2] = value_total
-    to_sibling[3].wait()
+    vec_sent.wait()
     vec = vec_own[...] + vec_in[...]
     vec_all[...] = jnp.zeros_like(vec_all)
     for j in range(parts):
@@ -759,75 +755,64 @@
         j = xor(dp, p, bits)
         for r in range(2):
             lanes = pl.ds(pl.multiple_of(other_bit(y, 0, r) * 128, 128), 128)
-            for i, piece in enumerate((pq, pk, pv)):
+            for i, piece in enumerate(late[:3]):
                 piece.state[2 * p + r] = grads[i, pl.ds(pl.multiple_of(j * short, short), short), lanes]
-            ps.state[2 * p + r] = vec_all[j, :, lanes]
-    late = (pq, pk, pv, ps)
+            late[3].state[2 * p + r] = vec_all[j, :, lanes]
     for piece in late:
         piece.go(0)
 
-    for s in range(slots):
-        send_on[s].wait()
-        across_send[s] = (partial[2, s] + beside_recv[s, 1].astype(f32)).astype(bf16)
-    n = 4 + slots
-    over = remote(across_send, across_recv, send_sem.at[n], recv_sem.at[n], across)
-
-    steps = len(pa.steps)
-    for piece in (pa, pb, pc):
-        piece.come(1)
-        piece.go(2)
-    for piece in late:
-        piece.come(0)
-        piece.go(1)
+    advance(two, 0)
+    advance(one, 1)
+    advance(late, 0)
+    advance(two, 1)
     over.wait()
-    ready(dmid)
     for s in range(slots):
         some = slice(rows * s, rows * (s + 1))
         grad = partial[0, s] + beside_recv[s, 0].astype(f32) + across_recv[s].astype(f32) + query_grad[some]
         stand, inverse = standardize(atoms[s, own, :].astype(f32))
         out_ref[some, :] = (dmid[some, :] + norm_back(grad * gain, stand, inverse)).astype(bf16)
     for n in range(2, steps):
-        for piece in (pa, pb, pc):
-            piece.come(n)
-            if n + 1 < steps:
-                piece.go(n + 1)
-        for piece in late:
-            piece.come(n - 1)
-            piece.go(n)
-    at = 0
-    places = []
-    for piece in (pa, pc, pb, pq, pk, pv, ps):
-        places.append((piece, at))
-        at += piece.rows
-    for piece, at in places[:3]:
-        piece.share(total, core, y, at)
-    for n in range(steps - 1, len(pq.steps)):
-        for piece in late:
-            piece.come(n)
-            if n + 1 < len(pq.steps):
-                piece.go(n + 1)
-    for piece, at in places[3:]:
-        piece.share(total, core, y, at)
-    for piece, at in places:
-        piece.shared(total, core, y, at)
-    n = 5 + slots
-    remote(total.at[core], total.at[core], send_sem.at[n], recv_sem.at[n], beside).wait()
-
-
-def tail(parts, scale, dkt, dvt, dq, all_atoms, query_w, key_w, value_w, dmid, vectors, vec, pieces):
-    slots, width, full = dkt.shape
-    here = dq.shape[0]
-    hidden = width * 4
-    rows, half = here // slots, width // 2
+        advance(one, n)
+        advance(late, n - 1)
+        advance(two, n)
+
+    def place(group, at):
+        for piece in group:
+            piece.share(total.at[row, at : at + piece.rows])
+            at += piece.rows
+        return at
+
+    cut = place(early, 0)
+    mine, theirs = total.at[row, :cut], total.at[across[1], :cut]
+    arrive = send(mine, mine, across)
+    ends = [send(mine, mine, beside)]
+    for n in range(steps - 1, late_steps):
+        advance(late, n)
+    place(late, cut)
+    rest = total.at[row, cut:]
+    ends += [send(rest, rest, device) for device in (across, corner, beside)]
+    arrive.wait()
+    ends.append(send(theirs, theirs, beside))
+    for copy in ends:
+        copy.wait()
+
+
+def back(parts, scale, qt, dm, dmt, nm, k, vt, weights, cot, atoms, dmid, vectors, vec, pieces, query_w, key_w, value_w):
+    slots, width, full = vt.shape
+    rows, half = qt.shape[2], width // 2
+    here, hidden = slots * rows, width * 4
     vm = pl.BlockSpec(memory_space=pltpu.VMEM)
-    hbm = pl.BlockSpec(memory_space=pl.ANY)
     far = pl.BlockSpec(memory_space=pltpu.HBM)
-    kinds = make_parts(parts, width, hidden)
+    kinds = sum(make_parts(parts, width, hidden), [])
     count = sum(piece.rows for piece in kinds)
-    same = lambda array: pltpu.VMEM(array.shape, array.dtype)
-    loaded = [dkt, dvt, dq, all_atoms, query_w, key_w, value_w, dmid] + list(pieces)
-    transfers = 6 + slots
-    scratch = [same(array) for array in loaded] + [
+    transfers = 3 * slots + 9
+    scratch = [
+        pltpu.VMEM((slots, width, full), bf16),
+        pltpu.VMEM((slots, width, full), bf16),
+        pltpu.VMEM((slots, rows, width), bf16),
+        pltpu.VMEM((width, width), bf16),
+        pltpu.VMEM((width, width), bf16),
+        pltpu.VMEM((width, width), bf16),
         pltpu.VMEM((slots, half, full), bf16),
         pltpu.VMEM((slots, half, full), bf16),
         pltpu.VMEM((2, here, half), bf16),
@@ -843,87 +828,80 @@
         pltpu.VMEM((slots, rows, width), bf16),
         pltpu.VMEM((3, width, half), f32),
         pltpu.VMEM((parts, 16, half), f32),
-        pltpu.SemaphoreType.DMA((len(loaded),)),
+        pltpu.SemaphoreType.DMA((3,)),
         pltpu.SemaphoreType.DMA((transfers,)),
         pltpu.SemaphoreType.DMA((transfers,)),
     ]
     for piece in kinds:
         scratch += piece.scratch()
     return pl.pallas_call(
-        functools.partial(tail_kernel, parts, scale, hidden),
-        in_specs=[hbm] * 4 + [far] * 3 + [hbm] + [vm] * 3 + [hbm] * 6,
-        out_specs=[vm, vm],
+        functools.partial(back_kernel, parts, scale, hidden),
+        in_specs=[vm] * (13 + 2 * len(PIECES)) + [far] * 3,
+        out_specs=[vm] * 3,
         out_shape=[
+            jax.ShapeDtypeStruct(cot.shape, bf16),
             jax.ShapeDtypeStruct((here, width), bf16),
-            jax.ShapeDtypeStruct((2, count, half), f32),
+            jax.ShapeDtypeStruct((4, count, 128), bf16),
         ],
         scratch_shapes=scratch,
-        name="tail",
+        name="back",
         cost_estimate=pl.CostEstimate(
-            flops=10 * slots * full * width * width, transcendentals=0, bytes_accessed=12 << 20
+            flops=40 * slots * full * width * width, transcendentals=0, bytes_accessed=32 << 20
         ),
-        compiler_params=pltpu.CompilerParams(vmem_limit_bytes=26 << 20, collective_id=2, has_side_effects=True),
-    )(dkt, dvt, dq, all_atoms, query_w, key_w, value_w, dmid, *vectors, vec, *pieces)
+        compiler_params=pltpu.CompilerParams(vmem_limit_bytes=VMEM_BACK, collective_id=2, has_side_effects=True),
+    )(
+        qt, dm, dmt, nm, k, vt, weights, cot, atoms, dmid, *vectors, vec, *pieces,
+        *(pltpu.with_memory_space_constraint(array, pltpu.HBM) for array in (query_w, key_w, value_w)),
+    )
 
 
 def last_kernel(
-    total, grad_ref, made_ref, grad_out, made_out, uw, ow, iw, qw, kw, vw, again, ashift, qb, vb, ob, fgain, fshift, ub, ib
+    total, grad_ref, made_ref, pair, grad_out, made_out, uw, ow, iw, qw, kw, vw, again, ashift, qb, vb, ob, fgain,
+    fshift, ub, ib, pair_out, sem,
 ):
-    half = total.shape[2]
+    copy = pltpu.make_async_copy(pair, pair_out, sem)
+    copy.start()
     grad_out[...] = grad_ref[...]
     made_out[...] = made_ref[...]
     short = ow.shape[0]
+    blocks = iw.shape[1] // 2 // 256
+    spots = [spot for _, of in PIECES for spot in of] + [("query", 0), ("key", 0), ("value", 0)]
+    refs = {"outer": uw, "inner": iw, "out": ow, "query": qw, "key": kw, "value": vw}
     at = 0
-    for ref in (uw, ow):
-        n = ref.shape[0]
-        for c in range(2):
-            ref[:, half * c : half * (c + 1)] = total[c, at : at + n, :]
-        at += n
-    blocks = iw.shape[1] // 2 // half
-    for k in range(blocks):
-        for c in range(2):
-            n = c * blocks + k
-            iw[:, half * n : half * (n + 1)] = total[c, at : at + short, :]
+    for name, k in spots:
+        ref = refs[name]
+        first = short * k if name == "outer" else 0
+        for r in range(4):
+            core, y = r % 2, r // 2
+            col = 256 * (core * blocks + k if name == "inner" else core) + 128 * y
+            ref[first : first + short, col : col + 128] = total[r, at : at + short, :].astype(f32)
         at += short
-    for ref in (qw, kw, vw):
-        for c in range(2):
-            ref[:, half * c : half * (c + 1)] = total[c, at : at + short, :]
-        at += short
-    vec = total[0, at : at + 16, :]
     for i, ref in enumerate((again, ashift, qb, vb, ob, fgain, fshift, ub)):
-        ref[...] = vec[i : i + 1, :short]
-    ib[...] = vec[8:9, : ib.shape[1]]
-
-
-def last(parts, total, grad, made, hidden):
+        ref[...] = total[0, at : at + 16, :].astype(f32)[i : i + 1, :short]
+    for y in range(2):
+        n = min(128, ib.shape[1] - 128 * y)
+        if n > 0:
+            ib[:, 128 * y : 128 * y + n] = total[2 * y, at : at + 16, :].astype(f32)[8:9, :n]
+    copy.wait()
+
+
+def last(parts, total, grad, made, pair, hidden):
     here, width = grad.shape
     short, tall = width // parts, hidden // parts
     vm = pl.BlockSpec(memory_space=pltpu.VMEM)
     like = lambda *shape: jax.ShapeDtypeStruct(shape, f32)
     out_shape = [jax.ShapeDtypeStruct(grad.shape, bf16)] * 2
     out_shape += [like(tall, width), like(short, width), like(short, hidden)] + [like(short, width)] * 3
-    out_shape += [like(1, short)] * 8 + [like(1, tall)]
+    out_shape += [like(1, short)] * 8 + [like(1, tall), jax.ShapeDtypeStruct(pair.shape, bf16)]
     return pl.pallas_call(
         last_kernel,
-        in_specs=[vm] * 3,
-        out_specs=[vm] * len(out_shape),
+        in_specs=[vm] * 3 + [pl.BlockSpec(memory_space=pl.ANY)],
+        out_specs=[vm] * (len(out_shape) - 1) + [pl.BlockSpec(memory_space=pl.ANY)],
         out_shape=out_shape,
+        scratch_shapes=[pltpu.SemaphoreType.DMA],
         name="last",
         compiler_params=pltpu.CompilerParams(vmem_limit_bytes=16 << 20),
-    )(total, grad, made)
-
-
-def make_swap(parts, group):
-    def swap(array, dp_bit=None, row_bit=None):
-        pairs = []
-        for d in range(parts):
-            for r in range(group):
-                e = d if dp_bit is None else d ^ (1 << dp_bit)
-                t = r if row_bit is None else r ^ (1 << row_bit)
-                pairs.append((d * group + r, e * group + t))
-        return lax.ppermute(array, ("dp", "rows"), pairs)
-
-    return swap
+    )(total, grad, made, pair)
 
 
 def local(
@@ -956,13 +934,12 @@
     scale = (width // heads) ** (-0.5)
     here = slots * part_rows
     hidden = inner_weight.shape[1]
-    swap = make_swap(parts, group)
     flat = lambda array: array.reshape(here, width)
     all_atoms, mask, q, qt, k, kt, v, vt = front(
         scale, full, atoms, mol_counts, (attn_gain, attn_shift, query_bias, value_bias), query_weight, key_weight, value_weight
     )
     pair_out, weights, mixed, inverse_sum = attention_forward(q, kt, v, pair_bias, mask)
-    atoms_out, a_keep, a_send, b_keep, b_send, c_keep, c_send, scaled, centre, scaled_turned, grad_middle, vec = middle(
+    atoms_out, *pieces, scaled, centre, scaled_turned, grad_middle, vec = middle(
         parts,
         flat(mixed),
         flat(inverse_sum),
@@ -974,27 +951,28 @@
         outer_weight,
         slots,
     )
-    a_got, b_got, c_got = swap(a_send, dp_bit=0), swap(b_send, row_bit=1), swap(c_send, dp_bit=1)
-    pair_grad, dq, dkt, dvt = attention_backward(
-        qt, scaled.reshape(q.shape), scaled_turned, centre.reshape(q.shape), k, vt, weights, pair_cotangent
-    )
-    grad, total = tail(
+    pair_grad, grad, total = back(
         parts,
         scale,
-        dkt,
-        dvt,
-        flat(dq),
+        qt,
+        scaled.reshape(q.shape),
+        scaled_turned,
+        centre.reshape(q.shape),
+        k,
+        vt,
+        weights,
+        pair_cotangent,
         all_atoms,
+        grad_middle,
+        (attn_gain, attn_shift),
+        vec,
+        pieces,
         query_weight,
         key_weight,
         value_weight,
-        grad_middle,
-        (attn_gain, attn_shift),
-        vec,
-        (a_keep, a_got, b_keep, b_got, c_keep, c_got),
     )
-    grad, made, uw, ow, iw, qw, kw, vw, again, ashift, qb, vb, ob, fgain, fshift, ub, ib = last(
-        parts, total, grad, atoms_out, hidden
+    grad, made, uw, ow, iw, qw, kw, vw, again, ashift, qb, vb, ob, fgain, fshift, ub, ib, pair_grad = last(
+        parts, total, grad, atoms_out, pair_grad, hidden
     )
     line = lambda array: array.reshape(-1)
     return (

time: 79.5 us -> 74.5 us (0.937)
  starting transfers between devices: 4.73 us -> 0 us
    ppermute x3 -> x0, starting transfers between devices: 4.73 us -> none  [swap(): return lax.ppermute(array, ('dp', 'rows'), pairs)]
    pallas_call x1, Pallas kernels: 7.89 us -> 9.31 us  [middle(): pl.pallas_call(functools.partial(middle_kernel, parts), in_specs=[vm] * 9...]
    pallas_call x3 -> x2, Pallas kernels: 46.8 us -> 45.4 us  [the longest x1 41.4 us: back(): pl.pallas_call(functools.partial(back_kernel, parts, scale, hidden), in_s...]
  transfers between devices with their start and end apart: 3 -> 0, of which waited for: 0 -> 0; matrix products, arithmetic and copies ran while one was open for 0% -> 0% of each run, Pallas kernels for 12% -> 0%
where the time goes in v5:
time: 74.5 us; the launch traced here: 74.4 us
  Pallas kernels  73.3 us (98%)
  between operations  1.01 us (1%)
    pallas_call x1, Pallas kernels, back(): pl.pallas_call(functools.partial(back_kernel, parts, scale, hidden), in_s...  41.4 us
    pallas_call x1, Pallas kernels, front(): pl.pallas_call(functools.partial(front_kernel, scale), in_specs=[vm, pl.B...  11.4 us
    pallas_call x1, Pallas kernels, middle(): pl.pallas_call(functools.partial(middle_kernel, parts), in_specs=[vm] * 9...  9.31 us
    pallas_call x1, Pallas kernels, attention_forward(): pl.pallas_call(forward_kernel, grid=(slots, heads // step), in_specs=[nat...  7.2 us
    pallas_call x1, Pallas kernels, last(): pl.pallas_call(last_kernel, in_specs=[vm] * 3 + [pl.BlockSpec(memory_spac...  4.01 us

profile of v5, /device:TPU:0, one launch (start us, length us, event | category | flops | bytes accessed | tf_op | source)
XLA Modules:
  0.0 74.4 jit_solution(9574829363388700888)
XLA Ops:
  0.7 0.0 copy-start
  0.7 11.4 %front.1 = (bf16[3,256,512]{2,1,0:T(8,128)(2,1)S(1)}, f32[3,64,256]{2,1,0:T(8,128)S(1)}, bf16[3,64,512]{2,1,0:T(8,128)(2,1)S(1)}, bf16[3,512,64]{2,1,0:T(8,128)(...) custom-call(bf16[3,64,512]{2,1,0:T(8,128)(2,1)} %atoms_ref.1, ...), custom_call_target="tpu_custom_call" | custom-call | flops 9663676416 | bytes 33554432 | tf_op jit(solution)/shard_map/front/pallas_call | solution.py:192
  12.0 0.0 copy-start.1
  12.1 0.0 copy-start.2
  12.1 0.0 copy-start.3
  12.1 0.0 copy-start.4
  12.1 0.0 copy-start.5
  12.1 0.0 copy-start.6
  12.1 0.0 copy-start.7
  12.1 0.0 slice-start
  12.1 0.0 copy-done
  12.2 0.0 slice-start.1
  12.2 7.2 %attention_forward.1 = (bf16[3,64,64,256]{3,2,1,0:T(8,128)(2,1)}, bf16[3,64,64,256]{3,2,1,0:T(8,128)(2,1)S(1)}, f32[3,64,512]{2,1,0:T(8,128)S(1)}, f32[3,64,512]{2,1,0:T(8,128)S(1)}) custom-call(bf16[3,64,512]{2,1,0:T(8,128)(2,1)S(1)} %get-tuple-element.71.q_ref, bf16[3,512,256]{2,1,0:T(8,128)(2,1)S(1)} %get-tuple-element.72.kt_ref, ...), custom_call_target="tpu_custom_call" | custom-call | flops 3221225472 | bytes 18874368 | tf_op jit(solution)/shard_map/attention_forward/pallas_call | solution.py:249
  19.4 0.0 copy-start.8
  19.4 0.0 copy-start.9
  19.4 0.0 copy-done.1
  19.4 0.0 copy-done.2
  19.4 0.0 copy-done.3
  19.4 0.0 copy-done.4
  19.4 0.0 copy-done.5
  19.4 0.0 copy-done.6
  19.4 0.0 copy-done.7
  19.4 9.3 %middle.1 = (bf16[192,512]{1,0:T(8,128)(2,1)S(1)}, f32[8,128,128]{2,1,0:T(8,128)S(1)}, bf16[8,128,128]{2,1,0:T(8,128)(2,1)S(1)}, f32[8,64,128]{2,1,0:T(8,128)S(1...) custom-call(f32[192,512]{1,0:T(8,128)S(1)} %bitcast.21, ...), custom_call_target="tpu_custom_call" | custom-call | flops 2415919104 | bytes 12582912 | tf_op jit(solution)/shard_map/middle/pallas_call | solution.py:497
  28.7 0.0 slice-done
  28.8 0.0 slice-done.1
  28.8 0.0 copy-done.8
  28.8 0.0 copy-done.9
  28.8 41.4 %back.1 = (bf16[3,64,64,256]{3,2,1,0:T(8,128)(2,1)S(1)}, bf16[192,512]{1,0:T(8,128)(2,1)S(1)}, bf16[4,784,128]{2,1,0:T(8,128)(2,1)S(1)}) custom-call(bf16[3,512,64]{2,1,0:T(8,128)(2,1)S(1)} %get-tuple-element.70.refs_0_, bf16[3,64,512]{2,1,0:T(8,128)(2,1)S(1)} %bitcast.23, bf16[3,512,64]{2,1,0:T(8,128)(2,1)S(1)} %get-tuple-element.78.refs_2_, ...), custom_call_target="tpu_custom_call" | custom-call | flops 8053063680 | bytes 33554432 | tf_op jit(solution)/shard_map/back/pallas_call | solution.py:837
  70.2 4.0 %last.1 = (bf16[192,512]{1,0:T(8,128)(2,1)}, bf16[192,512]{1,0:T(8,128)(2,1)}, f32[256,512]{1,0:T(8,128)}, f32[64,512]{1,0:T(8,128)}, f32[64,2048]{1,0:T(8,128)}...) custom-call(bf16[4,784,128]{2,1,0:T(8,128)(2,1)S(1)} %get-tuple-elem, ...), custom_call_target="tpu_custom_call" | custom-call | tf_op jit(solution)/shard_map/last/pallas_call | solution.py:896
  (1 shorter events, 0.0 us)
Async XLA Ops:
  0.7 11.5 %copy-start = (bf16[3,64,64,256]{3,2,1,0:T(8,128)(2,1)S(1)}, bf16[3,64,64,256]{3,2,1,0:T(8,128)(2,1)}, u32[]{:S(2)}) copy-start(bf16[3,64,64,256]{3,2,1,0:T(8,128)(2,1)} %bias_ref.2) | copy-start | bytes 18874372
  12.0 7.3 %copy-start.1 = (bf16[3,64,512]{2,1,0:T(8,128)(2,1)S(1)}, bf16[3,64,512]{2,1,0:T(8,128)(2,1)}, u32[]{:S(2)}) copy-start(bf16[3,64,512]{2,1,0:T(8,128)(2,1)} %atoms_ref.1) | copy-start | bytes 589828
  12.1 7.3 %copy-start.2 = (bf16[3,64,512]{2,1,0:T(8,128)(2,1)S(1)}, bf16[3,64,512]{2,1,0:T(8,128)(2,1)}, u32[]{:S(2)}) copy-start(bf16[3,64,512]{2,1,0:T(8,128)(2,1)} %param.38) | copy-start | bytes 589828
  12.1 7.3 %copy-start.3 = (bf16[2048]{0:T(1024)(128)(2,1)S(1)}, bf16[2048]{0:T(1024)(128)(2,1)}, u32[]{:S(2)}) copy-start(bf16[2048]{0:T(1024)(128)(2,1)} %bias_ref.3) | copy-start | bytes 12292
  12.1 7.3 %copy-start.4 = (bf16[512]{0:T(512)(128)(2,1)S(1)}, bf16[512]{0:T(512)(128)(2,1)}, u32[]{:S(2)}) copy-start(bf16[512]{0:T(512)(128)(2,1)} %out_b.1) | copy-start | bytes 3076
  12.1 7.3 %copy-start.5 = (bf16[512]{0:T(512)(128)(2,1)S(1)}, bf16[512]{0:T(512)(128)(2,1)}, u32[]{:S(2)}) copy-start(bf16[512]{0:T(512)(128)(2,1)} %gain_ref.3) | copy-start | bytes 3076
  12.1 7.3 %copy-start.6 = (bf16[512]{0:T(512)(128)(2,1)S(1)}, bf16[512]{0:T(512)(128)(2,1)}, u32[]{:S(2)}) copy-start(bf16[512]{0:T(512)(128)(2,1)} %shift_ref.3) | copy-start | bytes 3076
  12.1 7.3 %copy-start.7 = (bf16[512]{0:T(512)(128)(2,1)S(1)}, bf16[512]{0:T(512)(128)(2,1)}, u32[]{:S(2)}) copy-start(bf16[512]{0:T(512)(128)(2,1)} %outer_b.1) | copy-start | bytes 3076
  12.1 16.6 %slice-start = ((s8[6291456]{0:T(1024)(128)(4,1)}), s8[4194304]{0:T(1024)(128)(4,1)S(1)}, s32[]{:S(2)}) async-start(s8[6291456]{0:T(1024)(128)(4,1)} %bitcast.17), calls=%async_computation | async-start | bytes 8388608
  12.2 16.6 %slice-start.1 = ((s8[6291456]{0:T(1024)(128)(4,1)}), s8[2097152]{0:T(1024)(128)(4,1)S(1)}, s32[]{:S(2)}) async-start(s8[6291456]{0:T(1024)(128)(4,1)} %bitcast.17), calls=%async_computation.1 | async-start | bytes 4194304
  19.4 9.4 %copy-start.8 = (bf16[512]{0:T(512)(128)(2,1)S(1)}, bf16[512]{0:T(512)(128)(2,1)}, u32[]{:S(2)}) copy-start(bf16[512]{0:T(512)(128)(2,1)} %refs_10_.1) | copy-start | bytes 3076
  19.4 9.4 %copy-start.9 = (bf16[512]{0:T(512)(128)(2,1)S(1)}, bf16[512]{0:T(512)(128)(2,1)}, u32[]{:S(2)}) copy-start(bf16[512]{0:T(512)(128)(2,1)} %refs_11_.1) | copy-start | bytes 3076

commit v6 on v5

--- a/solution.py
+++ b/solution.py
@@ -525,8 +525,7 @@
             vmem_limit_bytes=20 << 20, collective_id=1, has_side_effects=True
         ),
     )(
-        mix, rl, atoms, dy, *vectors,
-        *(pltpu.with_memory_space_constraint(array, pltpu.HBM) for array in (out_w, inner_w, outer_w)),
+        mix, rl, atoms, dy, *vectors, out_w, inner_w, outer_w,
     )
 
 
@@ -855,14 +854,20 @@
     )
 
 
-def last_kernel(
-    total, grad_ref, made_ref, pair, grad_out, made_out, uw, ow, iw, qw, kw, vw, again, ashift, qb, vb, ob, fgain,
-    fshift, ub, ib, pair_out, sem,
-):
-    copy = pltpu.make_async_copy(pair, pair_out, sem)
-    copy.start()
-    grad_out[...] = grad_ref[...]
-    made_out[...] = made_ref[...]
+def last_kernel(total, grad_ref, made_ref, pair, *refs):
+    count = 18
+    outs, refs = refs[:count], refs[count:]
+    (grad_out, made_out, *_, pair_out), (uw, ow, iw, qw, kw, vw), small, sem = outs, refs[:6], refs[6:15], refs[15]
+    copies = []
+
+    def move(source, target):
+        copy = pltpu.make_async_copy(source, target, sem.at[len(copies)])
+        copy.start()
+        copies.append(copy)
+
+    move(pair, pair_out)
+    move(grad_ref, grad_out)
+    move(made_ref, made_out)
     short = ow.shape[0]
     blocks = iw.shape[1] // 2 // 256
     spots = [spot for _, of in PIECES for spot in of] + [("query", 0), ("key", 0), ("value", 0)]
@@ -876,29 +881,37 @@
             col = 256 * (core * blocks + k if name == "inner" else core) + 128 * y
             ref[first : first + short, col : col + 128] = total[r, at : at + short, :].astype(f32)
         at += short
-    for i, ref in enumerate((again, ashift, qb, vb, ob, fgain, fshift, ub)):
+    for ref, out in zip((uw, ow, iw, qw, kw, vw), outs[2:8]):
+        move(ref, out)
+    for i, ref in enumerate(small[:8]):
         ref[...] = total[0, at : at + 16, :].astype(f32)[i : i + 1, :short]
+    ib = small[8]
     for y in range(2):
         n = min(128, ib.shape[1] - 128 * y)
         if n > 0:
             ib[:, 128 * y : 128 * y + n] = total[2 * y, at : at + 16, :].astype(f32)[8:9, :n]
-    copy.wait()
+    for ref, out in zip(small, outs[8:17]):
+        move(ref, out)
+    for copy in copies:
+        copy.wait()
 
 
 def last(parts, total, grad, made, pair, hidden):
     here, width = grad.shape
     short, tall = width // parts, hidden // parts
     vm = pl.BlockSpec(memory_space=pltpu.VMEM)
-    like = lambda *shape: jax.ShapeDtypeStruct(shape, f32)
+    hbm = pl.BlockSpec(memory_space=pl.ANY)
+    shapes = [(tall, width), (short, width), (short, hidden)] + [(short, width)] * 3
+    shapes += [(1, short)] * 8 + [(1, tall)]
     out_shape = [jax.ShapeDtypeStruct(grad.shape, bf16)] * 2
-    out_shape += [like(tall, width), like(short, width), like(short, hidden)] + [like(short, width)] * 3
-    out_shape += [like(1, short)] * 8 + [like(1, tall), jax.ShapeDtypeStruct(pair.shape, bf16)]
+    out_shape += [jax.ShapeDtypeStruct(shape, f32) for shape in shapes]
+    out_shape.append(jax.ShapeDtypeStruct(pair.shape, bf16))
     return pl.pallas_call(
         last_kernel,
-        in_specs=[vm] * 3 + [pl.BlockSpec(memory_space=pl.ANY)],
-        out_specs=[vm] * (len(out_shape) - 1) + [pl.BlockSpec(memory_space=pl.ANY)],
+        in_specs=[vm] + [hbm] * 3,
+        out_specs=[hbm] * len(out_shape),
         out_shape=out_shape,
-        scratch_shapes=[pltpu.SemaphoreType.DMA],
+        scratch_shapes=[pltpu.VMEM(shape, f32) for shape in shapes] + [pltpu.SemaphoreType.DMA((len(out_shape),))],
         name="last",
         compiler_params=pltpu.CompilerParams(vmem_limit_bytes=16 << 20),
     )(total, grad, made, pair)

time: 74.5 us -> 72.7 us (0.976)
  Pallas kernels: 73.3 us -> 71.4 us
    pallas_call x1, Pallas kernels: 9.31 us -> 7.92 us  [middle(): pl.pallas_call(functools.partial(middle_kernel, parts), in_specs=[vm] * 9...]
where the time goes in v6:
time: 72.7 us; the launch traced here: 72.5 us
  Pallas kernels  71.4 us (98%)
  between operations  1.06 us (1%)
    pallas_call x1, Pallas kernels, back(): pl.pallas_call(functools.partial(back_kernel, parts, scale, hidden), in_s...  41.6 us
    pallas_call x1, Pallas kernels, front(): pl.pallas_call(functools.partial(front_kernel, scale), in_specs=[vm, pl.B...  11.4 us
    pallas_call x1, Pallas kernels, middle(): pl.pallas_call(functools.partial(middle_kernel, parts), in_specs=[vm] * 9...  7.92 us
    pallas_call x1, Pallas kernels, attention_forward(): pl.pallas_call(forward_kernel, grid=(slots, heads // step), in_specs=[nat...  7.04 us
    pallas_call x1, Pallas kernels, last(): pl.pallas_call(last_kernel, in_specs=[vm] + [hbm] * 3, out_specs=[hbm] *...  3.46 us

profile of v6, /device:TPU:0, one launch (start us, length us, event | category | flops | bytes accessed | tf_op | source)
XLA Modules:
  0.0 72.5 jit_solution(17153378719791114252)
XLA Ops:
  0.7 0.0 copy-start
  0.7 11.4 %front.1 = (bf16[3,256,512]{2,1,0:T(8,128)(2,1)S(1)}, f32[3,64,256]{2,1,0:T(8,128)S(1)}, bf16[3,64,512]{2,1,0:T(8,128)(2,1)S(1)}, bf16[3,512,64]{2,1,0:T(8,128)(...) custom-call(bf16[3,64,512]{2,1,0:T(8,128)(2,1)} %atoms_ref.1, ...), custom_call_target="tpu_custom_call" | custom-call | flops 9663676416 | bytes 33554432 | tf_op jit(solution)/shard_map/front/pallas_call | solution.py:192
  12.0 0.0 copy-start.1
  12.1 0.0 copy-start.2
  12.1 0.0 copy-start.3
  12.1 0.0 copy-start.4
  12.1 0.0 copy-start.5
  12.1 0.0 copy-start.6
  12.1 0.0 copy-start.7
  12.1 0.0 copy-start.8
  12.1 0.0 copy-start.9
  12.2 0.0 copy-start.10
  12.2 0.0 slice-start
  12.2 0.0 copy-done
  12.2 0.0 slice-start.1
  12.2 7.0 %attention_forward.1 = (bf16[3,64,64,256]{3,2,1,0:T(8,128)(2,1)}, bf16[3,64,64,256]{3,2,1,0:T(8,128)(2,1)S(1)}, f32[3,64,512]{2,1,0:T(8,128)S(1)}, f32[3,64,512]{2,1,0:T(8,128)S(1)}) custom-call(bf16[3,64,512]{2,1,0:T(8,128)(2,1)S(1)} %get-tuple-element.71.q_ref, bf16[3,512,256]{2,1,0:T(8,128)(2,1)S(1)} %get-tuple-element.72.kt_ref, ...), custom_call_target="tpu_custom_call" | custom-call | flops 3221225472 | bytes 18874368 | tf_op jit(solution)/shard_map/attention_forward/pallas_call | solution.py:249
  19.2 0.0 copy-start.11
  19.2 0.0 copy-start.12
  19.2 0.0 copy-done.1
  19.2 0.0 copy-done.2
  19.3 0.0 copy-done.3
  19.3 0.0 copy-done.4
  19.3 0.0 copy-done.5
  19.3 0.0 copy-done.6
  19.3 0.0 copy-done.7
  19.3 0.0 copy-done.8
  19.3 0.0 copy-done.9
  19.3 0.0 copy-done.10
  19.3 7.9 %middle.1 = (bf16[192,512]{1,0:T(8,128)(2,1)S(1)}, f32[8,128,128]{2,1,0:T(8,128)S(1)}, bf16[8,128,128]{2,1,0:T(8,128)(2,1)S(1)}, f32[8,64,128]{2,1,0:T(8,128)S(1...) custom-call(f32[192,512]{1,0:T(8,128)S(1)} %bitcast.21, ...), custom_call_target="tpu_custom_call" | custom-call | flops 2415919104 | bytes 12582912 | tf_op jit(solution)/shard_map/middle/pallas_call | solution.py:497
  27.3 0.0 slice-done
  27.3 0.0 slice-done.1
  27.3 0.0 copy-done.11
  27.3 0.0 copy-done.12
  27.3 41.6 %back.1 = (bf16[3,64,64,256]{3,2,1,0:T(8,128)(2,1)S(1)}, bf16[192,512]{1,0:T(8,128)(2,1)S(1)}, bf16[4,784,128]{2,1,0:T(8,128)(2,1)S(1)}) custom-call(bf16[3,512,64]{2,1,0:T(8,128)(2,1)S(1)} %get-tuple-element.70.refs_0_, bf16[3,64,512]{2,1,0:T(8,128)(2,1)S(1)} %bitcast.23, bf16[3,512,64]{2,1,0:T(8,128)(2,1)S(1)} %get-tuple-element.78.refs_2_, ...), custom_call_target="tpu_custom_call" | custom-call | flops 8053063680 | bytes 33554432 | tf_op jit(solution)/shard_map/back/pallas_call | solution.py:836
  68.9 3.5 %last.1 = (bf16[192,512]{1,0:T(8,128)(2,1)}, bf16[192,512]{1,0:T(8,128)(2,1)}, f32[256,512]{1,0:T(8,128)}, f32[64,512]{1,0:T(8,128)}, f32[64,2048]{1,0:T(8,128)}...) custom-call(bf16[4,784,128]{2,1,0:T(8,128)(2,1)S(1)} %get-tuple-elem, ...), custom_call_target="tpu_custom_call" | custom-call | tf_op jit(solution)/shard_map/last/pallas_call | solution.py:909
  (1 shorter events, 0.0 us)
Async XLA Ops:
  0.7 11.5 %copy-start = (bf16[3,64,64,256]{3,2,1,0:T(8,128)(2,1)S(1)}, bf16[3,64,64,256]{3,2,1,0:T(8,128)(2,1)}, u32[]{:S(2)}) copy-start(bf16[3,64,64,256]{3,2,1,0:T(8,128)(2,1)} %bias_ref.2) | copy-start | bytes 18874372
  12.0 7.2 %copy-start.1 = (bf16[512,2048]{1,0:T(8,128)(2,1)S(1)}, bf16[512,2048]{1,0:T(8,128)(2,1)}, u32[]{:S(2)}) copy-start(bf16[512,2048]{1,0:T(8,128)(2,1)} %inner_w.1) | copy-start | bytes 6291460
  12.1 7.2 %copy-start.2 = (bf16[2048,512]{1,0:T(8,128)(2,1)S(1)}, bf16[2048,512]{1,0:T(8,128)(2,1)}, u32[]{:S(2)}) copy-start(bf16[2048,512]{1,0:T(8,128)(2,1)} %outer_w.1) | copy-start | bytes 6291460
  12.1 7.2 %copy-start.3 = (bf16[512,512]{1,0:T(8,128)(2,1)S(1)}, bf16[512,512]{1,0:T(8,128)(2,1)}, u32[]{:S(2)}) copy-start(bf16[512,512]{1,0:T(8,128)(2,1)} %out_w.1) | copy-start | bytes 1572868
  12.1 7.2 %copy-start.4 = (bf16[3,64,512]{2,1,0:T(8,128)(2,1)S(1)}, bf16[3,64,512]{2,1,0:T(8,128)(2,1)}, u32[]{:S(2)}) copy-start(bf16[3,64,512]{2,1,0:T(8,128)(2,1)} %atoms_ref.1) | copy-start | bytes 589828
  12.1 7.2 %copy-start.5 = (bf16[3,64,512]{2,1,0:T(8,128)(2,1)S(1)}, bf16[3,64,512]{2,1,0:T(8,128)(2,1)}, u32[]{:S(2)}) copy-start(bf16[3,64,512]{2,1,0:T(8,128)(2,1)} %param.38) | copy-start | bytes 589828
  12.1 7.2 %copy-start.6 = (bf16[2048]{0:T(1024)(128)(2,1)S(1)}, bf16[2048]{0:T(1024)(128)(2,1)}, u32[]{:S(2)}) copy-start(bf16[2048]{0:T(1024)(128)(2,1)} %bias_ref.3) | copy-start | bytes 12292
  12.1 7.2 %copy-start.7 = (bf16[512]{0:T(512)(128)(2,1)S(1)}, bf16[512]{0:T(512)(128)(2,1)}, u32[]{:S(2)}) copy-start(bf16[512]{0:T(512)(128)(2,1)} %out_b.1) | copy-start | bytes 3076
  12.1 7.2 %copy-start.8 = (bf16[512]{0:T(512)(128)(2,1)S(1)}, bf16[512]{0:T(512)(128)(2,1)}, u32[]{:S(2)}) copy-start(bf16[512]{0:T(512)(128)(2,1)} %gain_ref.3) | copy-start | bytes 3076
  12.1 7.2 %copy-start.9 = (bf16[512]{0:T(512)(128)(2,1)S(1)}, bf16[512]{0:T(512)(128)(2,1)}, u32[]{:S(2)}) copy-start(bf16[512]{0:T(512)(128)(2,1)} %shift_ref.3) | copy-start | bytes 3076
  12.2 7.2 %copy-start.10 = (bf16[512]{0:T(512)(128)(2,1)S(1)}, bf16[512]{0:T(512)(128)(2,1)}, u32[]{:S(2)}) copy-start(bf16[512]{0:T(512)(128)(2,1)} %outer_b.1) | copy-start | bytes 3076
  12.2 15.1 %slice-start = ((s8[6291456]{0:T(1024)(128)(4,1)}), s8[4194304]{0:T(1024)(128)(4,1)S(1)}, s32[]{:S(2)}) async-start(s8[6291456]{0:T(1024)(128)(4,1)} %bitcast.17), calls=%async_computation | async-start | bytes 8388608
  12.2 15.1 %slice-start.1 = ((s8[6291456]{0:T(1024)(128)(4,1)}), s8[2097152]{0:T(1024)(128)(4,1)S(1)}, s32[]{:S(2)}) async-start(s8[6291456]{0:T(1024)(128)(4,1)} %bitcast.17), calls=%async_computation.1 | async-start | bytes 4194304
  19.2 8.0 %copy-start.11 = (bf16[512]{0:T(512)(128)(2,1)S(1)}, bf16[512]{0:T(512)(128)(2,1)}, u32[]{:S(2)}) copy-start(bf16[512]{0:T(512)(128)(2,1)} %refs_10_.1) | copy-start | bytes 3076
  19.2 8.1 %copy-start.12 = (bf16[512]{0:T(512)(128)(2,1)S(1)}, bf16[512]{0:T(512)(128)(2,1)}, u32[]{:S(2)}) copy-start(bf16[512]{0:T(512)(128)(2,1)} %refs_11_.1) | copy-start | bytes 3076

commit v7 on v6

--- a/solution.py
+++ b/solution.py
@@ -160,16 +160,23 @@
         mask_ref[s] = jnp.where(count(keys_at) == count(queries_at), 0.0, -BIG)
 
     forward = []
-    for s in range(slots):
-        near[s].wait()
-        project(s, y)
+
+    def pass_on(s):
         far[s].wait()
         n = 2 * slots + s
         forward.append(remote(there(s), there(s), send_sem.at[n], recv_sem.at[n], (dp, beside)))
+
+    for s in range(slots):
+        if s == slots - 1:
+            pass_on(0)
+        near[s].wait()
+        project(s, y)
+    for s in range(slots):
         masks(s)
-        if s:
-            forward[s - 1].wait()
-            project(s - 1, 1 - y)
+    for s in range(1, slots):
+        pass_on(s)
+        forward[s - 1].wait()
+        project(s - 1, 1 - y)
     forward[-1].wait()
     project(slots - 1, 1 - y)
 
@@ -321,9 +328,9 @@
     shift_ref,
     outer_b,
     bias_ref,
-    out_w,
-    inner_w,
-    outer_w,
+    ow,
+    iw,
+    uw,
     out_ref,
     *refs,
 ):
@@ -334,9 +341,6 @@
     dmt_ref,
     dmid_ref,
     vec_ref,
-    ow,
-    iw,
-    uw,
     act,
     dpre,
     dpre_in,
@@ -347,7 +351,6 @@
     dyh,
     dy_in,
     grads,
-    load_sem,
     send_sem,
     recv_sem,
     ) = refs
@@ -362,15 +365,8 @@
     y = row // 2
     sibling = (dp, row + 1 - 2 * core)
 
-    loads = [
-        pltpu.make_async_copy(hbm, vmem, load_sem.at[i])
-        for i, (hbm, vmem) in enumerate(((out_w, ow), (inner_w, iw), (outer_w, uw)))
-    ]
-    for copy in loads:
-        copy.start()
     barrier = pltpu.get_barrier_semaphore()
     pl.semaphore_signal(barrier, inc=1, device_id=sibling, device_id_type=pl.DeviceIdType.MESH)
-    pl.semaphore_wait(barrier, 1)
     sent = []
 
     def send(source, target):
@@ -389,18 +385,16 @@
     dy = dy_ref[...]
     dyh[0] = dy[:, :half]
     dyh[1] = dy[:, half:]
-    send(dyh.at[1 - core], dy_in)
     mix = mix_ref[...]
     mixed[0] = mix.astype(bf16)
-    send(mixed.at[0], mixed.at[1])
-    loads[0].wait()
     middle = atoms_ref[...].astype(f32) + matmul(mixed[0], ow[...]) + wide(out_b)
     standard, inverse = standardize(middle)
     gain = wide(gain_ref)
     inner[0] = (standard * gain + wide(shift_ref)).astype(bf16)
+    pl.semaphore_wait(barrier, 1)
+    send(dyh.at[1 - core], dy_in)
+    send(mixed.at[0], mixed.at[1])
     send(inner.at[0], inner.at[1])
-    loads[1].wait()
-    loads[2].wait()
     result = middle + wide(outer_b)
     bias = wide(bias_ref)
     grad_inner = jnp.zeros((here, width), f32)
@@ -482,7 +476,6 @@
     tall, short = hidden // parts, width // parts
     assert hidden == 4 * width
     vm = pl.BlockSpec(memory_space=pltpu.VMEM)
-    hbm = pl.BlockSpec(memory_space=pltpu.HBM)
     like = jax.ShapeDtypeStruct
     out_shape = [
         like((here, width), bf16),
@@ -496,13 +489,10 @@
     transfers = 3 + blocks + blocks // 2 + 1
     return pl.pallas_call(
         functools.partial(middle_kernel, parts),
-        in_specs=[vm] * 9 + [hbm] * 3,
+        in_specs=[vm] * 12,
         out_specs=[vm] * len(out_shape),
         out_shape=out_shape,
         scratch_shapes=[
-            pltpu.VMEM((width, width), bf16),
-            pltpu.VMEM((width, hidden), bf16),
-            pltpu.VMEM((hidden, width), bf16),
             pltpu.VMEM((2, blocks, here, width), bf16),
             pltpu.VMEM((blocks, here, width), bf16),
             pltpu.VMEM((blocks // 2, here, width), bf16),
@@ -513,7 +503,6 @@
             pltpu.VMEM((2, here, half), bf16),
             pltpu.VMEM((here, half), bf16),
             pltpu.VMEM((2 * hidden + width, half), f32),
-            pltpu.SemaphoreType.DMA((3,)),
             pltpu.SemaphoreType.DMA((transfers,)),
             pltpu.SemaphoreType.DMA((transfers,)),
         ],

time: 72.7 us -> 71.8 us (0.988)
  Pallas kernels: 71.4 us -> 70.5 us
where the time goes in v7:
time: 71.8 us; the launch traced here: 71.6 us
  Pallas kernels  70.5 us (98%)
  between operations  1.06 us (1%)
    pallas_call x1, Pallas kernels, back(): pl.pallas_call(functools.partial(back_kernel, parts, scale, hidden), in_s...  41 us
    pallas_call x1, Pallas kernels, front(): pl.pallas_call(functools.partial(front_kernel, scale), in_specs=[vm, pl.B...  11.4 us
    pallas_call x1, Pallas kernels, middle(): pl.pallas_call(functools.partial(middle_kernel, parts), in_specs=[vm] * 1...  7.41 us
    pallas_call x1, Pallas kernels, attention_forward(): pl.pallas_call(forward_kernel, grid=(slots, heads // step), in_specs=[nat...  7.22 us
    pallas_call x1, Pallas kernels, last(): pl.pallas_call(last_kernel, in_specs=[vm] + [hbm] * 3, out_specs=[hbm] *...  3.46 us

profile of v7, /device:TPU:0, one launch (start us, length us, event | category | flops | bytes accessed | tf_op | source)
XLA Modules:
  0.0 71.6 jit_solution(4507247625081593292)
XLA Ops:
  0.7 0.0 copy-start
  0.7 11.4 %front.1 = (bf16[3,256,512]{2,1,0:T(8,128)(2,1)S(1)}, f32[3,64,256]{2,1,0:T(8,128)S(1)}, bf16[3,64,512]{2,1,0:T(8,128)(2,1)S(1)}, bf16[3,512,64]{2,1,0:T(8,128)(...) custom-call(bf16[3,64,512]{2,1,0:T(8,128)(2,1)} %atoms_ref.1, ...), custom_call_target="tpu_custom_call" | custom-call | flops 9663676416 | bytes 33554432 | tf_op jit(solution)/shard_map/front/pallas_call | solution.py:199
  12.0 0.0 copy-start.1
  12.1 0.0 copy-start.2
  12.1 0.0 copy-start.3
  12.1 0.0 copy-start.4
  12.1 0.0 copy-start.5
  12.1 0.0 copy-start.6
  12.1 0.0 copy-start.7
  12.1 0.0 copy-start.8
  12.1 0.0 copy-start.9
  12.2 0.0 copy-start.10
  12.2 0.0 slice-start
  12.2 0.0 copy-done
  12.2 0.0 slice-start.1
  12.2 7.2 %attention_forward.1 = (bf16[3,64,64,256]{3,2,1,0:T(8,128)(2,1)}, bf16[3,64,64,256]{3,2,1,0:T(8,128)(2,1)S(1)}, f32[3,64,512]{2,1,0:T(8,128)S(1)}, f32[3,64,512]{2,1,0:T(8,128)S(1)}) custom-call(bf16[3,64,512]{2,1,0:T(8,128)(2,1)S(1)} %get-tuple-element.71.q_ref, bf16[3,512,256]{2,1,0:T(8,128)(2,1)S(1)} %get-tuple-element.72.kt_ref, ...), custom_call_target="tpu_custom_call" | custom-call | flops 3221225472 | bytes 18874368 | tf_op jit(solution)/shard_map/attention_forward/pallas_call | solution.py:256
  19.4 0.0 copy-start.11
  19.4 0.0 copy-start.12
  19.4 0.0 copy-done.1
  19.4 0.0 copy-done.2
  19.4 0.0 copy-done.3
  19.4 0.0 copy-done.4
  19.5 0.0 copy-done.5
  19.5 0.0 copy-done.6
  19.5 0.0 copy-done.7
  19.5 0.0 copy-done.8
  19.5 0.0 copy-done.9
  19.5 0.0 copy-done.10
  19.5 7.4 %middle.1 = (bf16[192,512]{1,0:T(8,128)(2,1)S(1)}, f32[8,128,128]{2,1,0:T(8,128)S(1)}, bf16[8,128,128]{2,1,0:T(8,128)(2,1)S(1)}, f32[8,64,128]{2,1,0:T(8,128)S(1...) custom-call(f32[192,512]{1,0:T(8,128)S(1)} %bitcast.21, ...), custom_call_target="tpu_custom_call" | custom-call | flops 2415919104 | bytes 12582912 | tf_op jit(solution)/shard_map/middle/pallas_call | solution.py:490
  26.9 0.0 slice-done
  26.9 0.0 slice-done.1
  27.0 0.0 copy-done.11
  27.0 0.0 copy-done.12
  27.0 41.0 %back.1 = (bf16[3,64,64,256]{3,2,1,0:T(8,128)(2,1)S(1)}, bf16[192,512]{1,0:T(8,128)(2,1)S(1)}, bf16[4,784,128]{2,1,0:T(8,128)(2,1)S(1)}) custom-call(bf16[3,512,64]{2,1,0:T(8,128)(2,1)S(1)} %get-tuple-element.70.refs_0_, bf16[3,64,512]{2,1,0:T(8,128)(2,1)S(1)} %bitcast.23, bf16[3,512,64]{2,1,0:T(8,128)(2,1)S(1)} %get-tuple-element.78.refs_2_, ...), custom_call_target="tpu_custom_call" | custom-call | flops 8053063680 | bytes 33554432 | tf_op jit(solution)/shard_map/back/pallas_call | solution.py:825
  68.0 3.5 %last.1 = (bf16[192,512]{1,0:T(8,128)(2,1)}, bf16[192,512]{1,0:T(8,128)(2,1)}, f32[256,512]{1,0:T(8,128)}, f32[64,512]{1,0:T(8,128)}, f32[64,2048]{1,0:T(8,128)}...) custom-call(bf16[4,784,128]{2,1,0:T(8,128)(2,1)S(1)} %get-tuple-elem, ...), custom_call_target="tpu_custom_call" | custom-call | tf_op jit(solution)/shard_map/last/pallas_call | solution.py:898
  (1 shorter events, 0.0 us)
Async XLA Ops:
  0.7 11.5 %copy-start = (bf16[3,64,64,256]{3,2,1,0:T(8,128)(2,1)S(1)}, bf16[3,64,64,256]{3,2,1,0:T(8,128)(2,1)}, u32[]{:S(2)}) copy-start(bf16[3,64,64,256]{3,2,1,0:T(8,128)(2,1)} %bias_ref.2) | copy-start | bytes 18874372
  12.0 7.4 %copy-start.1 = (bf16[512,2048]{1,0:T(8,128)(2,1)S(1)}, bf16[512,2048]{1,0:T(8,128)(2,1)}, u32[]{:S(2)}) copy-start(bf16[512,2048]{1,0:T(8,128)(2,1)} %iw.1) | copy-start | bytes 6291460
  12.1 7.4 %copy-start.2 = (bf16[2048,512]{1,0:T(8,128)(2,1)S(1)}, bf16[2048,512]{1,0:T(8,128)(2,1)}, u32[]{:S(2)}) copy-start(bf16[2048,512]{1,0:T(8,128)(2,1)} %uw.1) | copy-start | bytes 6291460
  12.1 7.4 %copy-start.3 = (bf16[512,512]{1,0:T(8,128)(2,1)S(1)}, bf16[512,512]{1,0:T(8,128)(2,1)}, u32[]{:S(2)}) copy-start(bf16[512,512]{1,0:T(8,128)(2,1)} %ow.1) | copy-start | bytes 1572868
  12.1 7.4 %copy-start.4 = (bf16[3,64,512]{2,1,0:T(8,128)(2,1)S(1)}, bf16[3,64,512]{2,1,0:T(8,128)(2,1)}, u32[]{:S(2)}) copy-start(bf16[3,64,512]{2,1,0:T(8,128)(2,1)} %atoms_ref.1) | copy-start | bytes 589828
  12.1 7.4 %copy-start.5 = (bf16[3,64,512]{2,1,0:T(8,128)(2,1)S(1)}, bf16[3,64,512]{2,1,0:T(8,128)(2,1)}, u32[]{:S(2)}) copy-start(bf16[3,64,512]{2,1,0:T(8,128)(2,1)} %param.38) | copy-start | bytes 589828
  12.1 7.4 %copy-start.6 = (bf16[2048]{0:T(1024)(128)(2,1)S(1)}, bf16[2048]{0:T(1024)(128)(2,1)}, u32[]{:S(2)}) copy-start(bf16[2048]{0:T(1024)(128)(2,1)} %bias_ref.3) | copy-start | bytes 12292
  12.1 7.4 %copy-start.7 = (bf16[512]{0:T(512)(128)(2,1)S(1)}, bf16[512]{0:T(512)(128)(2,1)}, u32[]{:S(2)}) copy-start(bf16[512]{0:T(512)(128)(2,1)} %out_b.1) | copy-start | bytes 3076
  12.1 7.4 %copy-start.8 = (bf16[512]{0:T(512)(128)(2,1)S(1)}, bf16[512]{0:T(512)(128)(2,1)}, u32[]{:S(2)}) copy-start(bf16[512]{0:T(512)(128)(2,1)} %gain_ref.3) | copy-start | bytes 3076
  12.1 7.4 %copy-start.9 = (bf16[512]{0:T(512)(128)(2,1)S(1)}, bf16[512]{0:T(512)(128)(2,1)}, u32[]{:S(2)}) copy-start(bf16[512]{0:T(512)(128)(2,1)} %shift_ref.3) | copy-start | bytes 3076
  12.2 7.3 %copy-start.10 = (bf16[512]{0:T(512)(128)(2,1)S(1)}, bf16[512]{0:T(512)(128)(2,1)}, u32[]{:S(2)}) copy-start(bf16[512]{0:T(512)(128)(2,1)} %outer_b.1) | copy-start | bytes 3076
  12.2 14.8 %slice-start = ((s8[6291456]{0:T(1024)(128)(4,1)}), s8[4194304]{0:T(1024)(128)(4,1)S(1)}, s32[]{:S(2)}) async-start(s8[6291456]{0:T(1024)(128)(4,1)} %bitcast.17), calls=%async_computation | async-start | bytes 8388608
  12.2 14.8 %slice-start.1 = ((s8[6291456]{0:T(1024)(128)(4,1)}), s8[2097152]{0:T(1024)(128)(4,1)S(1)}, s32[]{:S(2)}) async-start(s8[6291456]{0:T(1024)(128)(4,1)} %bitcast.17), calls=%async_computation.1 | async-start | bytes 4194304
  19.4 7.5 %copy-start.11 = (bf16[512]{0:T(512)(128)(2,1)S(1)}, bf16[512]{0:T(512)(128)(2,1)}, u32[]{:S(2)}) copy-start(bf16[512]{0:T(512)(128)(2,1)} %refs_10_.1) | copy-start | bytes 3076
  19.4 7.5 %copy-start.12 = (bf16[512]{0:T(512)(128)(2,1)S(1)}, bf16[512]{0:T(512)(128)(2,1)}, u32[]{:S(2)}) copy-start(bf16[512]{0:T(512)(128)(2,1)} %refs_11_.1) | copy-start | bytes 3076

commit v8 on v7

--- a/solution.py
+++ b/solution.py
@@ -11,8 +11,8 @@
 BIG = 1e9
 HPL = 16
 CHUNK = 8
-STEP = 32
-VMEM_PAIR = 16 << 20
+STEP = 64
+VMEM_PAIR = 22 << 20
 VMEM_BACK = 26 << 20
 MESH = pl.DeviceIdType.MESH
 PIECES = (

time: 71.8 us -> 71.1 us (level)
    pallas_call x1, Pallas kernels: 7.22 us -> 6.48 us  [attention_forward(): pl.pallas_call(forward_kernel, grid=(slots, heads // step), in_specs=[nat...]
where the time goes in v8:
time: 71.1 us; the launch traced here: 71 us
  Pallas kernels  69.8 us (98%)
  between operations  1.08 us (2%)
    pallas_call x1, Pallas kernels, back(): pl.pallas_call(functools.partial(back_kernel, parts, scale, hidden), in_s...  41.2 us
    pallas_call x1, Pallas kernels, front(): pl.pallas_call(functools.partial(front_kernel, scale), in_specs=[vm, pl.B...  11.4 us
    pallas_call x1, Pallas kernels, middle(): pl.pallas_call(functools.partial(middle_kernel, parts), in_specs=[vm] * 1...  7.34 us
    pallas_call x1, Pallas kernels, attention_forward(): pl.pallas_call(forward_kernel, grid=(slots, heads // step), in_specs=[nat...  6.48 us
    pallas_call x1, Pallas kernels, last(): pl.pallas_call(last_kernel, in_specs=[vm] + [hbm] * 3, out_specs=[hbm] *...  3.46 us

profile of v8, /device:TPU:0, one launch (start us, length us, event | category | flops | bytes accessed | tf_op | source)
XLA Modules:
  0.0 71.0 jit_solution(14995867193673161143)
XLA Ops:
  0.7 0.0 copy-start
  0.7 11.4 %front.1 = (bf16[3,256,512]{2,1,0:T(8,128)(2,1)S(1)}, f32[3,64,256]{2,1,0:T(8,128)S(1)}, bf16[3,64,512]{2,1,0:T(8,128)(2,1)S(1)}, bf16[3,512,64]{2,1,0:T(8,128)(...) custom-call(bf16[3,64,512]{2,1,0:T(8,128)(2,1)} %atoms_ref.1, ...), custom_call_target="tpu_custom_call" | custom-call | flops 9663676416 | bytes 33554432 | tf_op jit(solution)/shard_map/front/pallas_call | solution.py:199
  12.0 0.0 copy-start.1
  12.1 0.0 copy-start.2
  12.1 0.0 copy-start.3
  12.1 0.0 copy-start.4
  12.1 0.0 copy-start.5
  12.1 0.0 copy-start.6
  12.1 0.0 copy-start.7
  12.1 0.0 copy-start.8
  12.1 0.0 copy-start.9
  12.2 0.0 copy-start.10
  12.2 0.0 slice-start
  12.2 0.0 copy-done
  12.2 0.0 slice-start.1
  12.2 6.5 %attention_forward.1 = (bf16[3,64,64,256]{3,2,1,0:T(8,128)(2,1)}, bf16[3,64,64,256]{3,2,1,0:T(8,128)(2,1)S(1)}, f32[3,64,512]{2,1,0:T(8,128)S(1)}, f32[3,64,512]{2,1,0:T(8,128)S(1)}) custom-call(bf16[3,64,512]{2,1,0:T(8,128)(2,1)S(1)} %get-tuple-element.71.q_ref, bf16[3,512,256]{2,1,0:T(8,128)(2,1)S(1)} %get-tuple-element.72.kt_ref, ...), custom_call_target="tpu_custom_call" | custom-call | flops 3221225472 | bytes 18874368 | tf_op jit(solution)/shard_map/attention_forward/pallas_call | solution.py:256
  18.7 0.0 copy-start.11
  18.7 0.0 copy-start.12
  18.7 0.0 copy-done.1
  18.7 0.0 copy-done.2
  18.7 0.0 copy-done.3
  18.7 0.0 copy-done.4
  18.7 0.0 copy-done.5
  18.7 0.0 copy-done.6
  18.7 0.0 copy-done.7
  18.7 0.0 copy-done.8
  18.8 0.0 copy-done.9
  18.8 0.0 copy-done.10
  18.8 7.3 %middle.1 = (bf16[192,512]{1,0:T(8,128)(2,1)S(1)}, f32[8,128,128]{2,1,0:T(8,128)S(1)}, bf16[8,128,128]{2,1,0:T(8,128)(2,1)S(1)}, f32[8,64,128]{2,1,0:T(8,128)S(1...) custom-call(f32[192,512]{1,0:T(8,128)S(1)} %bitcast.21, ...), custom_call_target="tpu_custom_call" | custom-call | flops 2415919104 | bytes 12582912 | tf_op jit(solution)/shard_map/middle/pallas_call | solution.py:490
  26.1 0.0 slice-done
  26.1 0.0 slice-done.1
  26.1 0.0 copy-done.11
  26.2 0.0 copy-done.12
  26.2 41.2 %back.1 = (bf16[3,64,64,256]{3,2,1,0:T(8,128)(2,1)S(1)}, bf16[192,512]{1,0:T(8,128)(2,1)S(1)}, bf16[4,784,128]{2,1,0:T(8,128)(2,1)S(1)}) custom-call(bf16[3,512,64]{2,1,0:T(8,128)(2,1)S(1)} %get-tuple-element.70.refs_0_, bf16[3,64,512]{2,1,0:T(8,128)(2,1)S(1)} %bitcast.23, bf16[3,512,64]{2,1,0:T(8,128)(2,1)S(1)} %get-tuple-element.78.refs_2_, ...), custom_call_target="tpu_custom_call" | custom-call | flops 8053063680 | bytes 33554432 | tf_op jit(solution)/shard_map/back/pallas_call | solution.py:825
  67.3 3.5 %last.1 = (bf16[192,512]{1,0:T(8,128)(2,1)}, bf16[192,512]{1,0:T(8,128)(2,1)}, f32[256,512]{1,0:T(8,128)}, f32[64,512]{1,0:T(8,128)}, f32[64,2048]{1,0:T(8,128)}...) custom-call(bf16[4,784,128]{2,1,0:T(8,128)(2,1)S(1)} %get-tuple-elem, ...), custom_call_target="tpu_custom_call" | custom-call | tf_op jit(solution)/shard_map/last/pallas_call | solution.py:898
  (1 shorter events, 0.0 us)
Async XLA Ops:
  0.7 11.5 %copy-start = (bf16[3,64,64,256]{3,2,1,0:T(8,128)(2,1)S(1)}, bf16[3,64,64,256]{3,2,1,0:T(8,128)(2,1)}, u32[]{:S(2)}) copy-start(bf16[3,64,64,256]{3,2,1,0:T(8,128)(2,1)} %bias_ref.2) | copy-start | bytes 18874372
  12.0 6.6 %copy-start.1 = (bf16[512,2048]{1,0:T(8,128)(2,1)S(1)}, bf16[512,2048]{1,0:T(8,128)(2,1)}, u32[]{:S(2)}) copy-start(bf16[512,2048]{1,0:T(8,128)(2,1)} %iw.1) | copy-start | bytes 6291460
  12.1 6.6 %copy-start.2 = (bf16[2048,512]{1,0:T(8,128)(2,1)S(1)}, bf16[2048,512]{1,0:T(8,128)(2,1)}, u32[]{:S(2)}) copy-start(bf16[2048,512]{1,0:T(8,128)(2,1)} %uw.1) | copy-start | bytes 6291460
  12.1 6.6 %copy-start.3 = (bf16[512,512]{1,0:T(8,128)(2,1)S(1)}, bf16[512,512]{1,0:T(8,128)(2,1)}, u32[]{:S(2)}) copy-start(bf16[512,512]{1,0:T(8,128)(2,1)} %ow.1) | copy-start | bytes 1572868
  12.1 6.6 %copy-start.4 = (bf16[3,64,512]{2,1,0:T(8,128)(2,1)S(1)}, bf16[3,64,512]{2,1,0:T(8,128)(2,1)}, u32[]{:S(2)}) copy-start(bf16[3,64,512]{2,1,0:T(8,128)(2,1)} %atoms_ref.1) | copy-start | bytes 589828
  12.1 6.6 %copy-start.5 = (bf16[3,64,512]{2,1,0:T(8,128)(2,1)S(1)}, bf16[3,64,512]{2,1,0:T(8,128)(2,1)}, u32[]{:S(2)}) copy-start(bf16[3,64,512]{2,1,0:T(8,128)(2,1)} %param.38) | copy-start | bytes 589828
  12.1 6.6 %copy-start.6 = (bf16[2048]{0:T(1024)(128)(2,1)S(1)}, bf16[2048]{0:T(1024)(128)(2,1)}, u32[]{:S(2)}) copy-start(bf16[2048]{0:T(1024)(128)(2,1)} %bias_ref.3) | copy-start | bytes 12292
  12.1 6.6 %copy-start.7 = (bf16[512]{0:T(512)(128)(2,1)S(1)}, bf16[512]{0:T(512)(128)(2,1)}, u32[]{:S(2)}) copy-start(bf16[512]{0:T(512)(128)(2,1)} %out_b.1) | copy-start | bytes 3076
  12.1 6.6 %copy-start.8 = (bf16[512]{0:T(512)(128)(2,1)S(1)}, bf16[512]{0:T(512)(128)(2,1)}, u32[]{:S(2)}) copy-start(bf16[512]{0:T(512)(128)(2,1)} %gain_ref.3) | copy-start | bytes 3076
  12.1 6.6 %copy-start.9 = (bf16[512]{0:T(512)(128)(2,1)S(1)}, bf16[512]{0:T(512)(128)(2,1)}, u32[]{:S(2)}) copy-start(bf16[512]{0:T(512)(128)(2,1)} %shift_ref.3) | copy-start | bytes 3076
  12.2 6.6 %copy-start.10 = (bf16[512]{0:T(512)(128)(2,1)S(1)}, bf16[512]{0:T(512)(128)(2,1)}, u32[]{:S(2)}) copy-start(bf16[512]{0:T(512)(128)(2,1)} %outer_b.1) | copy-start | bytes 3076
  12.2 14.0 %slice-start = ((s8[6291456]{0:T(1024)(128)(4,1)}), s8[4194304]{0:T(1024)(128)(4,1)S(1)}, s32[]{:S(2)}) async-start(s8[6291456]{0:T(1024)(128)(4,1)} %bitcast.17), calls=%async_computation | async-start | bytes 8388608
  12.2 13.9 %slice-start.1 = ((s8[6291456]{0:T(1024)(128)(4,1)}), s8[2097152]{0:T(1024)(128)(4,1)S(1)}, s32[]{:S(2)}) async-start(s8[6291456]{0:T(1024)(128)(4,1)} %bitcast.17), calls=%async_computation.1 | async-start | bytes 4194304
  18.7 7.5 %copy-start.11 = (bf16[512]{0:T(512)(128)(2,1)S(1)}, bf16[512]{0:T(512)(128)(2,1)}, u32[]{:S(2)}) copy-start(bf16[512]{0:T(512)(128)(2,1)} %refs_10_.1) | copy-start | bytes 3076
  18.7 7.5 %copy-start.12 = (bf16[512]{0:T(512)(128)(2,1)S(1)}, bf16[512]{0:T(512)(128)(2,1)}, u32[]{:S(2)}) copy-start(bf16[512]{0:T(512)(128)(2,1)} %refs_11_.1) | copy-start | bytes 3076

commit v9 on v8

--- a/solution.py
+++ b/solution.py
@@ -10,6 +10,7 @@
 f32, bf16 = jnp.float32, jnp.bfloat16
 BIG = 1e9
 HPL = 16
+WIDE = 16
 CHUNK = 8
 STEP = 64
 VMEM_PAIR = 22 << 20
@@ -227,18 +228,18 @@
         v = jnp.concatenate([v_ref[0, :, cols], ones], axis=1)
         mixed = jnp.zeros((rows, 128), f32)
         total = jnp.zeros((rows, 128), f32)
-        for c in range(HPL // CHUNK):
-            own = [lane_head == CHUNK * c + i for i in range(CHUNK)]
+        for c in range(HPL // WIDE):
+            own = [lane_head == WIDE * c + i for i in range(WIDE)]
             left = jnp.concatenate([jnp.where(o, q, 0.0).astype(bf16) for o in own], axis=0)
-            scores = matmul(left, kt).reshape(CHUNK, rows, full)
-            hs = slice(HPL * b + CHUNK * c, HPL * b + CHUNK * (c + 1))
+            scores = matmul(left, kt).reshape(WIDE, rows, full)
+            hs = slice(HPL * b + WIDE * c, HPL * b + WIDE * (c + 1))
             scores = scores + bias_ref[0, hs].astype(f32)
             out_ref[0, hs] = scores.astype(bf16)
             scores = scores + mask[None]
             highest = jnp.max(scores, axis=-1, keepdims=True)
             e = jnp.exp(scores - highest).astype(bf16)
             e_ref[0, hs] = e
-            sums = matmul(e.reshape(CHUNK * rows, full), v)
+            sums = matmul(e.reshape(WIDE * rows, full), v)
             for i, o in enumerate(own):
                 mixed = jnp.where(o, sums[rows * i : rows * (i + 1), :128], mixed)
                 total = jnp.where(o, sums[rows * i : rows * (i + 1), 128:], total)
@@ -712,7 +713,6 @@
     vec_own[12:16, :] = jnp.zeros((4, width), f32)
     vec_sent = send(vec_own, vec_in, beside)
 
-    advance(one, 0)
     for s in range(slots):
         send_on[s].wait()
         across_send[s] = (partial[2, s] + beside_recv[s, 1].astype(f32)).astype(bf16)
@@ -731,6 +731,7 @@
         value_total = value_total + times_transposed(turned, add(dvt[s, mine, :], dv_in[s]))
     grads[1] = key_total
     grads[2] = value_total
+    advance(one, 0)
     vec_sent.wait()
     vec = vec_own[...] + vec_in[...]
     vec_all[...] = jnp.zeros_like(vec_all)

time: 71.1 us -> 71 us (level)
  no operation moved by 1% of the time
where the time goes in v9:
time: 71 us; the launch traced here: 70.9 us
  Pallas kernels  69.7 us (98%)
  between operations  1.08 us (2%)
    pallas_call x1, Pallas kernels, back(): pl.pallas_call(functools.partial(back_kernel, parts, scale, hidden), in_s...  41.1 us
    pallas_call x1, Pallas kernels, front(): pl.pallas_call(functools.partial(front_kernel, scale), in_specs=[vm, pl.B...  11.4 us
    pallas_call x1, Pallas kernels, middle(): pl.pallas_call(functools.partial(middle_kernel, parts), in_specs=[vm] * 1...  7.33 us
    pallas_call x1, Pallas kernels, attention_forward(): pl.pallas_call(forward_kernel, grid=(slots, heads // step), in_specs=[nat...  6.45 us
    pallas_call x1, Pallas kernels, last(): pl.pallas_call(last_kernel, in_specs=[vm] + [hbm] * 3, out_specs=[hbm] *...  3.46 us

profile of v9, /device:TPU:0, one launch (start us, length us, event | category | flops | bytes accessed | tf_op | source)
XLA Modules:
  0.0 70.9 jit_solution(826674115810990950)
XLA Ops:
  0.7 0.0 copy-start
  0.7 11.4 %front.1 = (bf16[3,256,512]{2,1,0:T(8,128)(2,1)S(1)}, f32[3,64,256]{2,1,0:T(8,128)S(1)}, bf16[3,64,512]{2,1,0:T(8,128)(2,1)S(1)}, bf16[3,512,64]{2,1,0:T(8,128)(...) custom-call(bf16[3,64,512]{2,1,0:T(8,128)(2,1)} %atoms_ref.1, ...), custom_call_target="tpu_custom_call" | custom-call | flops 9663676416 | bytes 33554432 | tf_op jit(solution)/shard_map/front/pallas_call | solution.py:200
  12.0 0.0 copy-start.1
  12.1 0.0 copy-start.2
  12.1 0.0 copy-start.3
  12.1 0.0 copy-start.4
  12.1 0.0 copy-start.5
  12.1 0.0 copy-start.6
  12.1 0.0 copy-start.7
  12.1 0.0 copy-start.8
  12.1 0.0 copy-start.9
  12.2 0.0 copy-start.10
  12.2 0.0 slice-start
  12.2 0.0 copy-done
  12.2 0.0 slice-start.1
  12.2 6.4 %attention_forward.1 = (bf16[3,64,64,256]{3,2,1,0:T(8,128)(2,1)}, bf16[3,64,64,256]{3,2,1,0:T(8,128)(2,1)S(1)}, f32[3,64,512]{2,1,0:T(8,128)S(1)}, f32[3,64,512]{2,1,0:T(8,128)S(1)}) custom-call(bf16[3,64,512]{2,1,0:T(8,128)(2,1)S(1)} %get-tuple-element.71.q_ref, bf16[3,512,256]{2,1,0:T(8,128)(2,1)S(1)} %get-tuple-element.72.kt_ref, ...), custom_call_target="tpu_custom_call" | custom-call | flops 3221225472 | bytes 18874368 | tf_op jit(solution)/shard_map/attention_forward/pallas_call | solution.py:257
  18.6 0.0 copy-start.11
  18.7 0.0 copy-start.12
  18.7 0.0 copy-done.1
  18.7 0.0 copy-done.2
  18.7 0.0 copy-done.3
  18.7 0.0 copy-done.4
  18.7 0.0 copy-done.5
  18.7 0.0 copy-done.6
  18.7 0.0 copy-done.7
  18.7 0.0 copy-done.8
  18.7 0.0 copy-done.9
  18.7 0.0 copy-done.10
  18.7 7.3 %middle.1 = (bf16[192,512]{1,0:T(8,128)(2,1)S(1)}, f32[8,128,128]{2,1,0:T(8,128)S(1)}, bf16[8,128,128]{2,1,0:T(8,128)(2,1)S(1)}, f32[8,64,128]{2,1,0:T(8,128)S(1...) custom-call(f32[192,512]{1,0:T(8,128)S(1)} %bitcast.21, ...), custom_call_target="tpu_custom_call" | custom-call | flops 2415919104 | bytes 12582912 | tf_op jit(solution)/shard_map/middle/pallas_call | solution.py:491
  26.1 0.0 slice-done
  26.1 0.0 slice-done.1
  26.1 0.0 copy-done.11
  26.1 0.0 copy-done.12
  26.1 41.1 %back.1 = (bf16[3,64,64,256]{3,2,1,0:T(8,128)(2,1)S(1)}, bf16[192,512]{1,0:T(8,128)(2,1)S(1)}, bf16[4,784,128]{2,1,0:T(8,128)(2,1)S(1)}) custom-call(bf16[3,512,64]{2,1,0:T(8,128)(2,1)S(1)} %get-tuple-element.70.refs_0_, bf16[3,64,512]{2,1,0:T(8,128)(2,1)S(1)} %bitcast.23, bf16[3,512,64]{2,1,0:T(8,128)(2,1)S(1)} %get-tuple-element.78.refs_2_, ...), custom_call_target="tpu_custom_call" | custom-call | flops 8053063680 | bytes 33554432 | tf_op jit(solution)/shard_map/back/pallas_call | solution.py:826
  67.2 3.5 %last.1 = (bf16[192,512]{1,0:T(8,128)(2,1)}, bf16[192,512]{1,0:T(8,128)(2,1)}, f32[256,512]{1,0:T(8,128)}, f32[64,512]{1,0:T(8,128)}, f32[64,2048]{1,0:T(8,128)}...) custom-call(bf16[4,784,128]{2,1,0:T(8,128)(2,1)S(1)} %get-tuple-elem, ...), custom_call_target="tpu_custom_call" | custom-call | tf_op jit(solution)/shard_map/last/pallas_call | solution.py:899
  (1 shorter events, 0.0 us)
Async XLA Ops:
  0.7 11.5 %copy-start = (bf16[3,64,64,256]{3,2,1,0:T(8,128)(2,1)S(1)}, bf16[3,64,64,256]{3,2,1,0:T(8,128)(2,1)}, u32[]{:S(2)}) copy-start(bf16[3,64,64,256]{3,2,1,0:T(8,128)(2,1)} %bias_ref.2) | copy-start | bytes 18874372
  12.0 6.6 %copy-start.1 = (bf16[512,2048]{1,0:T(8,128)(2,1)S(1)}, bf16[512,2048]{1,0:T(8,128)(2,1)}, u32[]{:S(2)}) copy-start(bf16[512,2048]{1,0:T(8,128)(2,1)} %iw.1) | copy-start | bytes 6291460
  12.1 6.6 %copy-start.2 = (bf16[2048,512]{1,0:T(8,128)(2,1)S(1)}, bf16[2048,512]{1,0:T(8,128)(2,1)}, u32[]{:S(2)}) copy-start(bf16[2048,512]{1,0:T(8,128)(2,1)} %uw.1) | copy-start | bytes 6291460
  12.1 6.6 %copy-start.3 = (bf16[512,512]{1,0:T(8,128)(2,1)S(1)}, bf16[512,512]{1,0:T(8,128)(2,1)}, u32[]{:S(2)}) copy-start(bf16[512,512]{1,0:T(8,128)(2,1)} %ow.1) | copy-start | bytes 1572868
  12.1 6.6 %copy-start.4 = (bf16[3,64,512]{2,1,0:T(8,128)(2,1)S(1)}, bf16[3,64,512]{2,1,0:T(8,128)(2,1)}, u32[]{:S(2)}) copy-start(bf16[3,64,512]{2,1,0:T(8,128)(2,1)} %atoms_ref.1) | copy-start | bytes 589828
  12.1 6.6 %copy-start.5 = (bf16[3,64,512]{2,1,0:T(8,128)(2,1)S(1)}, bf16[3,64,512]{2,1,0:T(8,128)(2,1)}, u32[]{:S(2)}) copy-start(bf16[3,64,512]{2,1,0:T(8,128)(2,1)} %param.38) | copy-start | bytes 589828
  12.1 6.6 %copy-start.6 = (bf16[2048]{0:T(1024)(128)(2,1)S(1)}, bf16[2048]{0:T(1024)(128)(2,1)}, u32[]{:S(2)}) copy-start(bf16[2048]{0:T(1024)(128)(2,1)} %bias_ref.3) | copy-start | bytes 12292
  12.1 6.6 %copy-start.7 = (bf16[512]{0:T(512)(128)(2,1)S(1)}, bf16[512]{0:T(512)(128)(2,1)}, u32[]{:S(2)}) copy-start(bf16[512]{0:T(512)(128)(2,1)} %out_b.1) | copy-start | bytes 3076
  12.1 6.6 %copy-start.8 = (bf16[512]{0:T(512)(128)(2,1)S(1)}, bf16[512]{0:T(512)(128)(2,1)}, u32[]{:S(2)}) copy-start(bf16[512]{0:T(512)(128)(2,1)} %gain_ref.3) | copy-start | bytes 3076
  12.1 6.6 %copy-start.9 = (bf16[512]{0:T(512)(128)(2,1)S(1)}, bf16[512]{0:T(512)(128)(2,1)}, u32[]{:S(2)}) copy-start(bf16[512]{0:T(512)(128)(2,1)} %shift_ref.3) | copy-start | bytes 3076
  12.2 6.6 %copy-start.10 = (bf16[512]{0:T(512)(128)(2,1)S(1)}, bf16[512]{0:T(512)(128)(2,1)}, u32[]{:S(2)}) copy-start(bf16[512]{0:T(512)(128)(2,1)} %outer_b.1) | copy-start | bytes 3076
  12.2 13.9 %slice-start = ((s8[6291456]{0:T(1024)(128)(4,1)}), s8[4194304]{0:T(1024)(128)(4,1)S(1)}, s32[]{:S(2)}) async-start(s8[6291456]{0:T(1024)(128)(4,1)} %bitcast.17), calls=%async_computation | async-start | bytes 8388608
  12.2 13.9 %slice-start.1 = ((s8[6291456]{0:T(1024)(128)(4,1)}), s8[2097152]{0:T(1024)(128)(4,1)S(1)}, s32[]{:S(2)}) async-start(s8[6291456]{0:T(1024)(128)(4,1)} %bitcast.17), calls=%async_computation.1 | async-start | bytes 4194304
  18.6 7.5 %copy-start.11 = (bf16[512]{0:T(512)(128)(2,1)S(1)}, bf16[512]{0:T(512)(128)(2,1)}, u32[]{:S(2)}) copy-start(bf16[512]{0:T(512)(128)(2,1)} %refs_10_.1) | copy-start | bytes 3076
  18.7 7.5 %copy-start.12 = (bf16[512]{0:T(512)(128)(2,1)S(1)}, bf16[512]{0:T(512)(128)(2,1)}, u32[]{:S(2)}) copy-start(bf16[512]{0:T(512)(128)(2,1)} %refs_11_.1) | copy-start | bytes 3076
